TPU v7x, 128 devices: a whole 4x4x4 slice. The times are simulated.
128 devices in a mesh: head: 8 (over x_hi, z), frame: 16 (over x_lo, y, core).
Axes of the slice: x: 4 (x_hi: 2, x_lo: 2; x = x_hi * 2 + x_lo), y: 4, z: 4, core: 2. Of those that a mesh axis runs over, the one named last changes fastest.
Arguments:
- queries: bfloat16 [16384, 2048], P(('frame', 'head')), may hold values from -6 to 6
- key_states: bfloat16 [16384, 2048], P(('frame', 'head')), may hold values from -6 to 6
- value_states: bfloat16 [16384, 2048], P(('frame', 'head')), may hold values from -6 to 6
- attn_out: bfloat16 [16384, 2048], P(('frame', 'head')), may hold values from -6 to 6
- grad_out: bfloat16 [16384, 2048], P(('frame', 'head')), may hold values from -192 to 192
- frame_order: int32 [16], replicated, may hold values from 0 to 15, each once
- block_live: int32 [16, 8, 8], replicated, may hold values from 0 to 1, as said below
Outputs:
- grad_queries: bfloat16 [16384, 2048], P('frame', 'head')
- grad_keys: bfloat16 [16384, 2048], P('frame', 'head')
- grad_values: bfloat16 [16384, 2048], P('frame', 'head')
Inputs may be any that keep to these rules, and one draw needn't show every extreme that they name: `block_live`: every entry at distance 0 is 1; every entry at distances of 4 or more is 0.
All inputs are finite; a program needn't handle non-finite values.
Results may differ from a plain program's by a relative error of at most 0.0049.
Values may be sent and summed in bfloat16 or wider, within the bound.
A program may use at most 128 MiB of HBM per device.

v0:
```python
import jax
import jax.numpy as jnp
from jax import lax
from jax.sharding import PartitionSpec as P

HEADS = 16
HEAD_DIM = 128


def passed_along(value, axis, steps):
    count = lax.axis_size(axis)
    pairs = [(source, (source + steps) % count) for source in range(count)]
    return lax.ppermute(value, axis, pairs)


def pair_blocks(block_live, frame_order, slot_query, slot_key):
    distance = jnp.abs(frame_order[slot_query] - frame_order[slot_key])
    return lax.dynamic_index_in_dim(block_live, distance, 0, keepdims=False)


def pair_mask(blocks, length):
    count = blocks.shape[0]
    width = length // count
    spread = jnp.broadcast_to(blocks[:, None, :, None], (count, width, count, width))
    return spread.reshape(length, length) > 0


def pair_grads(query_blk, key_blk, value_blk, grad_blk, log_total, delta_rows, mask, scale):
    scores = scale * jnp.einsum(
        "qhd,khd->hqk", query_blk, key_blk, preferred_element_type=jnp.float32
    )
    probs = jnp.where(mask, jnp.exp(scores - log_total[:, :, None]), 0.0)
    grad_probs = jnp.einsum("qhd,khd->hqk", grad_blk, value_blk, preferred_element_type=jnp.float32)
    grad_scores = (probs * (grad_probs - delta_rows[:, :, None])).astype(jnp.bfloat16)
    grad_query = scale * jnp.einsum(
        "hqk,khd->qhd", grad_scores, key_blk, preferred_element_type=jnp.float32
    )
    grad_key = scale * jnp.einsum(
        "hqk,qhd->khd", grad_scores, query_blk, preferred_element_type=jnp.float32
    )
    grad_value = jnp.einsum(
        "hqk,qhd->khd", probs.astype(jnp.bfloat16), grad_blk, preferred_element_type=jnp.float32
    )
    return (grad_query, grad_key, grad_value)


def unchanged(totals):
    return totals


def local(queries, key_states, value_states, attn_out, grad_out, frame_order, block_live):
    head_here = HEADS // lax.axis_size("head")
    scale = HEAD_DIM ** (-0.5)
    frames = lax.axis_size("frame")
    slot_self = lax.axis_index("frame")
    query_h, key_h, value_h, grad_h, output_h = (
        lax.all_to_all(queries, "head", split_axis=1, concat_axis=0, tiled=True),
        lax.all_to_all(key_states, "head", split_axis=1, concat_axis=0, tiled=True),
        lax.all_to_all(value_states, "head", split_axis=1, concat_axis=0, tiled=True),
        lax.all_to_all(grad_out, "head", split_axis=1, concat_axis=0, tiled=True),
        lax.all_to_all(attn_out, "head", split_axis=1, concat_axis=0, tiled=True),
    )
    length = query_h.shape[0]
    products = grad_h.astype(jnp.float32) * output_h.astype(jnp.float32)
    delta_rows = jnp.sum(products.reshape(length, head_here, HEAD_DIM), axis=2).T
    shape3 = (length, head_here, HEAD_DIM)
    query3 = query_h.reshape(shape3)
    key3 = key_h.reshape(shape3)
    value3 = value_h.reshape(shape3)
    grad3 = grad_h.reshape(shape3)
    start_peak = jnp.full((head_here, length), -1e30, jnp.float32)
    start_total = jnp.zeros((head_here, length), jnp.float32)
    piece = lax.all_gather(key_h, "frame", axis=0, tiled=True)
    count = piece.shape[0] // length
    stacked = piece.reshape(count, length, head_here, HEAD_DIM)

    def one_frame(state, item):
        block, index = item
        blocks = pair_blocks(block_live, frame_order, slot_self, index)

        def one_update(current):
            peak, total = current
            mask = pair_mask(blocks, length)
            scores = scale * jnp.einsum(
                "qhd,khd->hqk", query3, block, preferred_element_type=jnp.float32
            )
            new_peak = jnp.maximum(peak, jnp.max(jnp.where(mask, scores, -1e30), axis=2))
            fresh = jnp.sum(jnp.where(mask, jnp.exp(scores - new_peak[:, :, None]), 0.0), axis=2)
            return (new_peak, total * jnp.exp(peak - new_peak) + fresh)

        return (lax.cond(jnp.any(blocks > 0), one_update, unchanged, state), None)

    peak, total = lax.scan(
        one_frame, (start_peak, start_total), (stacked, jnp.arange(count, dtype=jnp.int32))
    )[0]
    log_total = peak + jnp.log(total)
    zeros3 = jnp.zeros(shape3, jnp.float32)
    home_blocks = pair_blocks(block_live, frame_order, slot_self, slot_self)
    home_query, home_key, home_value = pair_grads(
        query3, key3, value3, grad3, log_total, delta_rows, pair_mask(home_blocks, length), scale
    )
    log_first, delta_first = passed_along((log_total, delta_rows), "frame", 1)

    def cycle_turn(step, state):
        query_c, grad_c, log_c, delta_c, query_acc, key_acc, value_acc = state
        query_c, grad_c = passed_along((query_c, grad_c), "frame", 1)
        slot_query = (slot_self - step) % frames
        blocks = pair_blocks(block_live, frame_order, slot_query, slot_self)

        def cycle_update(totals):
            terms = pair_grads(
                query_c, key3, value3, grad_c, log_c, delta_c, pair_mask(blocks, length), scale
            )
            return tuple((summed + addend for summed, addend in zip(totals, terms)))

        query_acc, key_acc, value_acc = lax.cond(
            jnp.any(blocks > 0), cycle_update, unchanged, (query_acc, key_acc, value_acc)
        )
        query_acc, log_c, delta_c = passed_along((query_acc, log_c, delta_c), "frame", 1)
        return (query_c, grad_c, log_c, delta_c, query_acc, key_acc, value_acc)

    start = (query3, grad3, log_first, delta_first, zeros3, home_key, home_value)
    final = lax.fori_loop(1, frames, cycle_turn, start)
    grad_query_all = home_query + final[4]
    grad_key_all, grad_value_all = (final[5], final[6])
    width = head_here * HEAD_DIM
    grad_query_low = grad_query_all.reshape(length, width).astype(jnp.bfloat16)
    grad_key_low = grad_key_all.reshape(length, width).astype(jnp.bfloat16)
    grad_value_low = grad_value_all.reshape(length, width).astype(jnp.bfloat16)
    return (grad_query_low, grad_key_low, grad_value_low)


def solution(mesh):
    in_specs = (
        P(("frame", "head"), None),
        P(("frame", "head"), None),
        P(("frame", "head"), None),
        P(("frame", "head"), None),
        P(("frame", "head"), None),
        P(),
        P(),
    )
    out_specs = (P("frame", "head"), P("frame", "head"), P("frame", "head"))
    return jax.shard_map(local, mesh=mesh, in_specs=in_specs, out_specs=out_specs, check_vma=False)
```

profile of v0, /device:TPU:1, one launch (start us, length us, event | category | flops | bytes accessed | tf_op | source)
XLA Modules:
  0.0 892.9 jit_solution(6110817460217224592)
XLA Ops:
  8.6 18.1 %all_to_all.80 = bf16[128,8,256]{0,2,1:T(8,128)(2,1)S(1)} all-to-all(bf16[128,8,256]{0,2,1:T(8,128)(2,1)S(1)} %bitcast.134), channel_id=1, replica_groups=mesh['head'=8,'frame'=16] {'head'}, dimensions={1} | all-to-all | bytes 1048576 | tf_op jit(solution)/shard_map/all_to_all | solution.py:58
  35.3 6.7 all-to-all-done
  47.6 10.4 %all-to-all-done.3 = bf16[128,8,256]{0,2,1:T(8,128)(2,1)S(1)} async-done(((bf16[128,8,256]{0,2,1:T(8,128)(2,1)}), bf16[128,8,256]{0,2,1:T(8,128)(2,1)S(1)}, u32[]{:S(2)}, u32[]{:S(2)}) %all-to-all-start.3) | async-done | bytes 524320 | tf_op jit(solution)/shard_map/all_to_all | solution.py:59
  63.1 11.5 %all-to-all-done.4 = bf16[128,8,256]{0,2,1:T(8,128)(2,1)S(1)} async-done(((bf16[128,8,256]{0,2,1:T(8,128)(2,1)}), bf16[128,8,256]{0,2,1:T(8,128)(2,1)S(1)}, u32[]{:S(2)}, u32[]{:S(2)}) %all-to-all-start.4) | async-done | bytes 524320 | tf_op jit(solution)/shard_map/all_to_all | solution.py:61
  96.8 4.6 fusion.37
  101.3 12.6 %reshape.82 = bf16[16,1024,2,128]{3,2,1,0:T(2,128)(2,1)} reshape(bf16[16384,256]{1,0:T(8,128)(2,1)} %all-gather.2.cloned.1.call-done) | data formatting | bytes 16777216 | tf_op jit(solution)/shard_map/reshape | solution.py:75
  113.9 8.6 copy.104
  122.5 133.2 %while.41 = (s32[]{:T(128)}, f32[2,1024]{1,0:T(2,128)S(1)}, f32[2,1024]{1,0:T(2,128)S(1)}, s32[16]{0:T(128)S(1)}, s32[16]{0:T(128)S(1)}, /*index=5*/s32[1]{0:T(1...) while((s32[]{:T(128)}, f32[2,1024]{1,0:T(2,128)S(1)}, ...), condition=%wide.region_6.7_spmd, body=%wide.region_0.6_spmd.sunk | while | flops 551555264 | bytes 23177424 | solution.py:93
  128.2 6.0 conditional.4
  139.9 6.0 conditional.4
  163.0 6.0 conditional.4
  174.7 6.0 conditional.4
  186.4 6.0 conditional.4
  220.9 6.0 conditional.4
  238.3 6.0 conditional.4
  256.1 8.1 fusion.28
  264.2 5.4 multiply_convert_fusion.1
  273.3 606.9 %while.42 = (s32[]{:T(128)}, bf16[1024,2,128]{2,0,1:T(8,128)(2,1)}, bf16[1024,2,128]{2,0,1:T(8,128)(2,1)}, f32[2,1024]{1,0:T(2,128)S(1)}, f32[2,1024]{1,0:T(2,12...) while((s32[]{:T(128)}, bf16[1024,2,128]{2,0,1:T(8,128)(2,1)}, ...), condition=%wide.region_12.13_spmd, body=%wide.region_8.12_spmd.sunk | while | flops 2706637056 | bytes 76146352 | solution.py:123
  277.0 8.1 collective-permute-done.1
  285.7 14.2 %conditional.5 = ((f32[1024,2,128]{2,0,1:T(8,128)S(1)}, f32[1024,2,128]{2,0,1:T(8,128)S(1)}, f32[1024,2,128]{2,0,1:T(8,128)})) conditional(s32[]{:T(128)} %convert_element_type.93, (f32[1024,2,128]{2,0,1:T(8,128)S(1)}, f32[1024,2,128]{2,0,1:T(8,128)S(1)}, f32[1024,2,128]{2,0,1:T(8,128)}) %tuple.106, (s32[8,8]{1,0:T(8,128)S(1)}, ...), branch_computations={%region_10.10_spmd, %region_11.11_spmd} | conditional | flops 2706636800 | bytes 63463924 | solution.py:116
  287.9 4.5 fusion.19
  300.0 13.8 %collective-permute-start.2 = (f32[2,1024]{1,0:T(2,128)S(1)}, f32[2,1024]{1,0:T(2,128)S(1)}, u32[]{:S(2)}, u32[]{:S(2)}) collective-permute-start(f32[2,1024]{1,0:T(2,128)S(1)} %copy.187), channel_id=1, source_target_pairs={{0,1},{1,2},{2,3},{3,4},{4,5},{5,6},{6,7},{7,8},{8,9},{9,10},{10,1... | collective-permute-start | bytes 24584 | tf_op jit(solution)/shard_map/while/body/eval_jaxpr/ppermute | solution.py:13
  317.0 8.8 collective-permute-start
  334.5 5.7 collective-permute-start.2
  349.6 12.8 %collective-permute-start = (bf16[1024,2,128]{2,0,1:T(8,128)(2,1)}, bf16[1024,2,128]{2,0,1:T(8,128)(2,1)S(1)}, u32[]{:S(2)}, u32[]{:S(2)}) collective-permute-start(bf16[1024,2,128]{2,0,1:T(8,128)(2,1)} %get-tuple-element.934), channel_id=1, source_target_pairs={{0,1},{1,2},{2,3},{3,4},{4,5},{5,6},{6,7},{7,8},{8,9},{9,10},{10,1... | collective-permute-start | bytes 1572872 | tf_op jit(solution)/shard_map/while/body/eval_jaxpr/ppermute | solution.py:13
  368.8 16.7 %collective-permute-start.4 = (f32[1024,2,128]{2,0,1:T(8,128)S(1)}, f32[1024,2,128]{2,0,1:T(8,128)S(1)}, u32[]{:S(2)}, u32[]{:S(2)}) collective-permute-start(f32[1024,2,128]{2,0,1:T(8,128)S(1)} %get-tuple-element.866), channel_id=1, source_target_pairs={{0,1},{1,2},{2,3},{3,4},{4,5},{5,6},{6,7},{7,8},{8,9},{9,10},{10,1... | collective-permute-start | bytes 3145736 | tf_op jit(solution)/shard_map/while/body/eval_jaxpr/ppermute | solution.py:13
  385.6 9.0 %collective-permute-start.3 = (f32[2,1024]{1,0:T(2,128)S(1)}, f32[2,1024]{1,0:T(2,128)S(1)}, u32[]{:S(2)}, u32[]{:S(2)}) collective-permute-start(f32[2,1024]{1,0:T(2,128)S(1)} %copy.188), channel_id=1, source_target_pairs={{0,1},{1,2},{2,3},{3,4},{4,5},{5,6},{6,7},{7,8},{8,9},{9,10},{10,1... | collective-permute-start | bytes 24584 | tf_op jit(solution)/shard_map/while/body/eval_jaxpr/ppermute | solution.py:13
  399.9 6.6 collective-permute-start
  412.9 14.2 %conditional.5 = ((f32[1024,2,128]{2,0,1:T(8,128)S(1)}, f32[1024,2,128]{2,0,1:T(8,128)S(1)}, f32[1024,2,128]{2,0,1:T(8,128)})) conditional(s32[]{:T(128)} %convert_element_type.93, (f32[1024,2,128]{2,0,1:T(8,128)S(1)}, f32[1024,2,128]{2,0,1:T(8,128)S(1)}, f32[1024,2,128]{2,0,1:T(8,128)}) %tuple.106, (s32[8,8]{1,0:T(8,128)S(1)}, ...), branch_computations={%region_10.10_spmd, %region_11.11_spmd} | conditional | flops 2706636800 | bytes 63463924 | solution.py:116
  415.1 4.5 fusion.19
  429.6 5.7 collective-permute-start.2
  450.5 5.2 collective-permute-done.1
  458.5 17.7 %collective-permute-start.2 = (f32[2,1024]{1,0:T(2,128)S(1)}, f32[2,1024]{1,0:T(2,128)S(1)}, u32[]{:S(2)}, u32[]{:S(2)}) collective-permute-start(f32[2,1024]{1,0:T(2,128)S(1)} %copy.187), channel_id=1, source_target_pairs={{0,1},{1,2},{2,3},{3,4},{4,5},{5,6},{6,7},{7,8},{8,9},{9,10},{10,1... | collective-permute-start | bytes 24584 | tf_op jit(solution)/shard_map/while/body/eval_jaxpr/ppermute | solution.py:13
  478.9 8.1 collective-permute-done.4
  491.3 11.8 %collective-permute-done.1 = bf16[1024,2,128]{2,0,1:T(8,128)(2,1)} collective-permute-done((bf16[1024,2,128]{2,0,1:T(8,128)(2,1)}, bf16[1024,2,128]{2,0,1:T(8,128)(2,1)}, u32[]{:S(2)}, u32[]{:S(2)}) %collective-permute-start.1) | collective-permute-done | bytes 524320 | tf_op jit(solution)/shard_map/while/body/eval_jaxpr/ppermute | solution.py:13
  503.7 14.2 %conditional.5 = ((f32[1024,2,128]{2,0,1:T(8,128)S(1)}, f32[1024,2,128]{2,0,1:T(8,128)S(1)}, f32[1024,2,128]{2,0,1:T(8,128)})) conditional(s32[]{:T(128)} %convert_element_type.93, (f32[1024,2,128]{2,0,1:T(8,128)S(1)}, f32[1024,2,128]{2,0,1:T(8,128)S(1)}, f32[1024,2,128]{2,0,1:T(8,128)}) %tuple.106, (s32[8,8]{1,0:T(8,128)S(1)}, ...), branch_computations={%region_10.10_spmd, %region_11.11_spmd} | conditional | flops 2706636800 | bytes 63463924 | solution.py:116
  505.9 4.5 fusion.19
  520.9 8.9 collective-permute-done.4
  538.9 5.6 collective-permute-done
  553.2 5.5 collective-permute-done.4
  573.4 16.7 %collective-permute-start.4 = (f32[1024,2,128]{2,0,1:T(8,128)S(1)}, f32[1024,2,128]{2,0,1:T(8,128)S(1)}, u32[]{:S(2)}, u32[]{:S(2)}) collective-permute-start(f32[1024,2,128]{2,0,1:T(8,128)S(1)} %get-tuple-element.866), channel_id=1, source_target_pairs={{0,1},{1,2},{2,3},{3,4},{4,5},{5,6},{6,7},{7,8},{8,9},{9,10},{10,1... | collective-permute-start | bytes 3145736 | tf_op jit(solution)/shard_map/while/body/eval_jaxpr/ppermute | solution.py:13
  592.9 8.9 collective-permute-done.4
  610.9 5.6 collective-permute-done
  625.1 5.5 collective-permute-done.4
  639.7 5.6 collective-permute-done
  645.3 16.7 %collective-permute-start.4 = (f32[1024,2,128]{2,0,1:T(8,128)S(1)}, f32[1024,2,128]{2,0,1:T(8,128)S(1)}, u32[]{:S(2)}, u32[]{:S(2)}) collective-permute-start(f32[1024,2,128]{2,0,1:T(8,128)S(1)} %get-tuple-element.866), channel_id=1, source_target_pairs={{0,1},{1,2},{2,3},{3,4},{4,5},{5,6},{6,7},{7,8},{8,9},{9,10},{10,1... | collective-permute-start | bytes 3145736 | tf_op jit(solution)/shard_map/while/body/eval_jaxpr/ppermute | solution.py:13
  664.9 8.9 collective-permute-done.4
  682.9 5.6 collective-permute-done
  688.5 14.2 %conditional.5 = ((f32[1024,2,128]{2,0,1:T(8,128)S(1)}, f32[1024,2,128]{2,0,1:T(8,128)S(1)}, f32[1024,2,128]{2,0,1:T(8,128)})) conditional(s32[]{:T(128)} %convert_element_type.93, (f32[1024,2,128]{2,0,1:T(8,128)S(1)}, f32[1024,2,128]{2,0,1:T(8,128)S(1)}, f32[1024,2,128]{2,0,1:T(8,128)}) %tuple.106, (s32[8,8]{1,0:T(8,128)S(1)}, ...), branch_computations={%region_10.10_spmd, %region_11.11_spmd} | conditional | flops 2706636800 | bytes 63463924 | solution.py:116
  690.7 4.5 fusion.19
  708.0 8.9 collective-permute-done.4
  722.9 7.2 collective-permute-done.1
  731.6 14.2 %conditional.5 = ((f32[1024,2,128]{2,0,1:T(8,128)S(1)}, f32[1024,2,128]{2,0,1:T(8,128)S(1)}, f32[1024,2,128]{2,0,1:T(8,128)})) conditional(s32[]{:T(128)} %convert_element_type.93, (f32[1024,2,128]{2,0,1:T(8,128)S(1)}, f32[1024,2,128]{2,0,1:T(8,128)S(1)}, f32[1024,2,128]{2,0,1:T(8,128)}) %tuple.106, (s32[8,8]{1,0:T(8,128)S(1)}, ...), branch_computations={%region_10.10_spmd, %region_11.11_spmd} | conditional | flops 2706636800 | bytes 63463924 | solution.py:116
  733.8 4.5 fusion.19
  748.8 8.9 collective-permute-done.4
  763.7 9.3 %collective-permute-done.1 = bf16[1024,2,128]{2,0,1:T(8,128)(2,1)} collective-permute-done((bf16[1024,2,128]{2,0,1:T(8,128)(2,1)}, bf16[1024,2,128]{2,0,1:T(8,128)(2,1)}, u32[]{:S(2)}, u32[]{:S(2)}) %collective-permute-start.1) | collective-permute-done | bytes 524320 | tf_op jit(solution)/shard_map/while/body/eval_jaxpr/ppermute | solution.py:13
  773.6 14.2 %conditional.5 = ((f32[1024,2,128]{2,0,1:T(8,128)S(1)}, f32[1024,2,128]{2,0,1:T(8,128)S(1)}, f32[1024,2,128]{2,0,1:T(8,128)})) conditional(s32[]{:T(128)} %convert_element_type.93, (f32[1024,2,128]{2,0,1:T(8,128)S(1)}, f32[1024,2,128]{2,0,1:T(8,128)S(1)}, f32[1024,2,128]{2,0,1:T(8,128)}) %tuple.106, (s32[8,8]{1,0:T(8,128)S(1)}, ...), branch_computations={%region_10.10_spmd, %region_11.11_spmd} | conditional | flops 2706636800 | bytes 63463924 | solution.py:116
  775.7 4.5 fusion.19
  790.7 8.9 collective-permute-done.4
  805.6 10.2 %collective-permute-done.1 = bf16[1024,2,128]{2,0,1:T(8,128)(2,1)} collective-permute-done((bf16[1024,2,128]{2,0,1:T(8,128)(2,1)}, bf16[1024,2,128]{2,0,1:T(8,128)(2,1)}, u32[]{:S(2)}, u32[]{:S(2)}) %collective-permute-start.1) | collective-permute-done | bytes 524320 | tf_op jit(solution)/shard_map/while/body/eval_jaxpr/ppermute | solution.py:13
  819.5 13.3 %collective-permute-done.4 = f32[1024,2,128]{2,0,1:T(8,128)S(1)} collective-permute-done((f32[1024,2,128]{2,0,1:T(8,128)S(1)}, f32[1024,2,128]{2,0,1:T(8,128)S(1)}, u32[]{:S(2)}, u32[]{:S(2)}) %collective-permute-start.4) | collective-permute-done | bytes 1048608 | tf_op jit(solution)/shard_map/while/body/eval_jaxpr/ppermute | solution.py:13
  836.3 12.6 %collective-permute-done.1 = bf16[1024,2,128]{2,0,1:T(8,128)(2,1)} collective-permute-done((bf16[1024,2,128]{2,0,1:T(8,128)(2,1)}, bf16[1024,2,128]{2,0,1:T(8,128)(2,1)}, u32[]{:S(2)}, u32[]{:S(2)}) %collective-permute-start.1) | collective-permute-done | bytes 524320 | tf_op jit(solution)/shard_map/while/body/eval_jaxpr/ppermute | solution.py:13
  849.5 12.2 %collective-permute-start.4 = (f32[1024,2,128]{2,0,1:T(8,128)S(1)}, f32[1024,2,128]{2,0,1:T(8,128)S(1)}, u32[]{:S(2)}, u32[]{:S(2)}) collective-permute-start(f32[1024,2,128]{2,0,1:T(8,128)S(1)} %get-tuple-element.866), channel_id=1, source_target_pairs={{0,1},{1,2},{2,3},{3,4},{4,5},{5,6},{6,7},{7,8},{8,9},{9,10},{10,1... | collective-permute-start | bytes 3145736 | tf_op jit(solution)/shard_map/while/body/eval_jaxpr/ppermute | solution.py:13
  864.6 15.6 %collective-permute-done.4 = f32[1024,2,128]{2,0,1:T(8,128)S(1)} collective-permute-done((f32[1024,2,128]{2,0,1:T(8,128)S(1)}, f32[1024,2,128]{2,0,1:T(8,128)S(1)}, u32[]{:S(2)}, u32[]{:S(2)}) %collective-permute-start.4) | collective-permute-done | bytes 1048608 | tf_op jit(solution)/shard_map/while/body/eval_jaxpr/ppermute | solution.py:13
  (503 shorter events, 343.2 us)
Async XLA Ops:
  7.2 94.1 %all-gather.2.cloned.1.call-start = ((), (), s32[]{:S(2)}) async-start(), calls=%async_computation.5 | async-start | bytes 8912896 | tf_op jit(solution)/shard_map/all_gather | solution.py:73
  29.8 12.3 %all-to-all-start = ((bf16[128,8,256]{0,2,1:T(8,128)(2,1)}), bf16[128,8,256]{0,2,1:T(8,128)(2,1)S(1)}, u32[]{:S(2)}, u32[]{:S(2)}) async-start(bf16[128,8,256]{0,2,1:T(8,128)(2,1)} %bitcast.11), calls=%async_computation | async-start | bytes 1048576 | tf_op jit(solution)/shard_map/all_to_all | solution.py:57
  42.0 16.0 %all-to-all-start.3 = ((bf16[128,8,256]{0,2,1:T(8,128)(2,1)}), bf16[128,8,256]{0,2,1:T(8,128)(2,1)S(1)}, u32[]{:S(2)}, u32[]{:S(2)}) async-start(bf16[128,8,256]{0,2,1:T(8,128)(2,1)} %bitcast.18), calls=%async_computation.3 | async-start | bytes 1048576 | tf_op jit(solution)/shard_map/all_to_all | solution.py:59
  58.0 16.6 %all-to-all-start.4 = ((bf16[128,8,256]{0,2,1:T(8,128)(2,1)}), bf16[128,8,256]{0,2,1:T(8,128)(2,1)S(1)}, u32[]{:S(2)}, u32[]{:S(2)}) async-start(bf16[128,8,256]{0,2,1:T(8,128)(2,1)} %bitcast.20), calls=%async_computation.4 | async-start | bytes 1048576 | tf_op jit(solution)/shard_map/all_to_all | solution.py:61
  74.6 17.3 %all-to-all-start.2 = ((bf16[128,8,256]{0,2,1:T(8,128)(2,1)}), bf16[128,8,256]{0,2,1:T(8,128)(2,1)}, u32[]{:S(2)}, u32[]{:S(2)}) async-start(bf16[128,8,256]{0,2,1:T(8,128)(2,1)} %bitcast.16), calls=%async_computation.2 | async-start | bytes 1048576 | tf_op jit(solution)/shard_map/all_to_all | solution.py:60
  96.5 176.7 %collective-permute-start.6 = (f32[2,1024]{1,0:T(2,128)S(1)}, f32[2,1024]{1,0:T(2,128)S(1)}, u32[]{:S(2)}, u32[]{:S(2)}) collective-permute-start(f32[2,1024]{1,0:T(2,128)S(1)} %bitcast.139), channel_id=1, source_target_pairs={{0,1},{1,2},{2,3},{3,4},{4,5},{5,6},{6,7},{7,8},{8,9},{9,10},{10,1... | collective-permute-start | bytes 24584 | tf_op jit(solution)/shard_map/ppermute | solution.py:13
  255.8 17.4 %collective-permute-start.5 = (f32[2,1024]{1,0:T(2,128)S(1)}, f32[2,1024]{1,0:T(2,128)S(1)}, u32[]{:S(2)}, u32[]{:S(2)}) collective-permute-start(f32[2,1024]{1,0:T(2,128)S(1)} %log_add_fusion), channel_id=1, source_target_pairs={{0,1},{1,2},{2,3},{3,4},{4,5},{5,6},{6,7},{7,8},{8,9},{9,10},{10,1... | collective-permute-start | bytes 24584 | tf_op jit(solution)/shard_map/ppermute | solution.py:13
  273.6 12.1 %collective-permute-start = (bf16[1024,2,128]{2,0,1:T(8,128)(2,1)}, bf16[1024,2,128]{2,0,1:T(8,128)(2,1)S(1)}, u32[]{:S(2)}, u32[]{:S(2)}) collective-permute-start(bf16[1024,2,128]{2,0,1:T(8,128)(2,1)} %get-tuple-element.934), channel_id=1, source_target_pairs={{0,1},{1,2},{2,3},{3,4},{4,5},{5,6},{6,7},{7,8},{8,9},{9,10},{10,1... | collective-permute-start | bytes 1572872 | tf_op jit(solution)/shard_map/while/body/eval_jaxpr/ppermute | solution.py:13
  300.0 16.6 %collective-permute-start.4 = (f32[1024,2,128]{2,0,1:T(8,128)S(1)}, f32[1024,2,128]{2,0,1:T(8,128)S(1)}, u32[]{:S(2)}, u32[]{:S(2)}) collective-permute-start(f32[1024,2,128]{2,0,1:T(8,128)S(1)} %get-tuple-element.866), channel_id=1, source_target_pairs={{0,1},{1,2},{2,3},{3,4},{4,5},{5,6},{6,7},{7,8},{8,9},{9,10},{10,1... | collective-permute-start | bytes 3145736 | tf_op jit(solution)/shard_map/while/body/eval_jaxpr/ppermute | solution.py:13
  300.0 16.6 %collective-permute-start.2 = (f32[2,1024]{1,0:T(2,128)S(1)}, f32[2,1024]{1,0:T(2,128)S(1)}, u32[]{:S(2)}, u32[]{:S(2)}) collective-permute-start(f32[2,1024]{1,0:T(2,128)S(1)} %copy.187), channel_id=1, source_target_pairs={{0,1},{1,2},{2,3},{3,4},{4,5},{5,6},{6,7},{7,8},{8,9},{9,10},{10,1... | collective-permute-start | bytes 24584 | tf_op jit(solution)/shard_map/while/body/eval_jaxpr/ppermute | solution.py:13
  316.7 15.8 %collective-permute-start.1 = (bf16[1024,2,128]{2,0,1:T(8,128)(2,1)}, bf16[1024,2,128]{2,0,1:T(8,128)(2,1)}, u32[]{:S(2)}, u32[]{:S(2)}) collective-permute-start(bf16[1024,2,128]{2,0,1:T(8,128)(2,1)} %get-tuple-element.935), channel_id=1, source_target_pairs={{0,1},{1,2},{2,3},{3,4},{4,5},{5,6},{6,7},{7,8},{8,9},{9,10},{10,1... | collective-permute-start | bytes 1572872 | tf_op jit(solution)/shard_map/while/body/eval_jaxpr/ppermute | solution.py:13
  317.0 16.1 %collective-permute-start = (bf16[1024,2,128]{2,0,1:T(8,128)(2,1)}, bf16[1024,2,128]{2,0,1:T(8,128)(2,1)S(1)}, u32[]{:S(2)}, u32[]{:S(2)}) collective-permute-start(bf16[1024,2,128]{2,0,1:T(8,128)(2,1)} %get-tuple-element.934), channel_id=1, source_target_pairs={{0,1},{1,2},{2,3},{3,4},{4,5},{5,6},{6,7},{7,8},{8,9},{9,10},{10,1... | collective-permute-start | bytes 1572872 | tf_op jit(solution)/shard_map/while/body/eval_jaxpr/ppermute | solution.py:13
  333.1 16.3 %collective-permute-start.4 = (f32[1024,2,128]{2,0,1:T(8,128)S(1)}, f32[1024,2,128]{2,0,1:T(8,128)S(1)}, u32[]{:S(2)}, u32[]{:S(2)}) collective-permute-start(f32[1024,2,128]{2,0,1:T(8,128)S(1)} %get-tuple-element.866), channel_id=1, source_target_pairs={{0,1},{1,2},{2,3},{3,4},{4,5},{5,6},{6,7},{7,8},{8,9},{9,10},{10,1... | collective-permute-start | bytes 3145736 | tf_op jit(solution)/shard_map/while/body/eval_jaxpr/ppermute | solution.py:13
  334.5 14.9 %collective-permute-start.2 = (f32[2,1024]{1,0:T(2,128)S(1)}, f32[2,1024]{1,0:T(2,128)S(1)}, u32[]{:S(2)}, u32[]{:S(2)}) collective-permute-start(f32[2,1024]{1,0:T(2,128)S(1)} %copy.187), channel_id=1, source_target_pairs={{0,1},{1,2},{2,3},{3,4},{4,5},{5,6},{6,7},{7,8},{8,9},{9,10},{10,1... | collective-permute-start | bytes 24584 | tf_op jit(solution)/shard_map/while/body/eval_jaxpr/ppermute | solution.py:13
  349.5 16.1 %collective-permute-start.1 = (bf16[1024,2,128]{2,0,1:T(8,128)(2,1)}, bf16[1024,2,128]{2,0,1:T(8,128)(2,1)}, u32[]{:S(2)}, u32[]{:S(2)}) collective-permute-start(bf16[1024,2,128]{2,0,1:T(8,128)(2,1)} %get-tuple-element.935), channel_id=1, source_target_pairs={{0,1},{1,2},{2,3},{3,4},{4,5},{5,6},{6,7},{7,8},{8,9},{9,10},{10,1... | collective-permute-start | bytes 1572872 | tf_op jit(solution)/shard_map/while/body/eval_jaxpr/ppermute | solution.py:13
  349.6 19.2 %collective-permute-start = (bf16[1024,2,128]{2,0,1:T(8,128)(2,1)}, bf16[1024,2,128]{2,0,1:T(8,128)(2,1)S(1)}, u32[]{:S(2)}, u32[]{:S(2)}) collective-permute-start(bf16[1024,2,128]{2,0,1:T(8,128)(2,1)} %get-tuple-element.934), channel_id=1, source_target_pairs={{0,1},{1,2},{2,3},{3,4},{4,5},{5,6},{6,7},{7,8},{8,9},{9,10},{10,1... | collective-permute-start | bytes 1572872 | tf_op jit(solution)/shard_map/while/body/eval_jaxpr/ppermute | solution.py:13
  368.8 28.4 %collective-permute-start.4 = (f32[1024,2,128]{2,0,1:T(8,128)S(1)}, f32[1024,2,128]{2,0,1:T(8,128)S(1)}, u32[]{:S(2)}, u32[]{:S(2)}) collective-permute-start(f32[1024,2,128]{2,0,1:T(8,128)S(1)} %get-tuple-element.866), channel_id=1, source_target_pairs={{0,1},{1,2},{2,3},{3,4},{4,5},{5,6},{6,7},{7,8},{8,9},{9,10},{10,1... | collective-permute-start | bytes 3145736 | tf_op jit(solution)/shard_map/while/body/eval_jaxpr/ppermute | solution.py:13
  385.5 11.8 %collective-permute-start.2 = (f32[2,1024]{1,0:T(2,128)S(1)}, f32[2,1024]{1,0:T(2,128)S(1)}, u32[]{:S(2)}, u32[]{:S(2)}) collective-permute-start(f32[2,1024]{1,0:T(2,128)S(1)} %copy.187), channel_id=1, source_target_pairs={{0,1},{1,2},{2,3},{3,4},{4,5},{5,6},{6,7},{7,8},{8,9},{9,10},{10,1... | collective-permute-start | bytes 24584 | tf_op jit(solution)/shard_map/while/body/eval_jaxpr/ppermute | solution.py:13
  385.6 11.8 %collective-permute-start.3 = (f32[2,1024]{1,0:T(2,128)S(1)}, f32[2,1024]{1,0:T(2,128)S(1)}, u32[]{:S(2)}, u32[]{:S(2)}) collective-permute-start(f32[2,1024]{1,0:T(2,128)S(1)} %copy.188), channel_id=1, source_target_pairs={{0,1},{1,2},{2,3},{3,4},{4,5},{5,6},{6,7},{7,8},{8,9},{9,10},{10,1... | collective-permute-start | bytes 24584 | tf_op jit(solution)/shard_map/while/body/eval_jaxpr/ppermute | solution.py:13
  397.4 12.3 %collective-permute-start.1 = (bf16[1024,2,128]{2,0,1:T(8,128)(2,1)}, bf16[1024,2,128]{2,0,1:T(8,128)(2,1)}, u32[]{:S(2)}, u32[]{:S(2)}) collective-permute-start(bf16[1024,2,128]{2,0,1:T(8,128)(2,1)} %get-tuple-element.935), channel_id=1, source_target_pairs={{0,1},{1,2},{2,3},{3,4},{4,5},{5,6},{6,7},{7,8},{8,9},{9,10},{10,1... | collective-permute-start | bytes 1572872 | tf_op jit(solution)/shard_map/while/body/eval_jaxpr/ppermute | solution.py:13
  399.9 13.0 %collective-permute-start = (bf16[1024,2,128]{2,0,1:T(8,128)(2,1)}, bf16[1024,2,128]{2,0,1:T(8,128)(2,1)S(1)}, u32[]{:S(2)}, u32[]{:S(2)}) collective-permute-start(bf16[1024,2,128]{2,0,1:T(8,128)(2,1)} %get-tuple-element.934), channel_id=1, source_target_pairs={{0,1},{1,2},{2,3},{3,4},{4,5},{5,6},{6,7},{7,8},{8,9},{9,10},{10,1... | collective-permute-start | bytes 1572872 | tf_op jit(solution)/shard_map/while/body/eval_jaxpr/ppermute | solution.py:13
  427.2 14.2 %collective-permute-start.4 = (f32[1024,2,128]{2,0,1:T(8,128)S(1)}, f32[1024,2,128]{2,0,1:T(8,128)S(1)}, u32[]{:S(2)}, u32[]{:S(2)}) collective-permute-start(f32[1024,2,128]{2,0,1:T(8,128)S(1)} %get-tuple-element.866), channel_id=1, source_target_pairs={{0,1},{1,2},{2,3},{3,4},{4,5},{5,6},{6,7},{7,8},{8,9},{9,10},{10,1... | collective-permute-start | bytes 3145736 | tf_op jit(solution)/shard_map/while/body/eval_jaxpr/ppermute | solution.py:13
  429.6 11.8 %collective-permute-start.2 = (f32[2,1024]{1,0:T(2,128)S(1)}, f32[2,1024]{1,0:T(2,128)S(1)}, u32[]{:S(2)}, u32[]{:S(2)}) collective-permute-start(f32[2,1024]{1,0:T(2,128)S(1)} %copy.187), channel_id=1, source_target_pairs={{0,1},{1,2},{2,3},{3,4},{4,5},{5,6},{6,7},{7,8},{8,9},{9,10},{10,1... | collective-permute-start | bytes 24584 | tf_op jit(solution)/shard_map/while/body/eval_jaxpr/ppermute | solution.py:13
  441.5 14.2 %collective-permute-start.1 = (bf16[1024,2,128]{2,0,1:T(8,128)(2,1)}, bf16[1024,2,128]{2,0,1:T(8,128)(2,1)}, u32[]{:S(2)}, u32[]{:S(2)}) collective-permute-start(bf16[1024,2,128]{2,0,1:T(8,128)(2,1)} %get-tuple-element.935), channel_id=1, source_target_pairs={{0,1},{1,2},{2,3},{3,4},{4,5},{5,6},{6,7},{7,8},{8,9},{9,10},{10,1... | collective-permute-start | bytes 1572872 | tf_op jit(solution)/shard_map/while/body/eval_jaxpr/ppermute | solution.py:13
  444.0 12.4 %collective-permute-start = (bf16[1024,2,128]{2,0,1:T(8,128)(2,1)}, bf16[1024,2,128]{2,0,1:T(8,128)(2,1)S(1)}, u32[]{:S(2)}, u32[]{:S(2)}) collective-permute-start(bf16[1024,2,128]{2,0,1:T(8,128)(2,1)} %get-tuple-element.934), channel_id=1, source_target_pairs={{0,1},{1,2},{2,3},{3,4},{4,5},{5,6},{6,7},{7,8},{8,9},{9,10},{10,1... | collective-permute-start | bytes 1572872 | tf_op jit(solution)/shard_map/while/body/eval_jaxpr/ppermute | solution.py:13
  456.4 30.6 %collective-permute-start.4 = (f32[1024,2,128]{2,0,1:T(8,128)S(1)}, f32[1024,2,128]{2,0,1:T(8,128)S(1)}, u32[]{:S(2)}, u32[]{:S(2)}) collective-permute-start(f32[1024,2,128]{2,0,1:T(8,128)S(1)} %get-tuple-element.866), channel_id=1, source_target_pairs={{0,1},{1,2},{2,3},{3,4},{4,5},{5,6},{6,7},{7,8},{8,9},{9,10},{10,1... | collective-permute-start | bytes 3145736 | tf_op jit(solution)/shard_map/while/body/eval_jaxpr/ppermute | solution.py:13
  458.5 28.6 %collective-permute-start.2 = (f32[2,1024]{1,0:T(2,128)S(1)}, f32[2,1024]{1,0:T(2,128)S(1)}, u32[]{:S(2)}, u32[]{:S(2)}) collective-permute-start(f32[2,1024]{1,0:T(2,128)S(1)} %copy.187), channel_id=1, source_target_pairs={{0,1},{1,2},{2,3},{3,4},{4,5},{5,6},{6,7},{7,8},{8,9},{9,10},{10,1... | collective-permute-start | bytes 24584 | tf_op jit(solution)/shard_map/while/body/eval_jaxpr/ppermute | solution.py:13
  487.1 16.0 %collective-permute-start.1 = (bf16[1024,2,128]{2,0,1:T(8,128)(2,1)}, bf16[1024,2,128]{2,0,1:T(8,128)(2,1)}, u32[]{:S(2)}, u32[]{:S(2)}) collective-permute-start(bf16[1024,2,128]{2,0,1:T(8,128)(2,1)} %get-tuple-element.935), channel_id=1, source_target_pairs={{0,1},{1,2},{2,3},{3,4},{4,5},{5,6},{6,7},{7,8},{8,9},{9,10},{10,1... | collective-permute-start | bytes 1572872 | tf_op jit(solution)/shard_map/while/body/eval_jaxpr/ppermute | solution.py:13
  487.2 16.5 %collective-permute-start = (bf16[1024,2,128]{2,0,1:T(8,128)(2,1)}, bf16[1024,2,128]{2,0,1:T(8,128)(2,1)S(1)}, u32[]{:S(2)}, u32[]{:S(2)}) collective-permute-start(bf16[1024,2,128]{2,0,1:T(8,128)(2,1)} %get-tuple-element.934), channel_id=1, source_target_pairs={{0,1},{1,2},{2,3},{3,4},{4,5},{5,6},{6,7},{7,8},{8,9},{9,10},{10,1... | collective-permute-start | bytes 1572872 | tf_op jit(solution)/shard_map/while/body/eval_jaxpr/ppermute | solution.py:13
  518.1 11.8 %collective-permute-start.3 = (f32[2,1024]{1,0:T(2,128)S(1)}, f32[2,1024]{1,0:T(2,128)S(1)}, u32[]{:S(2)}, u32[]{:S(2)}) collective-permute-start(f32[2,1024]{1,0:T(2,128)S(1)} %copy.188), channel_id=1, source_target_pairs={{0,1},{1,2},{2,3},{3,4},{4,5},{5,6},{6,7},{7,8},{8,9},{9,10},{10,1... | collective-permute-start | bytes 24584 | tf_op jit(solution)/shard_map/while/body/eval_jaxpr/ppermute | solution.py:13
  532.5 12.1 %collective-permute-start = (bf16[1024,2,128]{2,0,1:T(8,128)(2,1)}, bf16[1024,2,128]{2,0,1:T(8,128)(2,1)S(1)}, u32[]{:S(2)}, u32[]{:S(2)}) collective-permute-start(bf16[1024,2,128]{2,0,1:T(8,128)(2,1)} %get-tuple-element.934), channel_id=1, source_target_pairs={{0,1},{1,2},{2,3},{3,4},{4,5},{5,6},{6,7},{7,8},{8,9},{9,10},{10,1... | collective-permute-start | bytes 1572872 | tf_op jit(solution)/shard_map/while/body/eval_jaxpr/ppermute | solution.py:13
  544.5 14.1 %collective-permute-start.4 = (f32[1024,2,128]{2,0,1:T(8,128)S(1)}, f32[1024,2,128]{2,0,1:T(8,128)S(1)}, u32[]{:S(2)}, u32[]{:S(2)}) collective-permute-start(f32[1024,2,128]{2,0,1:T(8,128)S(1)} %get-tuple-element.866), channel_id=1, source_target_pairs={{0,1},{1,2},{2,3},{3,4},{4,5},{5,6},{6,7},{7,8},{8,9},{9,10},{10,1... | collective-permute-start | bytes 3145736 | tf_op jit(solution)/shard_map/while/body/eval_jaxpr/ppermute | solution.py:13
  546.9 11.8 %collective-permute-start.2 = (f32[2,1024]{1,0:T(2,128)S(1)}, f32[2,1024]{1,0:T(2,128)S(1)}, u32[]{:S(2)}, u32[]{:S(2)}) collective-permute-start(f32[2,1024]{1,0:T(2,128)S(1)} %copy.187), channel_id=1, source_target_pairs={{0,1},{1,2},{2,3},{3,4},{4,5},{5,6},{6,7},{7,8},{8,9},{9,10},{10,1... | collective-permute-start | bytes 24584 | tf_op jit(solution)/shard_map/while/body/eval_jaxpr/ppermute | solution.py:13
  561.3 12.1 %collective-permute-start = (bf16[1024,2,128]{2,0,1:T(8,128)(2,1)}, bf16[1024,2,128]{2,0,1:T(8,128)(2,1)S(1)}, u32[]{:S(2)}, u32[]{:S(2)}) collective-permute-start(bf16[1024,2,128]{2,0,1:T(8,128)(2,1)} %get-tuple-element.934), channel_id=1, source_target_pairs={{0,1},{1,2},{2,3},{3,4},{4,5},{5,6},{6,7},{7,8},{8,9},{9,10},{10,1... | collective-permute-start | bytes 1572872 | tf_op jit(solution)/shard_map/while/body/eval_jaxpr/ppermute | solution.py:13
  573.4 28.4 %collective-permute-start.4 = (f32[1024,2,128]{2,0,1:T(8,128)S(1)}, f32[1024,2,128]{2,0,1:T(8,128)S(1)}, u32[]{:S(2)}, u32[]{:S(2)}) collective-permute-start(f32[1024,2,128]{2,0,1:T(8,128)S(1)} %get-tuple-element.866), channel_id=1, source_target_pairs={{0,1},{1,2},{2,3},{3,4},{4,5},{5,6},{6,7},{7,8},{8,9},{9,10},{10,1... | collective-permute-start | bytes 3145736 | tf_op jit(solution)/shard_map/while/body/eval_jaxpr/ppermute | solution.py:13
  590.0 11.8 %collective-permute-start.2 = (f32[2,1024]{1,0:T(2,128)S(1)}, f32[2,1024]{1,0:T(2,128)S(1)}, u32[]{:S(2)}, u32[]{:S(2)}) collective-permute-start(f32[2,1024]{1,0:T(2,128)S(1)} %copy.187), channel_id=1, source_target_pairs={{0,1},{1,2},{2,3},{3,4},{4,5},{5,6},{6,7},{7,8},{8,9},{9,10},{10,1... | collective-permute-start | bytes 24584 | tf_op jit(solution)/shard_map/while/body/eval_jaxpr/ppermute | solution.py:13
  590.1 11.8 %collective-permute-start.3 = (f32[2,1024]{1,0:T(2,128)S(1)}, f32[2,1024]{1,0:T(2,128)S(1)}, u32[]{:S(2)}, u32[]{:S(2)}) collective-permute-start(f32[2,1024]{1,0:T(2,128)S(1)} %copy.188), channel_id=1, source_target_pairs={{0,1},{1,2},{2,3},{3,4},{4,5},{5,6},{6,7},{7,8},{8,9},{9,10},{10,1... | collective-permute-start | bytes 24584 | tf_op jit(solution)/shard_map/while/body/eval_jaxpr/ppermute | solution.py:13
  604.4 12.1 %collective-permute-start = (bf16[1024,2,128]{2,0,1:T(8,128)(2,1)}, bf16[1024,2,128]{2,0,1:T(8,128)(2,1)S(1)}, u32[]{:S(2)}, u32[]{:S(2)}) collective-permute-start(bf16[1024,2,128]{2,0,1:T(8,128)(2,1)} %get-tuple-element.934), channel_id=1, source_target_pairs={{0,1},{1,2},{2,3},{3,4},{4,5},{5,6},{6,7},{7,8},{8,9},{9,10},{10,1... | collective-permute-start | bytes 1572872 | tf_op jit(solution)/shard_map/while/body/eval_jaxpr/ppermute | solution.py:13
  616.5 14.1 %collective-permute-start.4 = (f32[1024,2,128]{2,0,1:T(8,128)S(1)}, f32[1024,2,128]{2,0,1:T(8,128)S(1)}, u32[]{:S(2)}, u32[]{:S(2)}) collective-permute-start(f32[1024,2,128]{2,0,1:T(8,128)S(1)} %get-tuple-element.866), channel_id=1, source_target_pairs={{0,1},{1,2},{2,3},{3,4},{4,5},{5,6},{6,7},{7,8},{8,9},{9,10},{10,1... | collective-permute-start | bytes 3145736 | tf_op jit(solution)/shard_map/while/body/eval_jaxpr/ppermute | solution.py:13
  618.9 11.8 %collective-permute-start.2 = (f32[2,1024]{1,0:T(2,128)S(1)}, f32[2,1024]{1,0:T(2,128)S(1)}, u32[]{:S(2)}, u32[]{:S(2)}) collective-permute-start(f32[2,1024]{1,0:T(2,128)S(1)} %copy.187), channel_id=1, source_target_pairs={{0,1},{1,2},{2,3},{3,4},{4,5},{5,6},{6,7},{7,8},{8,9},{9,10},{10,1... | collective-permute-start | bytes 24584 | tf_op jit(solution)/shard_map/while/body/eval_jaxpr/ppermute | solution.py:13
  633.3 12.1 %collective-permute-start = (bf16[1024,2,128]{2,0,1:T(8,128)(2,1)}, bf16[1024,2,128]{2,0,1:T(8,128)(2,1)S(1)}, u32[]{:S(2)}, u32[]{:S(2)}) collective-permute-start(bf16[1024,2,128]{2,0,1:T(8,128)(2,1)} %get-tuple-element.934), channel_id=1, source_target_pairs={{0,1},{1,2},{2,3},{3,4},{4,5},{5,6},{6,7},{7,8},{8,9},{9,10},{10,1... | collective-permute-start | bytes 1572872 | tf_op jit(solution)/shard_map/while/body/eval_jaxpr/ppermute | solution.py:13
  645.3 28.4 %collective-permute-start.4 = (f32[1024,2,128]{2,0,1:T(8,128)S(1)}, f32[1024,2,128]{2,0,1:T(8,128)S(1)}, u32[]{:S(2)}, u32[]{:S(2)}) collective-permute-start(f32[1024,2,128]{2,0,1:T(8,128)S(1)} %get-tuple-element.866), channel_id=1, source_target_pairs={{0,1},{1,2},{2,3},{3,4},{4,5},{5,6},{6,7},{7,8},{8,9},{9,10},{10,1... | collective-permute-start | bytes 3145736 | tf_op jit(solution)/shard_map/while/body/eval_jaxpr/ppermute | solution.py:13
  662.0 11.8 %collective-permute-start.2 = (f32[2,1024]{1,0:T(2,128)S(1)}, f32[2,1024]{1,0:T(2,128)S(1)}, u32[]{:S(2)}, u32[]{:S(2)}) collective-permute-start(f32[2,1024]{1,0:T(2,128)S(1)} %copy.187), channel_id=1, source_target_pairs={{0,1},{1,2},{2,3},{3,4},{4,5},{5,6},{6,7},{7,8},{8,9},{9,10},{10,1... | collective-permute-start | bytes 24584 | tf_op jit(solution)/shard_map/while/body/eval_jaxpr/ppermute | solution.py:13
  662.1 11.8 %collective-permute-start.3 = (f32[2,1024]{1,0:T(2,128)S(1)}, f32[2,1024]{1,0:T(2,128)S(1)}, u32[]{:S(2)}, u32[]{:S(2)}) collective-permute-start(f32[2,1024]{1,0:T(2,128)S(1)} %copy.188), channel_id=1, source_target_pairs={{0,1},{1,2},{2,3},{3,4},{4,5},{5,6},{6,7},{7,8},{8,9},{9,10},{10,1... | collective-permute-start | bytes 24584 | tf_op jit(solution)/shard_map/while/body/eval_jaxpr/ppermute | solution.py:13
  676.4 12.1 %collective-permute-start = (bf16[1024,2,128]{2,0,1:T(8,128)(2,1)}, bf16[1024,2,128]{2,0,1:T(8,128)(2,1)S(1)}, u32[]{:S(2)}, u32[]{:S(2)}) collective-permute-start(bf16[1024,2,128]{2,0,1:T(8,128)(2,1)} %get-tuple-element.934), channel_id=1, source_target_pairs={{0,1},{1,2},{2,3},{3,4},{4,5},{5,6},{6,7},{7,8},{8,9},{9,10},{10,1... | collective-permute-start | bytes 1572872 | tf_op jit(solution)/shard_map/while/body/eval_jaxpr/ppermute | solution.py:13
  702.7 14.2 %collective-permute-start.4 = (f32[1024,2,128]{2,0,1:T(8,128)S(1)}, f32[1024,2,128]{2,0,1:T(8,128)S(1)}, u32[]{:S(2)}, u32[]{:S(2)}) collective-permute-start(f32[1024,2,128]{2,0,1:T(8,128)S(1)} %get-tuple-element.866), channel_id=1, source_target_pairs={{0,1},{1,2},{2,3},{3,4},{4,5},{5,6},{6,7},{7,8},{8,9},{9,10},{10,1... | collective-permute-start | bytes 3145736 | tf_op jit(solution)/shard_map/while/body/eval_jaxpr/ppermute | solution.py:13
  705.2 11.8 %collective-permute-start.2 = (f32[2,1024]{1,0:T(2,128)S(1)}, f32[2,1024]{1,0:T(2,128)S(1)}, u32[]{:S(2)}, u32[]{:S(2)}) collective-permute-start(f32[2,1024]{1,0:T(2,128)S(1)} %copy.187), channel_id=1, source_target_pairs={{0,1},{1,2},{2,3},{3,4},{4,5},{5,6},{6,7},{7,8},{8,9},{9,10},{10,1... | collective-permute-start | bytes 24584 | tf_op jit(solution)/shard_map/while/body/eval_jaxpr/ppermute | solution.py:13
  705.3 11.8 %collective-permute-start.3 = (f32[2,1024]{1,0:T(2,128)S(1)}, f32[2,1024]{1,0:T(2,128)S(1)}, u32[]{:S(2)}, u32[]{:S(2)}) collective-permute-start(f32[2,1024]{1,0:T(2,128)S(1)} %copy.188), channel_id=1, source_target_pairs={{0,1},{1,2},{2,3},{3,4},{4,5},{5,6},{6,7},{7,8},{8,9},{9,10},{10,1... | collective-permute-start | bytes 24584 | tf_op jit(solution)/shard_map/while/body/eval_jaxpr/ppermute | solution.py:13
  717.1 13.0 %collective-permute-start.1 = (bf16[1024,2,128]{2,0,1:T(8,128)(2,1)}, bf16[1024,2,128]{2,0,1:T(8,128)(2,1)}, u32[]{:S(2)}, u32[]{:S(2)}) collective-permute-start(bf16[1024,2,128]{2,0,1:T(8,128)(2,1)} %get-tuple-element.935), channel_id=1, source_target_pairs={{0,1},{1,2},{2,3},{3,4},{4,5},{5,6},{6,7},{7,8},{8,9},{9,10},{10,1... | collective-permute-start | bytes 1572872 | tf_op jit(solution)/shard_map/while/body/eval_jaxpr/ppermute | solution.py:13
  719.6 12.1 %collective-permute-start = (bf16[1024,2,128]{2,0,1:T(8,128)(2,1)}, bf16[1024,2,128]{2,0,1:T(8,128)(2,1)S(1)}, u32[]{:S(2)}, u32[]{:S(2)}) collective-permute-start(bf16[1024,2,128]{2,0,1:T(8,128)(2,1)} %get-tuple-element.934), channel_id=1, source_target_pairs={{0,1},{1,2},{2,3},{3,4},{4,5},{5,6},{6,7},{7,8},{8,9},{9,10},{10,1... | collective-permute-start | bytes 1572872 | tf_op jit(solution)/shard_map/while/body/eval_jaxpr/ppermute | solution.py:13
  746.0 11.8 %collective-permute-start.3 = (f32[2,1024]{1,0:T(2,128)S(1)}, f32[2,1024]{1,0:T(2,128)S(1)}, u32[]{:S(2)}, u32[]{:S(2)}) collective-permute-start(f32[2,1024]{1,0:T(2,128)S(1)} %copy.188), channel_id=1, source_target_pairs={{0,1},{1,2},{2,3},{3,4},{4,5},{5,6},{6,7},{7,8},{8,9},{9,10},{10,1... | collective-permute-start | bytes 24584 | tf_op jit(solution)/shard_map/while/body/eval_jaxpr/ppermute | solution.py:13
  757.9 15.1 %collective-permute-start.1 = (bf16[1024,2,128]{2,0,1:T(8,128)(2,1)}, bf16[1024,2,128]{2,0,1:T(8,128)(2,1)}, u32[]{:S(2)}, u32[]{:S(2)}) collective-permute-start(bf16[1024,2,128]{2,0,1:T(8,128)(2,1)} %get-tuple-element.935), channel_id=1, source_target_pairs={{0,1},{1,2},{2,3},{3,4},{4,5},{5,6},{6,7},{7,8},{8,9},{9,10},{10,1... | collective-permute-start | bytes 1572872 | tf_op jit(solution)/shard_map/while/body/eval_jaxpr/ppermute | solution.py:13
  760.4 13.2 %collective-permute-start = (bf16[1024,2,128]{2,0,1:T(8,128)(2,1)}, bf16[1024,2,128]{2,0,1:T(8,128)(2,1)S(1)}, u32[]{:S(2)}, u32[]{:S(2)}) collective-permute-start(bf16[1024,2,128]{2,0,1:T(8,128)(2,1)} %get-tuple-element.934), channel_id=1, source_target_pairs={{0,1},{1,2},{2,3},{3,4},{4,5},{5,6},{6,7},{7,8},{8,9},{9,10},{10,1... | collective-permute-start | bytes 1572872 | tf_op jit(solution)/shard_map/while/body/eval_jaxpr/ppermute | solution.py:13
  788.0 11.8 %collective-permute-start.3 = (f32[2,1024]{1,0:T(2,128)S(1)}, f32[2,1024]{1,0:T(2,128)S(1)}, u32[]{:S(2)}, u32[]{:S(2)}) collective-permute-start(f32[2,1024]{1,0:T(2,128)S(1)} %copy.188), channel_id=1, source_target_pairs={{0,1},{1,2},{2,3},{3,4},{4,5},{5,6},{6,7},{7,8},{8,9},{9,10},{10,1... | collective-permute-start | bytes 24584 | tf_op jit(solution)/shard_map/while/body/eval_jaxpr/ppermute | solution.py:13
  799.8 16.0 %collective-permute-start.1 = (bf16[1024,2,128]{2,0,1:T(8,128)(2,1)}, bf16[1024,2,128]{2,0,1:T(8,128)(2,1)}, u32[]{:S(2)}, u32[]{:S(2)}) collective-permute-start(bf16[1024,2,128]{2,0,1:T(8,128)(2,1)} %get-tuple-element.935), channel_id=1, source_target_pairs={{0,1},{1,2},{2,3},{3,4},{4,5},{5,6},{6,7},{7,8},{8,9},{9,10},{10,1... | collective-permute-start | bytes 1572872 | tf_op jit(solution)/shard_map/while/body/eval_jaxpr/ppermute | solution.py:13
  802.3 14.2 %collective-permute-start = (bf16[1024,2,128]{2,0,1:T(8,128)(2,1)}, bf16[1024,2,128]{2,0,1:T(8,128)(2,1)S(1)}, u32[]{:S(2)}, u32[]{:S(2)}) collective-permute-start(bf16[1024,2,128]{2,0,1:T(8,128)(2,1)} %get-tuple-element.934), channel_id=1, source_target_pairs={{0,1},{1,2},{2,3},{3,4},{4,5},{5,6},{6,7},{7,8},{8,9},{9,10},{10,1... | collective-permute-start | bytes 1572872 | tf_op jit(solution)/shard_map/while/body/eval_jaxpr/ppermute | solution.py:13
  816.5 16.3 %collective-permute-start.4 = (f32[1024,2,128]{2,0,1:T(8,128)S(1)}, f32[1024,2,128]{2,0,1:T(8,128)S(1)}, u32[]{:S(2)}, u32[]{:S(2)}) collective-permute-start(f32[1024,2,128]{2,0,1:T(8,128)S(1)} %get-tuple-element.866), channel_id=1, source_target_pairs={{0,1},{1,2},{2,3},{3,4},{4,5},{5,6},{6,7},{7,8},{8,9},{9,10},{10,1... | collective-permute-start | bytes 3145736 | tf_op jit(solution)/shard_map/while/body/eval_jaxpr/ppermute | solution.py:13
  816.7 16.1 %collective-permute-start.2 = (f32[2,1024]{1,0:T(2,128)S(1)}, f32[2,1024]{1,0:T(2,128)S(1)}, u32[]{:S(2)}, u32[]{:S(2)}) collective-permute-start(f32[2,1024]{1,0:T(2,128)S(1)} %copy.187), channel_id=1, source_target_pairs={{0,1},{1,2},{2,3},{3,4},{4,5},{5,6},{6,7},{7,8},{8,9},{9,10},{10,1... | collective-permute-start | bytes 24584 | tf_op jit(solution)/shard_map/while/body/eval_jaxpr/ppermute | solution.py:13
  816.7 16.1 %collective-permute-start.3 = (f32[2,1024]{1,0:T(2,128)S(1)}, f32[2,1024]{1,0:T(2,128)S(1)}, u32[]{:S(2)}, u32[]{:S(2)}) collective-permute-start(f32[2,1024]{1,0:T(2,128)S(1)} %copy.188), channel_id=1, source_target_pairs={{0,1},{1,2},{2,3},{3,4},{4,5},{5,6},{6,7},{7,8},{8,9},{9,10},{10,1... | collective-permute-start | bytes 24584 | tf_op jit(solution)/shard_map/while/body/eval_jaxpr/ppermute | solution.py:13
  832.9 16.0 %collective-permute-start.1 = (bf16[1024,2,128]{2,0,1:T(8,128)(2,1)}, bf16[1024,2,128]{2,0,1:T(8,128)(2,1)}, u32[]{:S(2)}, u32[]{:S(2)}) collective-permute-start(bf16[1024,2,128]{2,0,1:T(8,128)(2,1)} %get-tuple-element.935), channel_id=1, source_target_pairs={{0,1},{1,2},{2,3},{3,4},{4,5},{5,6},{6,7},{7,8},{8,9},{9,10},{10,1... | collective-permute-start | bytes 1572872 | tf_op jit(solution)/shard_map/while/body/eval_jaxpr/ppermute | solution.py:13
  833.0 16.5 %collective-permute-start = (bf16[1024,2,128]{2,0,1:T(8,128)(2,1)}, bf16[1024,2,128]{2,0,1:T(8,128)(2,1)S(1)}, u32[]{:S(2)}, u32[]{:S(2)}) collective-permute-start(bf16[1024,2,128]{2,0,1:T(8,128)(2,1)} %get-tuple-element.934), channel_id=1, source_target_pairs={{0,1},{1,2},{2,3},{3,4},{4,5},{5,6},{6,7},{7,8},{8,9},{9,10},{10,1... | collective-permute-start | bytes 1572872 | tf_op jit(solution)/shard_map/while/body/eval_jaxpr/ppermute | solution.py:13
  849.5 30.6 %collective-permute-start.4 = (f32[1024,2,128]{2,0,1:T(8,128)S(1)}, f32[1024,2,128]{2,0,1:T(8,128)S(1)}, u32[]{:S(2)}, u32[]{:S(2)}) collective-permute-start(f32[1024,2,128]{2,0,1:T(8,128)S(1)} %get-tuple-element.866), channel_id=1, source_target_pairs={{0,1},{1,2},{2,3},{3,4},{4,5},{5,6},{6,7},{7,8},{8,9},{9,10},{10,1... | collective-permute-start | bytes 3145736 | tf_op jit(solution)/shard_map/while/body/eval_jaxpr/ppermute | solution.py:13
  861.7 18.5 %collective-permute-start.2 = (f32[2,1024]{1,0:T(2,128)S(1)}, f32[2,1024]{1,0:T(2,128)S(1)}, u32[]{:S(2)}, u32[]{:S(2)}) collective-permute-start(f32[2,1024]{1,0:T(2,128)S(1)} %copy.187), channel_id=1, source_target_pairs={{0,1},{1,2},{2,3},{3,4},{4,5},{5,6},{6,7},{7,8},{8,9},{9,10},{10,1... | collective-permute-start | bytes 24584 | tf_op jit(solution)/shard_map/while/body/eval_jaxpr/ppermute | solution.py:13
  861.8 18.4 %collective-permute-start.3 = (f32[2,1024]{1,0:T(2,128)S(1)}, f32[2,1024]{1,0:T(2,128)S(1)}, u32[]{:S(2)}, u32[]{:S(2)}) collective-permute-start(f32[2,1024]{1,0:T(2,128)S(1)} %copy.188), channel_id=1, source_target_pairs={{0,1},{1,2},{2,3},{3,4},{4,5},{5,6},{6,7},{7,8},{8,9},{9,10},{10,1... | collective-permute-start | bytes 24584 | tf_op jit(solution)/shard_map/while/body/eval_jaxpr/ppermute | solution.py:13
  (47 other events, 514.1 us)
Sparse Core Ops, SparseCore 0:
  27.9 68.8 all-gather.1
where the time goes:
time: 910 us; the launch traced here: 893 us
  waiting for transfers between devices  262 us (29%)
  starting transfers between devices  215 us (24%)
  local copies, waits for them, and re-layouts  132 us (15%)
  matrix products  122 us (13%)
  loops' own time  92.5 us (10%)
  other arithmetic  37.4 us (4%)
  blocking collectives  18.1 us (2%)
  between operations  14.4 us (2%)
    ppermute x77, waiting for transfers between devices, passed_along(): return lax.ppermute(value, axis, pairs)  231 us
    ppermute x77, starting transfers between devices, passed_along(): return lax.ppermute(value, axis, pairs)  200 us
    another operation x1, loops' own time, local(): lax.scan(one_frame, (start_peak, start_total), (stacked, jnp.arange(count...  60.4 us
    while x45, local copies, waits for them, and re-layouts  41.5 us
    dot_general x7, matrix products, pair_grads(): jnp.einsum('hqk,qhd->khd', probs.astype(jnp.bfloat16), grad_blk, preferre...  34.9 us
    another operation x1, loops' own time, local(): final = lax.fori_loop(1, frames, cycle_turn, start)  31 us
    dot_general x7, matrix products, pair_grads(): jnp.einsum('qhd,khd->hqk', grad_blk, value_blk, preferred_element_type=jn...  30.7 us
    dot_general x7, matrix products, one_update(): jnp.einsum('qhd,khd->hqk', query3, block, preferred_element_type=jnp.floa...  21 us
  transfers between devices with their start and end apart: 82, of which 55 were waited for; matrix products, arithmetic and copies ran while one was open for 22% of the time, Pallas kernels for 0%

commit v1 on v0

v1 whole, which is shorter than its diff:
```python
import functools
import math

import jax
import jax.numpy as jnp
from jax import lax
from jax.experimental import pallas as pl
from jax.experimental.pallas import tpu as pltpu
from jax.sharding import PartitionSpec as P

HEADS = 16
HEAD_DIM = 128
SCALE = HEAD_DIM ** (-0.5)
SCALE2 = SCALE * math.log2(math.e)
NBLK = 8
BLK = 128
RING = 4
GROUP = 8
SLOTS = 48
FAR = 1e30
MESH = pl.DeviceIdType.MESH
ANY = pl.BlockSpec(memory_space=pl.ANY)
SMEM = pl.BlockSpec(memory_space=pltpu.SMEM)
VMEM = pl.BlockSpec(memory_space=pltpu.VMEM)
NT = (((1,), (1,)), ((), ()))
TN = (((0,), (0,)), ((), ()))


def place():
    head = lax.axis_index("head")
    frame = lax.axis_index("frame")
    half = frame // GROUP
    member = frame % GROUP
    return head, half, member


def gather_kernel(*refs):
    count = 5
    srcs = refs[:count]
    bufs = refs[count : 2 * count]
    send1, recv1, send2, recv2 = refs[2 * count :]
    head, half, member = place()
    plane = head * 2 + half
    ring, core = member // 2, member % 2
    up = ((ring + 1) % RING) * 2 + core
    down = ((ring + RING - 1) % RING) * 2 + core
    far = ((ring + 2) % RING) * 2 + core
    twin = ring * 2 + 1 - core

    def plane_peer(step):
        other = (plane + step) % HEADS
        return other, {"head": other // 2, "frame": (other % 2) * GROUP + member}

    def group_peer(slot):
        return {"head": head, "frame": half * GROUP + slot}

    barrier = pltpu.get_barrier_semaphore()
    for step in range(1, HEADS):
        pl.semaphore_signal(barrier, inc=1, device_id=plane_peer(step)[1], device_id_type=MESH)
    for slot in (up, down, twin):
        pl.semaphore_signal(barrier, inc=1, device_id=group_peer(slot), device_id_type=MESH)
    pl.semaphore_wait(barrier, HEADS - 1 + 3)

    def column(a, other):
        if a == count - 1:
            return srcs[a].at[other]
        return srcs[a].at[:, pl.ds(pl.multiple_of(other * HEAD_DIM, HEAD_DIM), HEAD_DIM)]

    for a in range(count):
        for step in range(1, HEADS):
            other, device = plane_peer(step)
            pltpu.make_async_remote_copy(
                src_ref=column(a, other),
                dst_ref=bufs[a].at[half, member, head],
                send_sem=send1.at[a],
                recv_sem=recv1.at[a],
                device_id=device,
                device_id_type=MESH,
            ).start()
        pltpu.make_async_copy(column(a, plane), bufs[a].at[half, member, head], recv1.at[a]).start()

    pending = []

    def push(a, number, part, slot, arrive):
        copy = pltpu.make_async_remote_copy(
            src_ref=part,
            dst_ref=part,
            send_sem=send2.at[a, number],
            recv_sem=recv2.at[a, arrive],
            device_id=group_peer(slot),
            device_id_type=MESH,
        )
        copy.start()
        pending.append(copy)

    def arrived(a, number, part):
        pltpu.make_async_copy(part, part, recv2.at[a, number]).wait()

    for a in range(count):
        own = bufs[a].at[:, member]
        pltpu.make_async_copy(own, own, recv1.at[a]).wait()
        push(a, 0, own, up, 0)
        push(a, 1, own, down, 1)
        push(a, 2, own, twin, 4)
    for a in range(count):
        part = bufs[a].at[:, down]
        arrived(a, 0, part)
        push(a, 3, bufs[a].at[0, down], up, 2)
        push(a, 4, part, twin, 5)
        part = bufs[a].at[:, up]
        arrived(a, 1, part)
        push(a, 5, bufs[a].at[1, up], down, 3)
        push(a, 6, part, twin, 6)
    for a in range(count):
        part = bufs[a].at[0, far]
        arrived(a, 2, part)
        push(a, 7, part, twin, 7)
        part = bufs[a].at[1, far]
        arrived(a, 3, part)
        push(a, 8, part, twin, 8)
    twin_up = ((ring + 1) % RING) * 2 + 1 - core
    twin_down = ((ring + RING - 1) % RING) * 2 + 1 - core
    twin_far = ((ring + 2) % RING) * 2 + 1 - core
    for a in range(count):
        arrived(a, 4, bufs[a].at[:, twin])
        arrived(a, 5, bufs[a].at[:, twin_down])
        arrived(a, 6, bufs[a].at[:, twin_up])
        arrived(a, 7, bufs[a].at[0, twin_far])
        arrived(a, 8, bufs[a].at[1, twin_far])
    for copy in pending:
        copy.wait_send()
    for a in range(count):
        if a == count - 1:
            sent = srcs[a].at[pl.ds(0, HEADS - 1)]
        else:
            sent = srcs[a].at[:, pl.ds(0, (HEADS - 1) * HEAD_DIM)]
        pltpu.make_async_copy(sent, sent, send1.at[a]).wait()


def gather_all(key, value, query, grad, delta):
    whole = jax.ShapeDtypeStruct((2, GROUP, NBLK, BLK, HEAD_DIM), jnp.bfloat16)
    small = jax.ShapeDtypeStruct((2, GROUP, NBLK, 1, BLK), jnp.float32)
    return pl.pallas_call(
        gather_kernel,
        out_shape=(whole, whole, whole, whole, small),
        in_specs=[ANY] * 5,
        out_specs=(ANY,) * 5,
        scratch_shapes=[
            pltpu.SemaphoreType.DMA((5,)),
            pltpu.SemaphoreType.DMA((5,)),
            pltpu.SemaphoreType.DMA((5, 9)),
            pltpu.SemaphoreType.DMA((5, 9)),
        ],
        compiler_params=pltpu.CompilerParams(collective_id=0, has_side_effects=True),
        name="gather_all",
    )(key, value, query, grad, delta)


def share_kernel(own_ref, all_ref, send, recv, local):
    head, half, member = place()

    def peer(step):
        return {"head": head, "frame": half * GROUP + (member + step) % GROUP}

    barrier = pltpu.get_barrier_semaphore()
    for step in range(1, GROUP):
        pl.semaphore_signal(barrier, inc=1, device_id=peer(step), device_id_type=MESH)
    pl.semaphore_wait(barrier, GROUP - 1)
    copies = []
    for step in range(1, GROUP):
        copy = pltpu.make_async_remote_copy(
            src_ref=own_ref,
            dst_ref=all_ref.at[:, member],
            send_sem=send.at[step],
            recv_sem=recv.at[step],
            device_id=peer(step),
            device_id_type=MESH,
        )
        copy.start()
        copies.append(copy)
    mine = pltpu.make_async_copy(own_ref, all_ref.at[:, member], local)
    mine.start()
    mine.wait()
    for copy in copies:
        copy.wait()


def share_totals(own):
    return pl.pallas_call(
        share_kernel,
        out_shape=jax.ShapeDtypeStruct((2, GROUP, NBLK, 1, BLK), jnp.float32),
        in_specs=[VMEM],
        out_specs=VMEM,
        scratch_shapes=[
            pltpu.SemaphoreType.DMA((GROUP,)),
            pltpu.SemaphoreType.DMA((GROUP,)),
            pltpu.SemaphoreType.DMA,
        ],
        compiler_params=pltpu.CompilerParams(collective_id=1, has_side_effects=True),
        name="share_totals",
    )(own)


def dot(a, b, dims=(((1,), (0,)), ((), ()))):
    return lax.dot_general(a, b, dims, preferred_element_type=jnp.float32)


def query_kernel(member_ref, trips_ref, count_ref, list_ref, q_ref, g_ref, d_ref, k_ref, v_ref, dq_ref, lse_ref,
                 peak, total, acc):
    wide = 256
    member = member_ref[0]
    for unit in range(2):
        first = (unit * GROUP + member) * NBLK
        key = k_ref[pl.ds(first, NBLK)].reshape(NBLK * BLK, HEAD_DIM)
        value = v_ref[pl.ds(first, NBLK)].reshape(NBLK * BLK, HEAD_DIM)
        for part in range(NBLK * BLK // wide):
            i = part * 2
            query = q_ref[unit, 0, i : i + 2].reshape(wide, HEAD_DIM)
            grad = g_ref[unit, 0, i : i + 2].reshape(wide, HEAD_DIM)
            delta = jnp.concatenate([d_ref[unit, 0, i], d_ref[unit, 0, i + 1]], axis=1)
            scores = dot(key, query, NT) * SCALE2
            top = jnp.max(scores, axis=0, keepdims=True)
            probs = jnp.exp2(scores - top)
            summed = jnp.sum(probs, axis=0, keepdims=True)
            terms = (probs * (dot(value, grad, NT) - delta)).astype(jnp.bfloat16)
            partial = dot(key, terms, TN)
            for s in range(2):
                lanes = slice(s * BLK, (s + 1) * BLK)
                peak[unit * NBLK + i + s] = top[:, lanes]
                total[unit * NBLK + i + s] = summed[:, lanes]
                acc[unit * NBLK + i + s] = partial[:, lanes]

    def step(turn, carry):
        for unit in range(2):
            for i in range(NBLK):
                row = unit * NBLK + i
                entry = list_ref[row, turn]
                bias = jnp.where(turn < count_ref[row], 0.0, -FAR)
                key = k_ref[entry]
                value = v_ref[entry]
                scores = dot(key, q_ref[unit, 0, i], NT) * SCALE2 + bias
                before = peak[row]
                top = jnp.maximum(before, jnp.max(scores, axis=0, keepdims=True))
                shrink = jnp.exp2(before - top)
                probs = jnp.exp2(scores - top)
                terms = (probs * (dot(value, g_ref[unit, 0, i], NT) - d_ref[unit, 0, i])).astype(jnp.bfloat16)
                peak[row] = top
                total[row] = total[row] * shrink + jnp.sum(probs, axis=0, keepdims=True)
                acc[row] = acc[row] * shrink + dot(key, terms, TN)
        return carry

    lax.fori_loop(0, trips_ref[0], step, 0)
    for unit in range(2):
        for i in range(NBLK):
            row = unit * NBLK + i
            lse_ref[unit, i] = peak[row] + jnp.log2(total[row])
            done = acc[row] * (SCALE / total[row])
            dq_ref[unit, i] = done.T.astype(jnp.bfloat16)


def key_kernel(member_ref, trips_ref, count_ref, list_ref, k_ref, v_ref, d_ref, lse_ref, q_ref, g_ref, dk_ref, dv_ref,
               key_acc, value_acc):
    wide = 256
    member = member_ref[0]
    for unit in range(2):
        first = (unit * GROUP + member) * NBLK
        query = q_ref[pl.ds(first, NBLK)].reshape(NBLK * BLK, HEAD_DIM)
        grad = g_ref[pl.ds(first, NBLK)].reshape(NBLK * BLK, HEAD_DIM)
        delta = jnp.concatenate([d_ref[first + i] for i in range(NBLK)], axis=1)
        lse = jnp.concatenate([lse_ref[first + i] for i in range(NBLK)], axis=1)
        for part in range(NBLK * BLK // wide):
            u = part * 2
            key = k_ref[unit, 0, u : u + 2].reshape(wide, HEAD_DIM)
            value = v_ref[unit, 0, u : u + 2].reshape(wide, HEAD_DIM)
            probs = jnp.exp2(dot(key, query, NT) * SCALE2 - lse)
            terms = (probs * (dot(value, grad, NT) - delta)).astype(jnp.bfloat16)
            value_part = dot(probs.astype(jnp.bfloat16), grad)
            key_part = dot(terms, query)
            for s in range(2):
                rows = slice(s * BLK, (s + 1) * BLK)
                value_acc[unit * NBLK + u + s] = value_part[rows]
                key_acc[unit * NBLK + u + s] = key_part[rows]

    def step(turn, carry):
        for unit in range(2):
            for u in range(NBLK):
                row = unit * NBLK + u
                entry = list_ref[row, turn]
                bias = jnp.where(turn < count_ref[row], 0.0, FAR)
                query = q_ref[entry]
                grad = g_ref[entry]
                probs = jnp.exp2(dot(k_ref[unit, 0, u], query, NT) * SCALE2 - (lse_ref[entry] + bias))
                terms = (probs * (dot(v_ref[unit, 0, u], grad, NT) - d_ref[entry])).astype(jnp.bfloat16)
                value_acc[row] += dot(probs.astype(jnp.bfloat16), grad)
                key_acc[row] += dot(terms, query)
        return carry

    lax.fori_loop(0, trips_ref[0], step, 0)
    for unit in range(2):
        for u in range(NBLK):
            row = unit * NBLK + u
            dk_ref[unit, u] = (key_acc[row] * SCALE).astype(jnp.bfloat16)
            dv_ref[unit, u] = value_acc[row].astype(jnp.bfloat16)


def own_spec(rows, columns):
    return pl.BlockSpec((2, 1, NBLK, rows, columns), lambda g, member, *_: (0, member[0], 0, 0, 0))


def whole_spec(rows, columns):
    return pl.BlockSpec((2 * GROUP * NBLK, rows, columns), lambda *_: (0, 0, 0))


RESULT = pl.BlockSpec((2, NBLK, BLK, HEAD_DIM), lambda *_: (0, 0, 0, 0))
TOTALS = pl.BlockSpec((2, NBLK, 1, BLK), lambda *_: (0, 0, 0, 0))
PARAMS = pltpu.CompilerParams(vmem_limit_bytes=48 << 20)
LOW = jax.ShapeDtypeStruct((2, NBLK, BLK, HEAD_DIM), jnp.bfloat16)


def flat(array):
    return array.reshape((2 * GROUP * NBLK,) + array.shape[3:])


def query_pass(tables, query, grad, delta, key, value):
    return pl.pallas_call(
        query_kernel,
        out_shape=(LOW, jax.ShapeDtypeStruct((2, NBLK, 1, BLK), jnp.float32)),
        grid_spec=pltpu.PrefetchScalarGridSpec(
            num_scalar_prefetch=4,
            grid=(1,),
            in_specs=[
                own_spec(BLK, HEAD_DIM),
                own_spec(BLK, HEAD_DIM),
                own_spec(1, BLK),
                whole_spec(BLK, HEAD_DIM),
                whole_spec(BLK, HEAD_DIM),
            ],
            out_specs=(RESULT, TOTALS),
            scratch_shapes=[
                pltpu.VMEM((2 * NBLK, 1, BLK), jnp.float32),
                pltpu.VMEM((2 * NBLK, 1, BLK), jnp.float32),
                pltpu.VMEM((2 * NBLK, HEAD_DIM, BLK), jnp.float32),
            ],
        ),
        compiler_params=PARAMS,
        name="query_pass",
    )(*tables, query, grad, delta, flat(key), flat(value))


def key_pass(tables, key, value, delta, lse, query, grad):
    return pl.pallas_call(
        key_kernel,
        out_shape=(LOW, LOW),
        grid_spec=pltpu.PrefetchScalarGridSpec(
            num_scalar_prefetch=4,
            grid=(1,),
            in_specs=[
                own_spec(BLK, HEAD_DIM),
                own_spec(BLK, HEAD_DIM),
                whole_spec(1, BLK),
                whole_spec(1, BLK),
                whole_spec(BLK, HEAD_DIM),
                whole_spec(BLK, HEAD_DIM),
            ],
            out_specs=(RESULT, RESULT),
            scratch_shapes=[
                pltpu.VMEM((2 * NBLK, BLK, HEAD_DIM), jnp.float32),
                pltpu.VMEM((2 * NBLK, BLK, HEAD_DIM), jnp.float32),
            ],
        ),
        compiler_params=PARAMS,
        name="key_pass",
    )(*tables, key, value, flat(delta), flat(lse), flat(query), flat(grad))


def compact(live):
    rows = live.reshape(2 * NBLK, 2 * GROUP * NBLK)
    counts = jnp.sum(rows, axis=1)
    spot = jnp.arange(rows.shape[1], dtype=jnp.int32)
    ahead = jnp.sum(jnp.where(spot[None, :, None] > spot[None, None, :], rows[:, None, :], 0), axis=2)
    slot = jnp.arange(SLOTS, dtype=jnp.int32)
    match = (ahead[:, None, :] == slot[None, :, None]) & (rows[:, None, :] > 0)
    entries = jnp.sum(jnp.where(match, spot[None, None, :], 0), axis=2)
    return jnp.max(counts).reshape(1), counts, entries


def live_tables(frame_order, block_live, member):
    mine = jnp.stack([lax.dynamic_index_in_dim(frame_order, member, 0, False),
                      lax.dynamic_index_in_dim(frame_order, member + GROUP, 0, False)])
    distance = jnp.abs(mine[:, None] - frame_order[None, :])
    blocks = jnp.zeros((2, 2 * GROUP, NBLK, NBLK), jnp.int32)
    for d in range(1, 4):
        blocks = blocks + jnp.where((distance == d)[:, :, None, None], block_live[d][None, None], 0)
    return compact(blocks.transpose(0, 2, 1, 3)), compact(blocks.transpose(0, 3, 1, 2))


def local(queries, key_states, value_states, attn_out, grad_out, frame_order, block_live):
    _, half, member = place()
    products = grad_out.astype(jnp.float32) * attn_out.astype(jnp.float32)
    delta_local = jnp.sum(products.reshape(BLK, HEADS, HEAD_DIM), axis=2).T.reshape(HEADS, 1, BLK)
    where = member.astype(jnp.int32).reshape(1)
    by_query, by_key = live_tables(frame_order, block_live, member)
    key, value, query, grad, delta = gather_all(key_states, value_states, queries, grad_out, delta_local)
    dq, lse_own = query_pass((where, *by_query), query, grad, delta, key, value)
    lse = share_totals(lse_own)
    dk, dv = key_pass((where, *by_key), key, value, delta, lse, query, grad)
    swap = [(source, (source + GROUP) % (2 * GROUP)) for source in range(2 * GROUP)]

    def finish(result):
        result = result.reshape(2, NBLK * BLK, HEAD_DIM)
        kept = jnp.where(half == 0, result[0], result[1])
        sent = jnp.where(half == 0, result[1], result[0])
        came = lax.ppermute(sent, "frame", swap)
        return jnp.concatenate(
            [jnp.where(half == 0, kept, came), jnp.where(half == 0, came, kept)], axis=1
        )

    return finish(dq), finish(dk), finish(dv)


def solution(mesh):
    rows = P(("frame", "head"), None)
    out = P("frame", "head")
    return jax.shard_map(
        local,
        mesh=mesh,
        in_specs=(rows, rows, rows, rows, rows, P(), P()),
        out_specs=(out, out, out),
        check_vma=False,
    )
```

time: 910 us -> 211 us (0.23); the launches traced: 893 us -> 211 us
  waiting for transfers between devices: 262 us -> 10.6 us
  starting transfers between devices: 215 us -> 2.56 us
  Pallas kernels: 0 us -> 176 us
  matrix products: 122 us -> 0 us
  local copies, waits for them, and re-layouts: 132 us -> 10.8 us
  loops' own time: 92.5 us -> 0 us
  other arithmetic: 37.4 us -> 9.99 us
  blocking collectives: 18.1 us -> 0 us
  between operations: 14.4 us -> 0.81 us
    ppermute x77 -> x3, waiting for transfers between devices: 231 us -> 10.6 us  [finish(): came = lax.ppermute(sent, 'frame', swap)]
    ppermute x77 -> x3, starting transfers between devices: 200 us -> 2.56 us  [finish(): came = lax.ppermute(sent, 'frame', swap)]
    pallas_call x0 -> x4, Pallas kernels: none -> 176 us  [the longest x1 89.1 us: gather_all(): pl.pallas_call(gather_kernel, out_shape=(whole, whole, whole, whole, smal...]
    dot_general x42 -> x0, matrix products: 122 us -> none  [the longest x7 34.9 us: pair_grads(): jnp.einsum('hqk,qhd->khd', probs.astype(jnp.bfloat16), grad_blk, preferre...]
    another operation x33 -> x0, loops' own time: 92.5 us -> none  [the longest x1 60.4 us: local(): lax.scan(one_frame, (start_peak, start_total), (stacked, jnp.arange(count...]
    while x52 -> x0, local copies, waits for them, and re-layouts: 54.1 us -> none
    all_to_all x4 -> x0, waiting for transfers between devices: 30.2 us -> none  [the longest x1 11.5 us: local(): lax.all_to_all(attn_out, 'head', split_axis=1, concat_axis=0, tiled=True)]
    dynamic_slice x48 -> x1, local copies, waits for them, and re-layouts: 29.2 us -> 1.32 us  [live_tables(): lax.dynamic_index_in_dim(frame_order, member, 0, False)]
  transfers between devices with their start and end apart: 82 -> 3, of which waited for: 55 -> 2; matrix products, arithmetic and copies ran while one was open for 22% -> 1% of each run, Pallas kernels for 0% -> 22%
where the time goes in v1:
time: 211 us
  Pallas kernels  176 us (83%)
  local copies, waits for them, and re-layouts  10.8 us (5%)
  waiting for transfers between devices  10.6 us (5%)
  other arithmetic  9.99 us (5%)
  starting transfers between devices  2.56 us (1%)
    pallas_call x1, Pallas kernels, gather_all(): pl.pallas_call(gather_kernel, out_shape=(whole, whole, whole, whole, smal...  89.1 us
    pallas_call x1, Pallas kernels, query_pass(): pl.pallas_call(query_kernel, out_shape=(LOW, jax.ShapeDtypeStruct((2, NBL...  40.1 us
    pallas_call x1, Pallas kernels, key_pass(): pl.pallas_call(key_kernel, out_shape=(LOW, LOW), grid_spec=pltpu.Prefetch...  39.8 us
    ppermute x3, waiting for transfers between devices, finish(): came = lax.ppermute(sent, 'frame', swap)  10.6 us
    unnamed x16, local copies, waits for them, and re-layouts  7.13 us
    pallas_call x1, Pallas kernels, share_totals(): pl.pallas_call(share_kernel, out_shape=jax.ShapeDtypeStruct((2, GROUP, NB...  6.75 us
  transfers between devices with their start and end apart: 3, of which 2 were waited for; matrix products, arithmetic and copies ran while one was open for 1% of the time, Pallas kernels for 22%

profile of v1, /device:TPU:1, one launch (start us, length us, event | category | flops | bytes accessed | tf_op | source)
XLA Modules:
  0.0 210.6 jit_solution(530940944771059324)
XLA Ops:
  0.7 1.0 fusion.7
  1.6 0.1 copy.39
  1.8 0.1 copy.36
  1.9 0.1 copy.40
  2.0 0.1 copy.37
  2.1 0.1 copy.41
  2.3 0.1 copy.38
  2.4 1.3 fusion.8
  3.7 1.4 pad_add_fusion
  5.1 0.7 fusion.6
  5.8 0.8 fusion.3
  6.6 0.1 reduce_sum.68.count_ref
  6.7 0.6 reduce_max.18
  7.3 0.1 add.85
  7.4 0.1 add.88
  7.5 1.3 multiply_bitcast_fusion
  8.9 0.2 copy.42
  9.1 0.3 reduce_sum.71
  9.4 0.7 copy.32
  10.1 0.6 select_reduce_fusion
  10.7 0.4 select_reduce_fusion.3.list_ref
  11.1 89.1 %gather_all.1 = (bf16[2,8,8,128,128]{4,3,2,1,0:T(8,128)(2,1)}, bf16[2,8,8,128,128]{4,3,2,1,0:T(8,128)(2,1)}, bf16[2,8,8,128,128]{4,3,2,1,0:T(8,128)(2,1)}, bf16[...) custom-call(bf16[128,2048]{1,0:T(8,128)(2,1)} %refs_0_.1, bf16[128,2048]{1,0:T(8,128)(2,1)} %refs_1_.1, ...), custom_call_target="tpu_custom_call" | custom-call | tf_op jit(solution)/shard_map/gather_all/pallas_call | solution.py:143
  100.2 0.0 copy-start.1
  100.2 2.2 %copy-done.1 = bf16[2,8,8,128,128]{4,3,2,1,0:T(8,128)(2,1)S(1)} copy-done((bf16[2,8,8,128,128]{4,3,2,1,0:T(8,128)(2,1)S(1)}, bf16[2,8,8,128,128]{4,3,2,1,0:T(8,128)(2,1)}, u32[]{:S(2)}) %copy-start.1) | copy-done | bytes 4194328
  102.4 0.0 copy-start.2
  102.4 0.8 copy-done.2
  103.2 0.0 copy-start.3
  103.2 40.1 %query_pass.1 = (bf16[2,8,128,128]{3,2,1,0:T(8,128)(2,1)S(1)}, f32[2,8,1,128]{3,2,1,0:T(1,128)S(1)}) custom-call(s32[1]{0:T(128)} %bitcast.member_ref, s32[1]{0:T(128)} %bitcast.4.trips_ref, s32[16]{0:T(128)S(1)} %reduce_sum.68.count_ref, s32[16,48]{1,0:T(8,128)S(1)} %select_reduce_fusion.3.list_ref, bf16[2,8,8,128,128]{4,3,2,1,0:T(8,128)(2,1)S(1)} %copy-done.1, ...), custom_call_target="tpu_custom_call" | custom-call | tf_op jit(solution)/shard_map/query_pass/pallas_call | solution.py:325
  143.3 0.0 copy-start.5
  143.4 0.5 copy-done.5
  143.9 0.9 collective-permute-start
  144.9 0.6 reduce_max.19
  145.5 0.1 reduce_sum.73.count_ref
  145.6 6.8 %share_totals.1 = f32[2,8,8,1,128]{4,3,2,1,0:T(1,128)} custom-call(f32[2,8,1,128]{3,2,1,0:T(1,128)} %copy-done.5), custom_call_target="tpu_custom_call" | custom-call | tf_op jit(solution)/shard_map/share_totals/pallas_call | solution.py:189
  152.4 0.3 select_reduce_fusion.2.list_ref
  152.7 0.0 copy-done.3
  152.7 0.0 copy-start
  152.7 2.2 %copy-done = bf16[2,8,8,128,128]{4,3,2,1,0:T(8,128)(2,1)S(1)} copy-done((bf16[2,8,8,128,128]{4,3,2,1,0:T(8,128)(2,1)S(1)}, bf16[2,8,8,128,128]{4,3,2,1,0:T(8,128)(2,1)}, u32[]{:S(2)}) %copy-start) | copy-done | bytes 4194328
  154.9 0.0 copy-start.4
  154.9 0.8 copy-done.4
  155.7 39.8 %key_pass.1 = (bf16[2,8,128,128]{3,2,1,0:T(8,128)(2,1)S(1)}, bf16[2,8,128,128]{3,2,1,0:T(8,128)(2,1)S(1)}) custom-call(s32[1]{0:T(128)} %bitcast.member_ref, s32[1]{0:T(128)} %bitcast.14.trips_ref, s32[16]{0:T(128)S(1)} %reduce_sum.73.count_ref, s32[16,48]{1,0:T(8,128)S(1)} %select_reduce_fusion.2.list_ref, bf16[2,8,8,128,128]{4,3,2,1,0:T(8,128)(2,1)S(1)} %copy-done, ...), custom_call_target="tpu_custom_call" | custom-call | tf_op jit(solution)/shard_map/key_pass/pallas_call | solution.py:351
  195.5 0.6 collective-permute-start.1
  196.2 1.0 collective-permute-start.2
  197.2 0.0 collective-permute-done
  197.2 0.1 bitcast_select_fusion.5
  197.3 0.9 pad_maximum_fusion
  198.1 5.0 %collective-permute-done.1 = bf16[1024,128]{1,0:T(8,128)(2,1)S(1)} collective-permute-done((bf16[1024,128]{1,0:T(8,128)(2,1)S(1)}, bf16[1024,128]{1,0:T(8,128)(2,1)S(1)}, u32[]{:S(2)}, u32[]{:S(2)}) %collective-permute-start.1) | collective-permute-done | bytes 262176 | tf_op jit(solution)/shard_map/ppermute | solution.py:413
  203.2 5.6 %collective-permute-done.2 = bf16[1024,128]{1,0:T(8,128)(2,1)S(1)} collective-permute-done((bf16[1024,128]{1,0:T(8,128)(2,1)S(1)}, bf16[1024,128]{1,0:T(8,128)(2,1)S(1)}, u32[]{:S(2)}, u32[]{:S(2)}) %collective-permute-start.2) | collective-permute-done | bytes 262176 | tf_op jit(solution)/shard_map/ppermute | solution.py:413
  208.8 0.1 bitcast_select_fusion.1
  208.9 0.9 pad_maximum_fusion.2
  209.7 0.8 pad_maximum_fusion.1
  (6 shorter events, 0.1 us)
Async XLA Ops:
  100.2 2.2 %copy-start.1 = (bf16[2,8,8,128,128]{4,3,2,1,0:T(8,128)(2,1)S(1)}, bf16[2,8,8,128,128]{4,3,2,1,0:T(8,128)(2,1)}, u32[]{:S(2)}) copy-start(bf16[2,8,8,128,128]{4,3,2,1,0:T(8,128)(2,1)} %get-tuple-element.12.q_ref) | copy-start | bytes 12582916
  102.4 0.8 copy-start.2
  103.2 49.5 %copy-start.3 = (f32[2,8,8,1,128]{4,3,2,1,0:T(1,128)S(1)}, f32[2,8,8,1,128]{4,3,2,1,0:T(1,128)}, u32[]{:S(2)}) copy-start(f32[2,8,8,1,128]{4,3,2,1,0:T(1,128)} %get-tuple-element.14.d_ref) | copy-start | bytes 196612
  143.3 0.6 copy-start.5
  143.9 53.3 %collective-permute-start = (bf16[1024,128]{1,0:T(8,128)(2,1)S(1)}, bf16[1024,128]{1,0:T(8,128)(2,1)S(1)}, u32[]{:S(2)}, u32[]{:S(2)}) collective-permute-start(bf16[1024,128]{1,0:T(8,128)(2,1)S(1)} %bitcast.50), channel_id=1, source_target_pairs={{0,8},{1,9},{2,10},{3,11},{4,12},{5,13},{6,14},{7,15},{8,0},{9,1},... | collective-permute-start | bytes 786440 | tf_op jit(solution)/shard_map/ppermute | solution.py:413
  152.7 2.2 %copy-start = (bf16[2,8,8,128,128]{4,3,2,1,0:T(8,128)(2,1)S(1)}, bf16[2,8,8,128,128]{4,3,2,1,0:T(8,128)(2,1)}, u32[]{:S(2)}) copy-start(bf16[2,8,8,128,128]{4,3,2,1,0:T(8,128)(2,1)} %get-tuple-element.15.k_ref) | copy-start | bytes 12582916
  154.9 0.8 copy-start.4
  195.5 7.6 %collective-permute-start.1 = (bf16[1024,128]{1,0:T(8,128)(2,1)S(1)}, bf16[1024,128]{1,0:T(8,128)(2,1)S(1)}, u32[]{:S(2)}, u32[]{:S(2)}) collective-permute-start(bf16[1024,128]{1,0:T(8,128)(2,1)S(1)} %bitcast.51), channel_id=1, source_target_pairs={{0,8},{1,9},{2,10},{3,11},{4,12},{5,13},{6,14},{7,15},{8,0},{9,1},... | collective-permute-start | bytes 786440 | tf_op jit(solution)/shard_map/ppermute | solution.py:413
  196.2 12.6 %collective-permute-start.2 = (bf16[1024,128]{1,0:T(8,128)(2,1)S(1)}, bf16[1024,128]{1,0:T(8,128)(2,1)S(1)}, u32[]{:S(2)}, u32[]{:S(2)}) collective-permute-start(bf16[1024,128]{1,0:T(8,128)(2,1)S(1)} %bitcast.52), channel_id=1, source_target_pairs={{0,8},{1,9},{2,10},{3,11},{4,12},{5,13},{6,14},{7,15},{8,0},{9,1},... | collective-permute-start | bytes 786440 | tf_op jit(solution)/shard_map/ppermute | solution.py:413

commit v2 on v0

v2 whole, which is shorter than its diff:
```python
import math

import jax
import jax.numpy as jnp
from jax import lax
from jax.experimental import pallas as pl
from jax.experimental.pallas import tpu as pltpu
from jax.sharding import PartitionSpec as P

HEADS = 16
HEAD_DIM = 128
SCALE = HEAD_DIM ** (-0.5)
SCALE2 = SCALE * math.log2(math.e)
REACH = 4
NBLK = 8
BLK = 128
RING = 4
GROUP = 8
ROWS = 2 * NBLK
ENTRIES = 2 * GROUP * NBLK
SLOTS = 2 * (REACH - 1) * NBLK
COUNT_AT = BLK - 1
CHUNK = 5
PAIR = 2
WIDE = 512
FAR = 1e30
MESH = pl.DeviceIdType.MESH
ANY = pl.BlockSpec(memory_space=pl.ANY)
SMEM = pl.BlockSpec(memory_space=pltpu.SMEM)
VMEM = pl.BlockSpec(memory_space=pltpu.VMEM)
NN = (((1,), (0,)), ((), ()))
NT = (((1,), (1,)), ((), ()))
TN = (((0,), (0,)), ((), ()))
KEY, VALUE, QUERY, GRAD, DELTA = range(5)


def dot(a, b, dims=NN):
    return lax.dot_general(a, b, dims, preferred_element_type=jnp.float32)


def place():
    frame = lax.axis_index("frame")
    return lax.axis_index("head"), frame // GROUP, frame % GROUP


class Ring:
    def __init__(self):
        self.head, self.half, self.member = place()
        ring, core = self.member // 2, self.member % 2
        up, down, far = (ring + 1) % RING, (ring + RING - 1) % RING, (ring + 2) % RING
        self.up, self.down, self.far = up * 2 + core, down * 2 + core, far * 2 + core
        self.twin = ring * 2 + 1 - core
        self.twin_up, self.twin_down, self.twin_far = up * 2 + 1 - core, down * 2 + 1 - core, far * 2 + 1 - core

    def device(self, slot):
        return {"head": self.head, "frame": self.half * GROUP + slot}


def remote(src, dst, send, recv, device):
    copy = pltpu.make_async_remote_copy(
        src_ref=src, dst_ref=dst, send_sem=send, recv_sem=recv, device_id=device, device_id_type=MESH
    )
    copy.start()
    return copy


def arrived(part, sem):
    pltpu.make_async_copy(part, part, sem).wait()


def live_list(flags):
    spot = lax.broadcasted_iota(jnp.int32, (ENTRIES, ENTRIES), 0)
    later = lax.broadcasted_iota(jnp.int32, (ENTRIES, ENTRIES), 1)
    before = jnp.where(spot < later, 1.0, 0.0).astype(jnp.bfloat16)
    ahead = dot(flags.astype(jnp.bfloat16), before)
    lane = lax.broadcasted_iota(jnp.int32, (ROWS, ENTRIES), 1)
    value = lane.astype(jnp.float32) * flags
    ahead = jnp.where(flags > 0.0, ahead, -1.0)
    table = jnp.where(lane == COUNT_AT, jnp.sum(flags, axis=1, keepdims=True), 0.0)
    for k in range(SLOTS):
        found = jnp.sum(jnp.where(ahead == float(k), value, 0.0), axis=1, keepdims=True)
        table = jnp.where(lane == k, found, table)
    return table.astype(jnp.int32)


def write_tables(member, order_ref, live_ref, by_query_ref, by_key_ref):
    lane = lax.broadcasted_iota(jnp.int32, (1, ENTRIES), 1)
    order = jnp.zeros((1, ENTRIES), jnp.int32)
    for g in range(2 * GROUP):
        order = jnp.where(lane // NBLK == g, order_ref[g], order)
    rows = lax.broadcasted_iota(jnp.int32, (NBLK, ENTRIES), 0)
    lanes = lax.broadcasted_iota(jnp.int32, (NBLK, ENTRIES), 1)
    spread = jnp.where(lanes % NBLK == rows, 1.0, 0.0).astype(jnp.bfloat16)
    query_rows, key_rows = [], []
    for unit in range(2):
        distance = jnp.abs(order - order_ref[unit * GROUP + member])
        by_query = jnp.zeros((NBLK, ENTRIES), jnp.float32)
        by_key = jnp.zeros((NBLK, ENTRIES), jnp.float32)
        for d in range(1, REACH):
            blocks = live_ref[d].astype(jnp.float32).astype(jnp.bfloat16)
            here = distance == d
            by_query = jnp.where(here, dot(blocks, spread), by_query)
            by_key = jnp.where(here, dot(blocks, spread, TN), by_key)
        query_rows.append(by_query)
        key_rows.append(by_key)
    by_query_ref[...] = live_list(jnp.concatenate(query_rows, axis=0))
    by_key_ref[...] = live_list(jnp.concatenate(key_rows, axis=0))


def gather_kernel(order_ref, live_ref, grad_ref, out_ref, key_src, value_src, query_src, grad_src, key_all, value_all,
                  query_all, grad_all, delta_all, query_own, grad_own, peak, total, acc, by_query_ref, by_key_ref,
                  delta_src, send1, recv1, send2, recv2, load):
    ring = Ring()
    head, half, member = ring.head, ring.half, ring.member
    plane = head * 2 + half
    srcs = (key_src, value_src, query_src, grad_src, delta_src)
    bufs = (key_all, value_all, query_all, grad_all, delta_all)

    def plane_peer(step):
        other = (plane + step) % HEADS
        return other, {"head": other // 2, "frame": (other % 2) * GROUP + member}

    barrier = pltpu.get_barrier_semaphore()
    for step in range(1, HEADS):
        pl.semaphore_signal(barrier, inc=1, device_id=plane_peer(step)[1], device_id_type=MESH)
    for slot in (ring.up, ring.down, ring.twin):
        pl.semaphore_signal(barrier, inc=1, device_id=ring.device(slot), device_id_type=MESH)
    pl.semaphore_wait(barrier, HEADS - 1 + 3)

    def column(a, other):
        if a == DELTA:
            return srcs[a].at[other]
        return srcs[a].at[:, pl.ds(pl.multiple_of(other * HEAD_DIM, HEAD_DIM), HEAD_DIM)]

    def scatter(a):
        target = bufs[a].at[half, member, head]
        for step in range(1, HEADS):
            other, device = plane_peer(step)
            remote(column(a, other), target, send1.at[a], recv1.at[a], device)
        pltpu.make_async_copy(column(a, plane), target, recv1.at[a]).start()

    for a in (KEY, VALUE, QUERY, GRAD):
        scatter(a)
    for n in range(HEADS):
        lanes = slice(n * HEAD_DIM, (n + 1) * HEAD_DIM)
        products = grad_ref[:, lanes].astype(jnp.float32) * out_ref[:, lanes].astype(jnp.float32)
        delta_src[n] = jnp.sum(products.T, axis=0, keepdims=True)
    scatter(DELTA)

    pending = []

    def push(a, number, part, slot, arrive):
        pending.append(remote(part, part, send2.at[a, number], recv2.at[a, arrive], ring.device(slot)))

    for a in (KEY, VALUE, QUERY, GRAD, DELTA):
        own = bufs[a].at[:, member]
        arrived(own, recv1.at[a])
        push(a, 0, own, ring.up, 0)
        push(a, 1, own, ring.down, 1)
        push(a, 2, own, ring.twin, 4)
        if a in (QUERY, GRAD):
            kept = query_own if a == QUERY else grad_own
            pltpu.make_async_copy(own, kept, load.at[a - QUERY]).start()
        if a == KEY:
            write_tables(member, order_ref, live_ref, by_query_ref, by_key_ref)
    pltpu.make_async_copy(bufs[QUERY].at[:, member], query_own, load.at[0]).wait()
    pltpu.make_async_copy(bufs[GRAD].at[:, member], grad_own, load.at[1]).wait()

    span = WIDE // BLK
    for unit in range(2):
        key = key_all[unit, member].reshape(NBLK * BLK, HEAD_DIM)
        value = value_all[unit, member].reshape(NBLK * BLK, HEAD_DIM)
        for i in range(0, NBLK, span):
            query = query_own[unit, i : i + span].reshape(WIDE, HEAD_DIM)
            grad = grad_own[unit, i : i + span].reshape(WIDE, HEAD_DIM)
            delta = jnp.concatenate([delta_all[unit, member, i + s] for s in range(span)], axis=1)
            scores = dot(key, query, NT) * SCALE2
            top = jnp.max(scores, axis=0, keepdims=True)
            probs = jnp.exp2(scores - top)
            summed = jnp.sum(probs, axis=0, keepdims=True)
            terms = (probs * (dot(value, grad, NT) - delta)).astype(jnp.bfloat16)
            partial = dot(key, terms, TN)
            for s in range(span):
                lanes = slice(s * BLK, (s + 1) * BLK)
                row = unit * NBLK + i + s
                peak[row] = top[:, lanes]
                total[row] = summed[:, lanes]
                acc[row] = partial[:, lanes]

    for a in (KEY, VALUE, QUERY, GRAD, DELTA):
        part = bufs[a].at[:, ring.down]
        arrived(part, recv2.at[a, 0])
        if a not in (QUERY, GRAD):
            push(a, 3, bufs[a].at[0, ring.down], ring.up, 2)
        push(a, 4, part, ring.twin, 5)
        part = bufs[a].at[:, ring.up]
        arrived(part, recv2.at[a, 1])
        if a not in (QUERY, GRAD):
            push(a, 5, bufs[a].at[1, ring.up], ring.down, 3)
        push(a, 6, part, ring.twin, 6)
    for a in (KEY, VALUE, DELTA):
        part = bufs[a].at[0, ring.far]
        arrived(part, recv2.at[a, 2])
        push(a, 7, part, ring.twin, 7)
        part = bufs[a].at[1, ring.far]
        arrived(part, recv2.at[a, 3])
        push(a, 8, part, ring.twin, 8)
    for a in (KEY, VALUE, QUERY, GRAD, DELTA):
        arrived(bufs[a].at[:, ring.twin], recv2.at[a, 4])
        arrived(bufs[a].at[:, ring.twin_down], recv2.at[a, 5])
        arrived(bufs[a].at[:, ring.twin_up], recv2.at[a, 6])
        if a not in (QUERY, GRAD):
            arrived(bufs[a].at[0, ring.twin_far], recv2.at[a, 7])
            arrived(bufs[a].at[1, ring.twin_far], recv2.at[a, 8])
    for copy in pending:
        copy.wait_send()
    for a in range(5):
        sent = srcs[a].at[pl.ds(0, HEADS - 1)] if a == DELTA else srcs[a].at[:, pl.ds(0, (HEADS - 1) * HEAD_DIM)]
        arrived(sent, send1.at[a])


WHOLE = (2, GROUP, NBLK, BLK, HEAD_DIM)
STATS = (2, GROUP, NBLK, 1, BLK)
OWN = (2, NBLK, BLK, HEAD_DIM)
LIMIT = 24 << 20


def gather_all(order, live, key, value, query, grad, out):
    low, full, whole = jnp.bfloat16, jnp.float32, jnp.int32
    return pl.pallas_call(
        gather_kernel,
        out_shape=(
            jax.ShapeDtypeStruct(WHOLE, low),
            jax.ShapeDtypeStruct(WHOLE, low),
            jax.ShapeDtypeStruct(WHOLE, low),
            jax.ShapeDtypeStruct(WHOLE, low),
            jax.ShapeDtypeStruct(STATS, full),
            jax.ShapeDtypeStruct(OWN, low),
            jax.ShapeDtypeStruct(OWN, low),
            jax.ShapeDtypeStruct((ROWS, 1, BLK), full),
            jax.ShapeDtypeStruct((ROWS, 1, BLK), full),
            jax.ShapeDtypeStruct((ROWS, HEAD_DIM, BLK), full),
            jax.ShapeDtypeStruct((ROWS, ENTRIES), whole),
            jax.ShapeDtypeStruct((ROWS, ENTRIES), whole),
        ),
        in_specs=[SMEM, VMEM, VMEM, VMEM, ANY, ANY, ANY, ANY],
        out_specs=(VMEM, VMEM, ANY, ANY) + (VMEM,) * 8,
        scratch_shapes=[
            pltpu.VMEM((HEADS, 1, BLK), full),
            pltpu.SemaphoreType.DMA((5,)),
            pltpu.SemaphoreType.DMA((5,)),
            pltpu.SemaphoreType.DMA((5, 9)),
            pltpu.SemaphoreType.DMA((5, 9)),
            pltpu.SemaphoreType.DMA((2,)),
        ],
        compiler_params=pltpu.CompilerParams(collective_id=0, has_side_effects=True, vmem_limit_bytes=LIMIT),
        name="gather_all",
    )(order, live, grad, out, key, value, query, grad)


def turns(table, rows):
    most = table[rows[0], COUNT_AT]
    for row in rows[1:]:
        most = jnp.maximum(most, table[row, COUNT_AT])
    return (most + CHUNK - 1) // CHUNK


def query_kernel(table, query_own, grad_own, delta_all, key_ref, value_ref, peak_in, total_in, acc_in, dq_ref, lse_ref,
                 peak, total, acc):
    member = place()[2]
    peak[...] = peak_in[...]
    total[...] = total_in[...]
    acc[...] = acc_in[...]

    def step(turn, carry):
        for first in range(0, ROWS, PAIR):
            rows = range(first, first + PAIR)
            keys, scores, grads = [], [], []
            for row in rows:
                unit, i = row // NBLK, row % NBLK
                slots = [turn * CHUNK + c for c in range(CHUNK)]
                entries = [table[row, slot] for slot in slots]
                bias = [jnp.where(slot < table[row, COUNT_AT], 0.0, -FAR) for slot in slots]
                key = jnp.concatenate([key_ref[e] for e in entries], axis=0)
                value = jnp.concatenate([value_ref[e] for e in entries], axis=0)
                s = dot(key, query_own[unit, i], NT)
                s = jnp.concatenate([s[c * BLK : (c + 1) * BLK] * SCALE2 + bias[c] for c in range(CHUNK)], axis=0)
                keys.append(key)
                scores.append(s)
                grads.append(dot(value, grad_own[unit, i], NT) - delta_all[unit, member, i])
            results = []
            for n, row in enumerate(rows):
                before = peak[row]
                top = jnp.maximum(before, jnp.max(scores[n], axis=0, keepdims=True))
                probs = jnp.exp2(scores[n] - top)
                terms = (probs * grads[n]).astype(jnp.bfloat16)
                results.append((top, jnp.exp2(before - top), jnp.sum(probs, axis=0, keepdims=True), dot(keys[n], terms, TN)))
            for n, row in enumerate(rows):
                top, shrink, summed, product = results[n]
                peak[row] = top
                total[row] = total[row] * shrink + summed
                acc[row] = acc[row] * shrink + product
        return carry

    lax.fori_loop(0, turns(table, range(ROWS)), step, 0)
    for row in range(ROWS):
        unit, i = row // NBLK, row % NBLK
        lse_ref[unit, i] = peak[row] + jnp.log2(total[row])
        dq_ref[unit, i] = (acc[row] * (SCALE / total[row])).T.astype(jnp.bfloat16)


def flat(array):
    return array.reshape((ENTRIES,) + array.shape[3:])


def query_pass(table, query_own, grad_own, delta, key, value, peak, total, acc):
    return pl.pallas_call(
        query_kernel,
        out_shape=(jax.ShapeDtypeStruct(OWN, jnp.bfloat16), jax.ShapeDtypeStruct((2, NBLK, 1, BLK), jnp.float32)),
        in_specs=[SMEM] + [VMEM] * 8,
        out_specs=(VMEM, VMEM),
        scratch_shapes=[
            pltpu.VMEM((ROWS, 1, BLK), jnp.float32),
            pltpu.VMEM((ROWS, 1, BLK), jnp.float32),
            pltpu.VMEM((ROWS, HEAD_DIM, BLK), jnp.float32),
        ],
        compiler_params=pltpu.CompilerParams(vmem_limit_bytes=LIMIT),
        name="query_pass",
    )(table, query_own, grad_own, delta, flat(key), flat(value), peak, total, acc)


def share_kernel(lse_own, delta_all, query_own, grad_own, key_all, value_all, query_part, grad_part, lse_all, query_all,
                 grad_all, key_acc, value_acc, send, recv, send2, recv2, load):
    ring = Ring()
    member = ring.member

    barrier = pltpu.get_barrier_semaphore()
    for step in range(1, GROUP):
        slot = (member + step) % GROUP
        pl.semaphore_signal(barrier, inc=1, device_id=ring.device(slot), device_id_type=MESH)
    pl.semaphore_wait(barrier, GROUP - 1)
    pending = []
    for step in range(1, GROUP):
        device = ring.device((member + step) % GROUP)
        pending.append(remote(lse_own, lse_all.at[:, member], send.at[step], recv.at[step], device))
    mine = pltpu.make_async_copy(lse_own, lse_all.at[:, member], load.at[2, 0])
    mine.start()
    parts, alls = (query_part, grad_part), (query_all, grad_all)
    for a in range(2):
        pending.append(
            remote(parts[a].at[0, ring.down], alls[a].at[0, ring.down], send2.at[a, 0], recv2.at[a, 0], ring.device(ring.up))
        )
        pending.append(
            remote(parts[a].at[1, ring.up], alls[a].at[1, ring.up], send2.at[a, 1], recv2.at[a, 1], ring.device(ring.down))
        )
    held = (ring.member, ring.up, ring.down, ring.twin, ring.twin_up, ring.twin_down)
    loads = []
    for a in range(2):
        for n, slot in enumerate(held):
            loads.append(pltpu.make_async_copy(parts[a].at[:, slot], alls[a].at[:, slot], load.at[a, n]))
            loads[-1].start()

    def relay(n):
        for a in range(2):
            part = alls[a].at[n, ring.far]
            arrived(part, recv2.at[a, n])
            pending.append(remote(part, part, send2.at[a, 2 + n], recv2.at[a, 2 + n], ring.device(ring.twin)))

    for unit in range(2):
        query = query_own[unit].reshape(NBLK * BLK, HEAD_DIM)
        grad = grad_own[unit].reshape(NBLK * BLK, HEAD_DIM)
        delta = jnp.concatenate([delta_all[unit, member, i] for i in range(NBLK)], axis=1)
        lse = jnp.concatenate([lse_own[unit, i] for i in range(NBLK)], axis=1)
        span = WIDE // BLK
        for u in range(0, NBLK, span):
            key = key_all[unit, member, u : u + span].reshape(WIDE, HEAD_DIM)
            value = value_all[unit, member, u : u + span].reshape(WIDE, HEAD_DIM)
            probs = jnp.exp2(dot(key, query, NT) * SCALE2 - lse)
            terms = (probs * (dot(value, grad, NT) - delta)).astype(jnp.bfloat16)
            value_part = dot(probs.astype(jnp.bfloat16), grad)
            key_part = dot(terms, query)
            for s in range(span):
                rows = slice(s * BLK, (s + 1) * BLK)
                value_acc[unit * NBLK + u + s] = value_part[rows]
                key_acc[unit * NBLK + u + s] = key_part[rows]

    relay(0)
    relay(1)
    mine.wait()
    for copy in loads:
        copy.wait()
    for step in range(1, GROUP):
        arrived(lse_own, recv.at[step])
    for a in range(2):
        arrived(alls[a].at[0, ring.twin_far], recv2.at[a, 2])
        arrived(alls[a].at[1, ring.twin_far], recv2.at[a, 3])
    for copy in pending:
        copy.wait_send()


def share_totals(lse_own, delta, query_own, grad_own, key, value, query, grad):
    return pl.pallas_call(
        share_kernel,
        out_shape=(
            jax.ShapeDtypeStruct(STATS, jnp.float32),
            jax.ShapeDtypeStruct(WHOLE, jnp.bfloat16),
            jax.ShapeDtypeStruct(WHOLE, jnp.bfloat16),
            jax.ShapeDtypeStruct((ROWS, BLK, HEAD_DIM), jnp.float32),
            jax.ShapeDtypeStruct((ROWS, BLK, HEAD_DIM), jnp.float32),
        ),
        in_specs=[VMEM] * 6 + [ANY] * 2,
        out_specs=(VMEM,) * 5,
        scratch_shapes=[
            pltpu.SemaphoreType.DMA((GROUP,)),
            pltpu.SemaphoreType.DMA((GROUP,)),
            pltpu.SemaphoreType.DMA((2, 4)),
            pltpu.SemaphoreType.DMA((2, 4)),
            pltpu.SemaphoreType.DMA((3, 6)),
        ],
        compiler_params=pltpu.CompilerParams(collective_id=1, has_side_effects=True, vmem_limit_bytes=LIMIT),
        name="share_totals",
    )(lse_own, delta, query_own, grad_own, key, value, query, grad)


def key_kernel(other, table, key_all, value_all, delta_ref, lse_ref, query_ref, grad_ref, key_in, value_in, out_ref,
               key_acc, value_acc):
    _, half, member = place()
    unit = 1 - half if other else half
    base = unit * NBLK
    for u in range(NBLK):
        key_acc[u] = key_in[base + u]
        value_acc[u] = value_in[base + u]

    def step(turn, carry):
        for first in range(0, NBLK, PAIR):
            blocks = range(first, first + PAIR)
            loads, results = [], []
            for u in blocks:
                row = base + u
                slots = [turn * CHUNK + c for c in range(CHUNK)]
                entries = [table[row, slot] for slot in slots]
                bias = [jnp.where(slot < table[row, COUNT_AT], 0.0, FAR) for slot in slots]
                query = jnp.concatenate([query_ref[e] for e in entries], axis=0)
                grad = jnp.concatenate([grad_ref[e] for e in entries], axis=0)
                lse = jnp.concatenate([lse_ref[e] + b for e, b in zip(entries, bias)], axis=1)
                delta = jnp.concatenate([delta_ref[e] for e in entries], axis=1)
                scores = dot(key_all[unit, member, u], query, NT)
                grads = dot(value_all[unit, member, u], grad, NT)
                loads.append((query, grad, lse, delta, scores, grads))
            for query, grad, lse, delta, scores, grads in loads:
                probs = jnp.exp2(scores * SCALE2 - lse)
                terms = (probs * (grads - delta)).astype(jnp.bfloat16)
                results.append((dot(probs.astype(jnp.bfloat16), grad), dot(terms, query)))
            for n, u in enumerate(blocks):
                value_acc[u] += results[n][0]
                key_acc[u] += results[n][1]
        return carry

    lax.fori_loop(0, turns(table, [base + u for u in range(NBLK)]), step, 0)
    for u in range(NBLK):
        out_ref[0, u] = (key_acc[u] * SCALE).astype(jnp.bfloat16)
        out_ref[1, u] = value_acc[u].astype(jnp.bfloat16)


def key_pass(other, table, key, value, delta, lse, query, grad, key_acc, value_acc):
    def kernel(*refs):
        key_kernel(other, *refs)

    return pl.pallas_call(
        kernel,
        out_shape=jax.ShapeDtypeStruct(OWN, jnp.bfloat16),
        in_specs=[SMEM] + [VMEM] * 8,
        out_specs=VMEM,
        scratch_shapes=[
            pltpu.VMEM((NBLK, BLK, HEAD_DIM), jnp.float32),
            pltpu.VMEM((NBLK, BLK, HEAD_DIM), jnp.float32),
        ],
        compiler_params=pltpu.CompilerParams(vmem_limit_bytes=LIMIT),
        cost_estimate=pl.CostEstimate(flops=2_000_000_000, bytes_accessed=1 << 20, transcendentals=1 << 20),
        name="key_pass_sent" if other else "key_pass_kept",
    )(table, key, value, flat(delta), flat(lse), flat(query), flat(grad), key_acc, value_acc)


def local(queries, key_states, value_states, attn_out, grad_out, frame_order, block_live):
    half = place()[1]
    (key, value, query, grad, delta, query_own, grad_own, peak, total, acc, by_query, by_key) = gather_all(
        frame_order, block_live, key_states, value_states, queries, grad_out, attn_out
    )
    dq, lse_own = query_pass(by_query, query_own, grad_own, delta, key, value, peak, total, acc)
    swap = [(source, (source + GROUP) % (2 * GROUP)) for source in range(2 * GROUP)]

    def across(sent):
        return lax.ppermute(sent, "frame", swap)

    def join(kept, came):
        kept, came = kept.reshape(NBLK * BLK, HEAD_DIM), came.reshape(NBLK * BLK, HEAD_DIM)
        return jnp.concatenate([jnp.where(half == 0, kept, came), jnp.where(half == 0, came, kept)], axis=1)

    dq_came = across(jnp.where(half == 0, dq[1], dq[0]))
    lse, query, grad, key_acc, value_acc = share_totals(lse_own, delta, query_own, grad_own, key, value, query, grad)
    sums = (by_key, key, value, delta, lse, query, grad, key_acc, value_acc)
    came = across(key_pass(True, *sums))
    kept = key_pass(False, *sums)
    return join(jnp.where(half == 0, dq[0], dq[1]), dq_came), join(kept[0], came[0]), join(kept[1], came[1])


def solution(mesh):
    rows = P(("frame", "head"), None)
    out = P("frame", "head")
    return jax.shard_map(
        local,
        mesh=mesh,
        in_specs=(rows, rows, rows, rows, rows, P(), P()),
        out_specs=(out, out, out),
        check_vma=False,
    )
```

time: 910 us -> 132 us (0.15); the launches traced: 893 us -> 132 us
  waiting for transfers between devices: 262 us -> 7.17 us
  starting transfers between devices: 215 us -> 1.83 us
  local copies, waits for them, and re-layouts: 132 us -> 6.7 us
  matrix products: 122 us -> 0 us
  Pallas kernels: 0 us -> 114 us
  loops' own time: 92.5 us -> 0 us
  other arithmetic: 37.4 us -> 2.12 us
  blocking collectives: 18.1 us -> 0 us
  between operations: 14.4 us -> 0.74 us
    ppermute x77 -> x2, waiting for transfers between devices: 231 us -> 7.17 us  [across(): return lax.ppermute(sent, 'frame', swap)]
    ppermute x77 -> x2, starting transfers between devices: 200 us -> 1.83 us  [across(): return lax.ppermute(sent, 'frame', swap)]
    dot_general x42 -> x0, matrix products: 122 us -> none  [the longest x7 34.9 us: pair_grads(): jnp.einsum('hqk,qhd->khd', probs.astype(jnp.bfloat16), grad_blk, preferre...]
    pallas_call x0 -> x5, Pallas kernels: none -> 114 us  [the longest x1 77.4 us: gather_all(): pl.pallas_call(gather_kernel, out_shape=(jax.ShapeDtypeStruct(WHOLE, low)...]
    another operation x33 -> x0, loops' own time: 92.5 us -> none  [the longest x1 60.4 us: local(): lax.scan(one_frame, (start_peak, start_total), (stacked, jnp.arange(count...]
    while x52 -> x0, local copies, waits for them, and re-layouts: 54.1 us -> none
    all_to_all x4 -> x0, waiting for transfers between devices: 30.2 us -> none  [the longest x1 11.5 us: local(): lax.all_to_all(attn_out, 'head', split_axis=1, concat_axis=0, tiled=True)]
    dynamic_slice x48 -> x0, local copies, waits for them, and re-layouts: 29.2 us -> none  [the longest x32 19.3 us: pair_blocks(): distance = jnp.abs(frame_order[slot_query] - frame_order[slot_key])]
  transfers between devices with their start and end apart: 82 -> 2, of which waited for: 55 -> 1; matrix products, arithmetic and copies ran while one was open for 22% -> 1% of each run, Pallas kernels for 0% -> 21%
where the time goes in v2:
time: 132 us
  Pallas kernels  114 us (86%)
  waiting for transfers between devices  7.17 us (5%)
  local copies, waits for them, and re-layouts  6.7 us (5%)
  other arithmetic  2.12 us (2%)
  starting transfers between devices  1.83 us (1%)
    pallas_call x1, Pallas kernels, gather_all(): pl.pallas_call(gather_kernel, out_shape=(jax.ShapeDtypeStruct(WHOLE, low)...  77.4 us
    pallas_call x1, Pallas kernels, share_totals(): pl.pallas_call(share_kernel, out_shape=(jax.ShapeDtypeStruct(STATS, jnp.f...  18.8 us
    pallas_call x2, Pallas kernels, key_pass(): pl.pallas_call(kernel, out_shape=jax.ShapeDtypeStruct(OWN, jnp.bfloat16),...  8.68 us
    pallas_call x1, Pallas kernels, query_pass(): pl.pallas_call(query_kernel, out_shape=(jax.ShapeDtypeStruct(OWN, jnp.bfl...  8.67 us
    ppermute x2, waiting for transfers between devices, across(): return lax.ppermute(sent, 'frame', swap)  7.17 us
    unnamed x13, local copies, waits for them, and re-layouts  6.7 us
  transfers between devices with their start and end apart: 2, of which 1 were waited for; matrix products, arithmetic and copies ran while one was open for 1% of the time, Pallas kernels for 21%

profile of v2, /device:TPU:1, one launch (start us, length us, event | category | flops | bytes accessed | tf_op | source)
XLA Modules:
  0.0 132.1 jit_solution(12969355281170453845)
XLA Ops:
  0.6 0.8 copy.10.live_ref
  1.5 0.0 copy-start
  1.5 1.0 copy-done
  2.5 0.0 copy-start.1
  2.6 1.0 copy-done.1
  3.6 0.0 copy-start.2
  3.6 1.0 copy-done.2
  4.6 0.0 copy-start.3
  4.6 1.0 copy-done.3
  5.7 0.0 copy-start.4
  5.7 1.0 copy-done.4
  6.7 0.0 copy-start.5
  6.7 0.7 copy-done.5
  7.4 77.4 %gather_all.1 = (bf16[2,8,8,128,128]{4,3,2,1,0:T(8,128)(2,1)S(1)}, bf16[2,8,8,128,128]{4,3,2,1,0:T(8,128)(2,1)S(1)}, bf16[2,8,8,128,128]{4,3,2,1,0:T(8,128)(2,1)...) custom-call(s32[16]{0:T(128)S(1)} %copy-done.5, ...), custom_call_target="tpu_custom_call" | custom-call | tf_op jit(solution)/shard_map/gather_all/pallas_call | solution.py:230
  84.8 8.7 %query_pass.1 = (bf16[2,8,128,128]{3,2,1,0:T(8,128)(2,1)S(1)}, f32[2,8,1,128]{3,2,1,0:T(1,128)S(1)}) custom-call(s32[16,128]{1,0:T(8,128)S(1)} %get-tuple-element.22.table, bf16[2,8,128,128]{3,2,1,0:T(8,128)(2,1)S(1)} %get-tuple-element.23.query_own, bf16[2,8,128,128]{3,2,1,0:T(8,128)(2,1)S(1)} %get-tuple-element.24.grad_own, ...), custom_call_target="tpu_custom_call" | custom-call | tf_op jit(solution)/shard_map/query_pass/pallas_call | solution.py:317
  93.5 1.2 collective-permute-start
  94.7 18.8 %share_totals.1 = (f32[2,8,8,1,128]{4,3,2,1,0:T(1,128)S(1)}, bf16[2,8,8,128,128]{4,3,2,1,0:T(8,128)(2,1)S(1)}, bf16[2,8,8,128,128]{4,3,2,1,0:T(8,128)(2,1)S(1)},...) custom-call(f32[2,8,1,128]{3,2,1,0:T(1,128)S(1)} %get-tuple-element.33.lse_own, ...), custom_call_target="tpu_custom_call" | custom-call | tf_op jit(solution)/shard_map/share_totals/pallas_call | solution.py:402
  113.5 4.3 %key_pass_sent.1 = bf16[2,8,128,128]{3,2,1,0:T(8,128)(2,1)S(1)} custom-call(s32[16,128]{1,0:T(8,128)S(1)} %get-tuple-element.32.refs_0_, bf16[2,8,8,128,128]{4,3,2,1,0:T(8,128)(2,1)S(1)} %get-tuple-element.26.key_all.refs_1_, bf16[2,8,8,128,128]{4,3,2,1,0:T(8,128)(2,1)S(1)} %get-tuple-element.27.value_all.refs_2_, f32[128,1,128]{2,1,0:T(1,128)S(1)} %bitcast.24, ...), custom_call_target="tpu_custom_call" | custom-call | flops 2000000000 | bytes 1048576 | tf_op jit(solution)/shard_map/key_pass_sent/pallas_call | solution.py:469
  117.8 0.6 collective-permute-start.1
  118.5 4.3 %key_pass_kept.1 = bf16[2,8,128,128]{3,2,1,0:T(8,128)(2,1)S(1)} custom-call(s32[16,128]{1,0:T(8,128)S(1)} %get-tuple-element.32.refs_0_, bf16[2,8,8,128,128]{4,3,2,1,0:T(8,128)(2,1)S(1)} %get-tuple-element.26.key_all.refs_1_, bf16[2,8,8,128,128]{4,3,2,1,0:T(8,128)(2,1)S(1)} %get-tuple-element.27.value_all.refs_2_, f32[128,1,128]{2,1,0:T(1,128)S(1)} %bitcast.25, ...), custom_call_target="tpu_custom_call" | custom-call | flops 2000000000 | bytes 1048576 | tf_op jit(solution)/shard_map/key_pass_kept/pallas_call | solution.py:469
  122.8 0.0 collective-permute-done
  122.8 0.1 bitcast_select_fusion.1
  122.9 0.9 pad_maximum_fusion
  123.7 7.2 %collective-permute-done.1 = bf16[2,8,128,128]{3,2,1,0:T(8,128)(2,1)S(1)} collective-permute-done((bf16[2,8,128,128]{3,2,1,0:T(8,128)(2,1)S(1)}, bf16[2,8,128,128]{3,2,1,0:T(8,128)(2,1)S(1)}, u32[]{:S(2)}, u32[]{:S(2)}) %collective-permute-start.1) | collective-permute-done | bytes 524320 | tf_op jit(solution)/shard_map/ppermute | solution.py:493
  130.9 0.1 broadcast_select_fusion.1
  131.0 1.1 pad_maximum_fusion.1
  (1 shorter events, 0.0 us)
Async XLA Ops:
  1.5 1.0 copy-start
  2.5 1.0 copy-start.1
  3.6 1.0 copy-start.2
  4.6 1.0 copy-start.3
  5.7 1.0 copy-start.4
  6.7 0.7 copy-start.5
  93.5 29.3 %collective-permute-start = (bf16[8,128,128]{2,1,0:T(8,128)(2,1)S(1)}, bf16[8,128,128]{2,1,0:T(8,128)(2,1)S(1)}, u32[]{:S(2)}, u32[]{:S(2)}) collective-permute-start(bf16[8,128,128]{2,1,0:T(8,128)(2,1)S(1)} %get-tuple-element.48), channel_id=1, source_target_pairs={{0,8},{1,9},{2,10},{3,11},{4,12},{5,13},{6,14},{7,15},{8,0},{9,1},... | collective-permute-start | bytes 786440 | tf_op jit(solution)/shard_map/ppermute | solution.py:493
  117.8 13.1 %collective-permute-start.1 = (bf16[2,8,128,128]{3,2,1,0:T(8,128)(2,1)S(1)}, bf16[2,8,128,128]{3,2,1,0:T(8,128)(2,1)S(1)}, u32[]{:S(2)}, u32[]{:S(2)}) collective-permute-start(bf16[2,8,128,128]{3,2,1,0:T(8,128)(2,1)S(1)} %key_pass_sent.1), channel_id=1, source_target_pairs={{0,8},{1,9},{2,10},{3,11},{4,12},{5,13},{6,14},{7,15},{8,0},{9,1},... | collective-permute-start | bytes 1572872 | tf_op jit(solution)/shard_map/ppermute | solution.py:493

commit v3 on v2

--- a/solution.py
+++ b/solution.py
@@ -27,6 +27,7 @@
 MESH = pl.DeviceIdType.MESH
 ANY = pl.BlockSpec(memory_space=pl.ANY)
 SMEM = pl.BlockSpec(memory_space=pltpu.SMEM)
+HBM = pl.BlockSpec(memory_space=pltpu.HBM)
 VMEM = pl.BlockSpec(memory_space=pltpu.VMEM)
 NN = (((1,), (0,)), ((), ()))
 NT = (((1,), (1,)), ((), ()))
@@ -107,9 +108,9 @@
     by_key_ref[...] = live_list(jnp.concatenate(key_rows, axis=0))
 
 
-def gather_kernel(order_ref, live_ref, grad_ref, out_ref, key_src, value_src, query_src, grad_src, key_all, value_all,
-                  query_all, grad_all, delta_all, query_own, grad_own, peak, total, acc, by_query_ref, by_key_ref,
-                  delta_src, send1, recv1, send2, recv2, load):
+def gather_kernel(order_src, live_src, out_src, key_src, value_src, query_src, grad_src, key_all, value_all, query_all,
+                  grad_all, delta_all, query_own, grad_own, peak, total, acc, by_query_ref, by_key_ref, delta_src, raw,
+                  grad_raw, out_raw, order_ref, live_ref, send1, recv1, send2, recv2, send3, recv3, load):
     ring = Ring()
     head, half, member = ring.head, ring.half, ring.member
     plane = head * 2 + half
@@ -120,6 +121,14 @@
         other = (plane + step) % HEADS
         return other, {"head": other // 2, "frame": (other % 2) * GROUP + member}
 
+    fetches = [
+        pltpu.make_async_copy(grad_src, grad_raw, load.at[0]),
+        pltpu.make_async_copy(out_src, out_raw, load.at[1]),
+        pltpu.make_async_copy(order_src, order_ref, load.at[2]),
+        pltpu.make_async_copy(live_src, live_ref, load.at[3]),
+    ]
+    for fetch in fetches:
+        fetch.start()
     barrier = pltpu.get_barrier_semaphore()
     for step in range(1, HEADS):
         pl.semaphore_signal(barrier, inc=1, device_id=plane_peer(step)[1], device_id_type=MESH)
@@ -127,44 +136,66 @@
         pl.semaphore_signal(barrier, inc=1, device_id=ring.device(slot), device_id_type=MESH)
     pl.semaphore_wait(barrier, HEADS - 1 + 3)
 
-    def column(a, other):
-        if a == DELTA:
-            return srcs[a].at[other]
-        return srcs[a].at[:, pl.ds(pl.multiple_of(other * HEAD_DIM, HEAD_DIM), HEAD_DIM)]
-
-    def scatter(a):
-        target = bufs[a].at[half, member, head]
+    pending = []
+    pending.append(remote(query_src, raw.at[0], send3.at[0], recv3.at[0], ring.device(ring.up)))
+    pending.append(remote(query_src, raw.at[1], send3.at[1], recv3.at[1], ring.device(ring.down)))
+
+    def column(src, other):
+        if src is delta_src:
+            return src.at[other]
+        return src.at[:, pl.ds(pl.multiple_of(other * HEAD_DIM, HEAD_DIM), HEAD_DIM)]
+
+    def scatter(src, target, send, recv):
         for step in range(1, HEADS):
             other, device = plane_peer(step)
-            remote(column(a, other), target, send1.at[a], recv1.at[a], device)
-        pltpu.make_async_copy(column(a, plane), target, recv1.at[a]).start()
+            remote(column(src, other), target, send, recv, device)
+        pltpu.make_async_copy(column(src, plane), target, recv).start()
 
     for a in (KEY, VALUE, QUERY, GRAD):
-        scatter(a)
+        scatter(srcs[a], bufs[a].at[half, member, head], send1.at[a], recv1.at[a])
+    fetches[0].wait()
+    fetches[1].wait()
     for n in range(HEADS):
         lanes = slice(n * HEAD_DIM, (n + 1) * HEAD_DIM)
-        products = grad_ref[:, lanes].astype(jnp.float32) * out_ref[:, lanes].astype(jnp.float32)
+        products = grad_raw[:, lanes].astype(jnp.float32) * out_raw[:, lanes].astype(jnp.float32)
         delta_src[n] = jnp.sum(products.T, axis=0, keepdims=True)
-    scatter(DELTA)
-
-    pending = []
+    scatter(delta_src, bufs[DELTA].at[half, member, head], send1.at[DELTA], recv1.at[DELTA])
 
     def push(a, number, part, slot, arrive):
         pending.append(remote(part, part, send2.at[a, number], recv2.at[a, arrive], ring.device(slot)))
 
-    for a in (KEY, VALUE, QUERY, GRAD, DELTA):
+    def spread(a):
         own = bufs[a].at[:, member]
         arrived(own, recv1.at[a])
-        push(a, 0, own, ring.up, 0)
-        push(a, 1, own, ring.down, 1)
+        if a != QUERY:
+            push(a, 0, own, ring.up, 0)
+            push(a, 1, own, ring.down, 1)
         push(a, 2, own, ring.twin, 4)
-        if a in (QUERY, GRAD):
-            kept = query_own if a == QUERY else grad_own
-            pltpu.make_async_copy(own, kept, load.at[a - QUERY]).start()
-        if a == KEY:
-            write_tables(member, order_ref, live_ref, by_query_ref, by_key_ref)
-    pltpu.make_async_copy(bufs[QUERY].at[:, member], query_own, load.at[0]).wait()
-    pltpu.make_async_copy(bufs[GRAD].at[:, member], grad_own, load.at[1]).wait()
+
+    def pass_raw(number, slot):
+        scatter(raw.at[number], bufs[QUERY].at[half, slot, head], send1.at[5 + number], recv1.at[5 + number])
+
+    upper, lower = pl.ds(0, BLK // 2), pl.ds(BLK // 2, BLK // 2)
+    spread(KEY)
+    fetches[2].wait()
+    fetches[3].wait()
+    write_tables(member, order_ref, live_ref, by_query_ref, by_key_ref)
+    spread(VALUE)
+    arrived(raw.at[0], recv3.at[0])
+    pending.append(remote(raw.at[0, upper], raw.at[2, upper], send3.at[2], recv3.at[2], ring.device(ring.up)))
+    pass_raw(0, ring.down)
+    arrived(raw.at[1], recv3.at[1])
+    pending.append(remote(raw.at[1, lower], raw.at[2, lower], send3.at[3], recv3.at[3], ring.device(ring.down)))
+    pass_raw(1, ring.up)
+    spread(QUERY)
+    fetch_query = pltpu.make_async_copy(bufs[QUERY].at[:, member], query_own, load.at[4])
+    fetch_query.start()
+    spread(GRAD)
+    fetch_grad = pltpu.make_async_copy(bufs[GRAD].at[:, member], grad_own, load.at[5])
+    fetch_grad.start()
+    spread(DELTA)
+    fetch_query.wait()
+    fetch_grad.wait()
 
     span = WIDE // BLK
     for unit in range(2):
@@ -187,17 +218,26 @@
                 total[row] = summed[:, lanes]
                 acc[row] = partial[:, lanes]
 
-    for a in (KEY, VALUE, QUERY, GRAD, DELTA):
+    arrived(raw.at[2, upper], recv3.at[2])
+    arrived(raw.at[2, lower], recv3.at[3])
+    pass_raw(2, ring.far)
+    arrived(bufs[QUERY].at[:, ring.down], recv1.at[5])
+    push(QUERY, 4, bufs[QUERY].at[:, ring.down], ring.twin, 5)
+    arrived(bufs[QUERY].at[:, ring.up], recv1.at[6])
+    push(QUERY, 6, bufs[QUERY].at[:, ring.up], ring.twin, 6)
+    for a in (KEY, VALUE, GRAD, DELTA):
         part = bufs[a].at[:, ring.down]
         arrived(part, recv2.at[a, 0])
-        if a not in (QUERY, GRAD):
+        if a != GRAD:
             push(a, 3, bufs[a].at[0, ring.down], ring.up, 2)
         push(a, 4, part, ring.twin, 5)
         part = bufs[a].at[:, ring.up]
         arrived(part, recv2.at[a, 1])
-        if a not in (QUERY, GRAD):
+        if a != GRAD:
             push(a, 5, bufs[a].at[1, ring.up], ring.down, 3)
         push(a, 6, part, ring.twin, 6)
+    arrived(bufs[QUERY].at[:, ring.far], recv1.at[7])
+    push(QUERY, 7, bufs[QUERY].at[:, ring.far], ring.twin, 7)
     for a in (KEY, VALUE, DELTA):
         part = bufs[a].at[0, ring.far]
         arrived(part, recv2.at[a, 2])
@@ -209,13 +249,16 @@
         arrived(bufs[a].at[:, ring.twin], recv2.at[a, 4])
         arrived(bufs[a].at[:, ring.twin_down], recv2.at[a, 5])
         arrived(bufs[a].at[:, ring.twin_up], recv2.at[a, 6])
-        if a not in (QUERY, GRAD):
+        if a == QUERY:
+            arrived(bufs[a].at[:, ring.twin_far], recv2.at[a, 7])
+        elif a != GRAD:
             arrived(bufs[a].at[0, ring.twin_far], recv2.at[a, 7])
             arrived(bufs[a].at[1, ring.twin_far], recv2.at[a, 8])
     for copy in pending:
         copy.wait_send()
-    for a in range(5):
-        sent = srcs[a].at[pl.ds(0, HEADS - 1)] if a == DELTA else srcs[a].at[:, pl.ds(0, (HEADS - 1) * HEAD_DIM)]
+    for a in range(8):
+        source = srcs[a] if a < 5 else raw.at[a - 5]
+        sent = source.at[pl.ds(0, HEADS - 1)] if a == DELTA else source.at[:, pl.ds(0, (HEADS - 1) * HEAD_DIM)]
         arrived(sent, send1.at[a])
 
 
@@ -243,19 +286,26 @@
             jax.ShapeDtypeStruct((ROWS, ENTRIES), whole),
             jax.ShapeDtypeStruct((ROWS, ENTRIES), whole),
         ),
-        in_specs=[SMEM, VMEM, VMEM, VMEM, ANY, ANY, ANY, ANY],
-        out_specs=(VMEM, VMEM, ANY, ANY) + (VMEM,) * 8,
+        in_specs=[HBM] * 7,
+        out_specs=(VMEM, VMEM, VMEM, ANY) + (VMEM,) * 8,
         scratch_shapes=[
             pltpu.VMEM((HEADS, 1, BLK), full),
-            pltpu.SemaphoreType.DMA((5,)),
-            pltpu.SemaphoreType.DMA((5,)),
+            pltpu.VMEM((3, BLK, HEADS * HEAD_DIM), low),
+            pltpu.VMEM((BLK, HEADS * HEAD_DIM), low),
+            pltpu.VMEM((BLK, HEADS * HEAD_DIM), low),
+            pltpu.SMEM((2 * GROUP,), whole),
+            pltpu.VMEM((2 * GROUP, NBLK, NBLK), whole),
+            pltpu.SemaphoreType.DMA((8,)),
+            pltpu.SemaphoreType.DMA((8,)),
             pltpu.SemaphoreType.DMA((5, 9)),
             pltpu.SemaphoreType.DMA((5, 9)),
-            pltpu.SemaphoreType.DMA((2,)),
+            pltpu.SemaphoreType.DMA((4,)),
+            pltpu.SemaphoreType.DMA((4,)),
+            pltpu.SemaphoreType.DMA((6,)),
         ],
         compiler_params=pltpu.CompilerParams(collective_id=0, has_side_effects=True, vmem_limit_bytes=LIMIT),
         name="gather_all",
-    )(order, live, grad, out, key, value, query, grad)
+    )(order, live, out, key, value, query, grad)
 
 
 def turns(table, rows):
@@ -329,8 +379,8 @@
     )(table, query_own, grad_own, delta, flat(key), flat(value), peak, total, acc)
 
 
-def share_kernel(lse_own, delta_all, query_own, grad_own, key_all, value_all, query_part, grad_part, lse_all, query_all,
-                 grad_all, key_acc, value_acc, send, recv, send2, recv2, load):
+def share_kernel(lse_own, delta_all, query_own, grad_own, key_all, value_all, grad_part, lse_all, grad_all,
+                 key_acc, value_acc, send, recv, send2, recv2, load):
     ring = Ring()
     member = ring.member
 
@@ -343,28 +393,24 @@
     for step in range(1, GROUP):
         device = ring.device((member + step) % GROUP)
         pending.append(remote(lse_own, lse_all.at[:, member], send.at[step], recv.at[step], device))
-    mine = pltpu.make_async_copy(lse_own, lse_all.at[:, member], load.at[2, 0])
+    mine = pltpu.make_async_copy(lse_own, lse_all.at[:, member], load.at[6])
     mine.start()
-    parts, alls = (query_part, grad_part), (query_all, grad_all)
-    for a in range(2):
-        pending.append(
-            remote(parts[a].at[0, ring.down], alls[a].at[0, ring.down], send2.at[a, 0], recv2.at[a, 0], ring.device(ring.up))
-        )
-        pending.append(
-            remote(parts[a].at[1, ring.up], alls[a].at[1, ring.up], send2.at[a, 1], recv2.at[a, 1], ring.device(ring.down))
-        )
+    pending.append(
+        remote(grad_part.at[0, ring.down], grad_all.at[0, ring.down], send2.at[0], recv2.at[0], ring.device(ring.up))
+    )
+    pending.append(
+        remote(grad_part.at[1, ring.up], grad_all.at[1, ring.up], send2.at[1], recv2.at[1], ring.device(ring.down))
+    )
     held = (ring.member, ring.up, ring.down, ring.twin, ring.twin_up, ring.twin_down)
     loads = []
-    for a in range(2):
-        for n, slot in enumerate(held):
-            loads.append(pltpu.make_async_copy(parts[a].at[:, slot], alls[a].at[:, slot], load.at[a, n]))
-            loads[-1].start()
+    for n, slot in enumerate(held):
+        loads.append(pltpu.make_async_copy(grad_part.at[:, slot], grad_all.at[:, slot], load.at[n]))
+        loads[-1].start()
 
     def relay(n):
-        for a in range(2):
-            part = alls[a].at[n, ring.far]
-            arrived(part, recv2.at[a, n])
-            pending.append(remote(part, part, send2.at[a, 2 + n], recv2.at[a, 2 + n], ring.device(ring.twin)))
+        part = grad_all.at[n, ring.far]
+        arrived(part, recv2.at[n])
+        pending.append(remote(part, part, send2.at[2 + n], recv2.at[2 + n], ring.device(ring.twin)))
 
     for unit in range(2):
         query = query_own[unit].reshape(NBLK * BLK, HEAD_DIM)
@@ -391,35 +437,33 @@
         copy.wait()
     for step in range(1, GROUP):
         arrived(lse_own, recv.at[step])
-    for a in range(2):
-        arrived(alls[a].at[0, ring.twin_far], recv2.at[a, 2])
-        arrived(alls[a].at[1, ring.twin_far], recv2.at[a, 3])
+    arrived(grad_all.at[0, ring.twin_far], recv2.at[2])
+    arrived(grad_all.at[1, ring.twin_far], recv2.at[3])
     for copy in pending:
         copy.wait_send()
 
 
-def share_totals(lse_own, delta, query_own, grad_own, key, value, query, grad):
+def share_totals(lse_own, delta, query_own, grad_own, key, value, grad):
     return pl.pallas_call(
         share_kernel,
         out_shape=(
             jax.ShapeDtypeStruct(STATS, jnp.float32),
             jax.ShapeDtypeStruct(WHOLE, jnp.bfloat16),
-            jax.ShapeDtypeStruct(WHOLE, jnp.bfloat16),
             jax.ShapeDtypeStruct((ROWS, BLK, HEAD_DIM), jnp.float32),
             jax.ShapeDtypeStruct((ROWS, BLK, HEAD_DIM), jnp.float32),
         ),
-        in_specs=[VMEM] * 6 + [ANY] * 2,
-        out_specs=(VMEM,) * 5,
+        in_specs=[VMEM] * 6 + [ANY],
+        out_specs=(VMEM,) * 4,
         scratch_shapes=[
             pltpu.SemaphoreType.DMA((GROUP,)),
             pltpu.SemaphoreType.DMA((GROUP,)),
-            pltpu.SemaphoreType.DMA((2, 4)),
-            pltpu.SemaphoreType.DMA((2, 4)),
-            pltpu.SemaphoreType.DMA((3, 6)),
+            pltpu.SemaphoreType.DMA((4,)),
+            pltpu.SemaphoreType.DMA((4,)),
+            pltpu.SemaphoreType.DMA((7,)),
         ],
         compiler_params=pltpu.CompilerParams(collective_id=1, has_side_effects=True, vmem_limit_bytes=LIMIT),
         name="share_totals",
-    )(lse_own, delta, query_own, grad_own, key, value, query, grad)
+    )(lse_own, delta, query_own, grad_own, key, value, grad)
 
 
 def key_kernel(other, table, key_all, value_all, delta_ref, lse_ref, query_ref, grad_ref, key_in, value_in, out_ref,
@@ -497,7 +541,7 @@
         return jnp.concatenate([jnp.where(half == 0, kept, came), jnp.where(half == 0, came, kept)], axis=1)
 
     dq_came = across(jnp.where(half == 0, dq[1], dq[0]))
-    lse, query, grad, key_acc, value_acc = share_totals(lse_own, delta, query_own, grad_own, key, value, query, grad)
+    lse, grad, key_acc, value_acc = share_totals(lse_own, delta, query_own, grad_own, key, value, grad)
     sums = (by_key, key, value, delta, lse, query, grad, key_acc, value_acc)
     came = across(key_pass(True, *sums))
     kept = key_pass(False, *sums)

time: 132 us -> 125 us (0.947)
  Pallas kernels: 114 us -> 106 us
    pallas_call x1, Pallas kernels: 18.8 us -> 12.6 us  [share_totals(): pl.pallas_call(share_kernel, out_shape=(jax.ShapeDtypeStruct(STATS, jnp.f...]
  transfers between devices with their start and end apart: 2 -> 2, of which waited for: 1 -> 1; matrix products, arithmetic and copies ran while one was open for 1% -> 1% of each run, Pallas kernels for 21% -> 17%
where the time goes in v3:
time: 125 us
  Pallas kernels  106 us (85%)
  waiting for transfers between devices  6.97 us (6%)
  local copies, waits for them, and re-layouts  6.7 us (5%)
  other arithmetic  2.12 us (2%)
  starting transfers between devices  1.81 us (1%)
    pallas_call x1, Pallas kernels, gather_all(): pl.pallas_call(gather_kernel, out_shape=(jax.ShapeDtypeStruct(WHOLE, low)...  76.2 us
    pallas_call x1, Pallas kernels, share_totals(): pl.pallas_call(share_kernel, out_shape=(jax.ShapeDtypeStruct(STATS, jnp.f...  12.6 us
    pallas_call x2, Pallas kernels, key_pass(): pl.pallas_call(kernel, out_shape=jax.ShapeDtypeStruct(OWN, jnp.bfloat16),...  8.85 us
    pallas_call x1, Pallas kernels, query_pass(): pl.pallas_call(query_kernel, out_shape=(jax.ShapeDtypeStruct(OWN, jnp.bfl...  8.63 us
    ppermute x2, waiting for transfers between devices, across(): return lax.ppermute(sent, 'frame', swap)  6.97 us
    unnamed x13, local copies, waits for them, and re-layouts  6.7 us
  transfers between devices with their start and end apart: 2, of which 1 were waited for; matrix products, arithmetic and copies ran while one was open for 1% of the time, Pallas kernels for 17%

profile of v3, /device:TPU:1, one launch (start us, length us, event | category | flops | bytes accessed | tf_op | source)
XLA Modules:
  0.0 124.6 jit_solution(17510691658079475233)
XLA Ops:
  0.6 0.8 copy.10.live_src
  1.5 0.0 copy-start
  1.5 1.0 copy-done
  2.5 0.0 copy-start.1
  2.6 1.0 copy-done.1
  3.6 0.0 copy-start.2
  3.6 1.0 copy-done.2
  4.6 0.0 copy-start.3
  4.6 1.0 copy-done.3
  5.7 0.0 copy-start.4
  5.7 1.0 copy-done.4
  6.7 0.0 copy-start.5
  6.7 0.7 copy-done.5
  7.4 76.2 %gather_all.1 = (bf16[2,8,8,128,128]{4,3,2,1,0:T(8,128)(2,1)S(1)}, bf16[2,8,8,128,128]{4,3,2,1,0:T(8,128)(2,1)S(1)}, bf16[2,8,8,128,128]{4,3,2,1,0:T(8,128)(2,1)...) custom-call(s32[16]{0:T(128)S(1)} %copy-done.5, ...), custom_call_target="tpu_custom_call" | custom-call | tf_op jit(solution)/shard_map/gather_all/pallas_call | solution.py:273
  83.6 8.6 %query_pass.1 = (bf16[2,8,128,128]{3,2,1,0:T(8,128)(2,1)S(1)}, f32[2,8,1,128]{3,2,1,0:T(1,128)S(1)}) custom-call(s32[16,128]{1,0:T(8,128)S(1)} %get-tuple-element.21.table, bf16[2,8,128,128]{3,2,1,0:T(8,128)(2,1)S(1)} %get-tuple-element.22.query_own, bf16[2,8,128,128]{3,2,1,0:T(8,128)(2,1)S(1)} %get-tuple-element.23.grad_own, ...), custom_call_target="tpu_custom_call" | custom-call | tf_op jit(solution)/shard_map/query_pass/pallas_call | solution.py:367
  92.3 0.6 collective-permute-start
  92.8 12.6 %share_totals.1 = (f32[2,8,8,1,128]{4,3,2,1,0:T(1,128)S(1)}, bf16[2,8,8,128,128]{4,3,2,1,0:T(8,128)(2,1)S(1)}, f32[16,128,128]{2,1,0:T(8,128)S(1)}, f32[16,128,128]{2,1,0:T(8,128)S(1)}) custom-call(f32[2,8,1,128]{3,2,1,0:T(1,128)S(1)} %get-tuple-element.32.lse_own, f32[2,8,8,1,128]{4,3,2,1,0:T(1,128)S(1)} %get-tuple-element.24.delta_all, ...), custom_call_target="tpu_custom_call" | custom-call | tf_op jit(solution)/shard_map/share_totals/pallas_call | solution.py:447
  105.5 4.4 %key_pass_sent.1 = bf16[2,8,128,128]{3,2,1,0:T(8,128)(2,1)S(1)} custom-call(s32[16,128]{1,0:T(8,128)S(1)} %get-tuple-element.31.refs_0_, bf16[2,8,8,128,128]{4,3,2,1,0:T(8,128)(2,1)S(1)} %get-tuple-element.25.key_all.refs_1_, bf16[2,8,8,128,128]{4,3,2,1,0:T(8,128)(2,1)S(1)} %get-tuple-element.26.value_all.refs_2_, f32[128,1,128]{2,1,0:T(1,128)S(1)} %bitcast.24, ...), custom_call_target="tpu_custom_call" | custom-call | flops 2000000000 | bytes 1048576 | tf_op jit(solution)/shard_map/key_pass_sent/pallas_call | solution.py:513
  109.9 1.2 collective-permute-start.1
  111.1 4.4 %key_pass_kept.1 = bf16[2,8,128,128]{3,2,1,0:T(8,128)(2,1)S(1)} custom-call(s32[16,128]{1,0:T(8,128)S(1)} %get-tuple-element.31.refs_0_, bf16[2,8,8,128,128]{4,3,2,1,0:T(8,128)(2,1)S(1)} %get-tuple-element.25.key_all.refs_1_, bf16[2,8,8,128,128]{4,3,2,1,0:T(8,128)(2,1)S(1)} %get-tuple-element.26.value_all.refs_2_, f32[128,1,128]{2,1,0:T(1,128)S(1)} %bitcast.25, ...), custom_call_target="tpu_custom_call" | custom-call | flops 2000000000 | bytes 1048576 | tf_op jit(solution)/shard_map/key_pass_kept/pallas_call | solution.py:513
  115.6 0.0 collective-permute-done
  115.6 0.1 bitcast_select_fusion.1
  115.6 0.9 pad_maximum_fusion
  116.5 7.0 %collective-permute-done.1 = bf16[2,8,128,128]{3,2,1,0:T(8,128)(2,1)S(1)} collective-permute-done((bf16[2,8,128,128]{3,2,1,0:T(8,128)(2,1)S(1)}, bf16[2,8,128,128]{3,2,1,0:T(8,128)(2,1)S(1)}, u32[]{:S(2)}, u32[]{:S(2)}) %collective-permute-start.1) | collective-permute-done | bytes 524320 | tf_op jit(solution)/shard_map/ppermute | solution.py:537
  123.5 0.1 broadcast_select_fusion.1
  123.5 1.1 pad_maximum_fusion.1
  (1 shorter events, 0.0 us)
Async XLA Ops:
  1.5 1.0 copy-start
  2.5 1.0 copy-start.1
  3.6 1.0 copy-start.2
  4.6 1.0 copy-start.3
  5.7 1.0 copy-start.4
  6.7 0.7 copy-start.5
  92.3 23.3 %collective-permute-start = (bf16[8,128,128]{2,1,0:T(8,128)(2,1)S(1)}, bf16[8,128,128]{2,1,0:T(8,128)(2,1)S(1)}, u32[]{:S(2)}, u32[]{:S(2)}) collective-permute-start(bf16[8,128,128]{2,1,0:T(8,128)(2,1)S(1)} %get-tuple-element.46), channel_id=1, source_target_pairs={{0,8},{1,9},{2,10},{3,11},{4,12},{5,13},{6,14},{7,15},{8,0},{9,1},... | collective-permute-start | bytes 786440 | tf_op jit(solution)/shard_map/ppermute | solution.py:537
  109.9 13.6 %collective-permute-start.1 = (bf16[2,8,128,128]{3,2,1,0:T(8,128)(2,1)S(1)}, bf16[2,8,128,128]{3,2,1,0:T(8,128)(2,1)S(1)}, u32[]{:S(2)}, u32[]{:S(2)}) collective-permute-start(bf16[2,8,128,128]{3,2,1,0:T(8,128)(2,1)S(1)} %key_pass_sent.1), channel_id=1, source_target_pairs={{0,8},{1,9},{2,10},{3,11},{4,12},{5,13},{6,14},{7,15},{8,0},{9,1},... | collective-permute-start | bytes 1572872 | tf_op jit(solution)/shard_map/ppermute | solution.py:537

commit v4 on v3

--- a/solution.py
+++ b/solution.py
@@ -305,7 +305,7 @@
         ],
         compiler_params=pltpu.CompilerParams(collective_id=0, has_side_effects=True, vmem_limit_bytes=LIMIT),
         name="gather_all",
-    )(order, live, out, key, value, query, grad)
+    )(*(pltpu.with_memory_space_constraint(x, pltpu.HBM) for x in (order, live, out, key, value, query, grad)))
 
 
 def turns(table, rows):

time: 125 us -> 119 us (0.952)
  local copies, waits for them, and re-layouts: 6.7 us -> 1.47 us
    unnamed x13 -> x1, local copies, waits for them, and re-layouts: 6.7 us -> 1.47 us
  transfers between devices with their start and end apart: 2 -> 2, of which waited for: 1 -> 1; matrix products, arithmetic and copies ran while one was open for 1% -> 1% of each run, Pallas kernels for 17% -> 18%
where the time goes in v4:
time: 119 us
  Pallas kernels  106 us (89%)
  waiting for transfers between devices  6.93 us (6%)
  other arithmetic  2.12 us (2%)
  starting transfers between devices  1.8 us (2%)
  local copies, waits for them, and re-layouts  1.47 us (1%)
    pallas_call x1, Pallas kernels, gather_all(): pl.pallas_call(gather_kernel, out_shape=(jax.ShapeDtypeStruct(WHOLE, low)...  76.2 us
    pallas_call x1, Pallas kernels, share_totals(): pl.pallas_call(share_kernel, out_shape=(jax.ShapeDtypeStruct(STATS, jnp.f...  12.6 us
    pallas_call x2, Pallas kernels, key_pass(): pl.pallas_call(kernel, out_shape=jax.ShapeDtypeStruct(OWN, jnp.bfloat16),...  8.74 us
    pallas_call x1, Pallas kernels, query_pass(): pl.pallas_call(query_kernel, out_shape=(jax.ShapeDtypeStruct(OWN, jnp.bfl...  8.68 us
    ppermute x2, waiting for transfers between devices, across(): return lax.ppermute(sent, 'frame', swap)  6.93 us
  transfers between devices with their start and end apart: 2, of which 1 were waited for; matrix products, arithmetic and copies ran while one was open for 1% of the time, Pallas kernels for 18%

profile of v4, /device:TPU:1, one launch (start us, length us, event | category | flops | bytes accessed | tf_op | source)
XLA Modules:
  0.0 119.2 jit_solution(13166077347993484398)
XLA Ops:
  0.6 1.5 %copy.10.live_src = s32[16,8,8]{2,1,0:T(8,128)} copy(s32[16,8,8]{0,2,1:T(8,128)} %param.13) | data formatting | bytes 8192 | tf_op args[6]
  2.1 76.2 %gather_all.1 = (bf16[2,8,8,128,128]{4,3,2,1,0:T(8,128)(2,1)S(1)}, bf16[2,8,8,128,128]{4,3,2,1,0:T(8,128)(2,1)S(1)}, bf16[2,8,8,128,128]{4,3,2,1,0:T(8,128)(2,1)...) custom-call(s32[16]{0:T(128)} %order_src.1, ...), custom_call_target="tpu_custom_call" | custom-call | tf_op jit(solution)/shard_map/gather_all/pallas_call | solution.py:273
  78.3 8.7 %query_pass.1 = (bf16[2,8,128,128]{3,2,1,0:T(8,128)(2,1)S(1)}, f32[2,8,1,128]{3,2,1,0:T(1,128)S(1)}) custom-call(s32[16,128]{1,0:T(8,128)S(1)} %get-tuple-element.21.table, bf16[2,8,128,128]{3,2,1,0:T(8,128)(2,1)S(1)} %get-tuple-element.22.query_own, bf16[2,8,128,128]{3,2,1,0:T(8,128)(2,1)S(1)} %get-tuple-element.23.grad_own, ...), custom_call_target="tpu_custom_call" | custom-call | tf_op jit(solution)/shard_map/query_pass/pallas_call | solution.py:367
  87.1 0.6 collective-permute-start
  87.6 12.6 %share_totals.1 = (f32[2,8,8,1,128]{4,3,2,1,0:T(1,128)S(1)}, bf16[2,8,8,128,128]{4,3,2,1,0:T(8,128)(2,1)S(1)}, f32[16,128,128]{2,1,0:T(8,128)S(1)}, f32[16,128,128]{2,1,0:T(8,128)S(1)}) custom-call(f32[2,8,1,128]{3,2,1,0:T(1,128)S(1)} %get-tuple-element.32.lse_own, f32[2,8,8,1,128]{4,3,2,1,0:T(1,128)S(1)} %get-tuple-element.24.delta_all, ...), custom_call_target="tpu_custom_call" | custom-call | tf_op jit(solution)/shard_map/share_totals/pallas_call | solution.py:447
  100.2 4.4 %key_pass_sent.1 = bf16[2,8,128,128]{3,2,1,0:T(8,128)(2,1)S(1)} custom-call(s32[16,128]{1,0:T(8,128)S(1)} %get-tuple-element.31.refs_0_, bf16[2,8,8,128,128]{4,3,2,1,0:T(8,128)(2,1)S(1)} %get-tuple-element.25.key_all.refs_1_, bf16[2,8,8,128,128]{4,3,2,1,0:T(8,128)(2,1)S(1)} %get-tuple-element.26.value_all.refs_2_, f32[128,1,128]{2,1,0:T(1,128)S(1)} %bitcast.24, ...), custom_call_target="tpu_custom_call" | custom-call | flops 2000000000 | bytes 1048576 | tf_op jit(solution)/shard_map/key_pass_sent/pallas_call | solution.py:513
  104.6 1.2 %collective-permute-start.1 = (bf16[2,8,128,128]{3,2,1,0:T(8,128)(2,1)S(1)}, bf16[2,8,128,128]{3,2,1,0:T(8,128)(2,1)S(1)}, u32[]{:S(2)}, u32[]{:S(2)}) collective-permute-start(bf16[2,8,128,128]{3,2,1,0:T(8,128)(2,1)S(1)} %key_pass_sent.1), channel_id=1, source_target_pairs={{0,8},{1,9},{2,10},{3,11},{4,12},{5,13},{6,14},{7,15},{8,0},{9,1},... | collective-permute-start | bytes 1572872 | tf_op jit(solution)/shard_map/ppermute | solution.py:537
  105.8 4.4 %key_pass_kept.1 = bf16[2,8,128,128]{3,2,1,0:T(8,128)(2,1)S(1)} custom-call(s32[16,128]{1,0:T(8,128)S(1)} %get-tuple-element.31.refs_0_, bf16[2,8,8,128,128]{4,3,2,1,0:T(8,128)(2,1)S(1)} %get-tuple-element.25.key_all.refs_1_, bf16[2,8,8,128,128]{4,3,2,1,0:T(8,128)(2,1)S(1)} %get-tuple-element.26.value_all.refs_2_, f32[128,1,128]{2,1,0:T(1,128)S(1)} %bitcast.25, ...), custom_call_target="tpu_custom_call" | custom-call | flops 2000000000 | bytes 1048576 | tf_op jit(solution)/shard_map/key_pass_kept/pallas_call | solution.py:513
  110.2 0.0 collective-permute-done
  110.2 0.1 bitcast_select_fusion.1
  110.3 0.9 pad_maximum_fusion
  111.2 6.9 %collective-permute-done.1 = bf16[2,8,128,128]{3,2,1,0:T(8,128)(2,1)S(1)} collective-permute-done((bf16[2,8,128,128]{3,2,1,0:T(8,128)(2,1)S(1)}, bf16[2,8,128,128]{3,2,1,0:T(8,128)(2,1)S(1)}, u32[]{:S(2)}, u32[]{:S(2)}) %collective-permute-start.1) | collective-permute-done | bytes 524320 | tf_op jit(solution)/shard_map/ppermute | solution.py:537
  118.1 0.1 broadcast_select_fusion.1
  118.2 1.1 pad_maximum_fusion.1
  (1 shorter events, 0.0 us)
Async XLA Ops:
  87.1 23.2 %collective-permute-start = (bf16[8,128,128]{2,1,0:T(8,128)(2,1)S(1)}, bf16[8,128,128]{2,1,0:T(8,128)(2,1)S(1)}, u32[]{:S(2)}, u32[]{:S(2)}) collective-permute-start(bf16[8,128,128]{2,1,0:T(8,128)(2,1)S(1)} %get-tuple-element.46), channel_id=1, source_target_pairs={{0,8},{1,9},{2,10},{3,11},{4,12},{5,13},{6,14},{7,15},{8,0},{9,1},... | collective-permute-start | bytes 786440 | tf_op jit(solution)/shard_map/ppermute | solution.py:537
  104.6 13.5 %collective-permute-start.1 = (bf16[2,8,128,128]{3,2,1,0:T(8,128)(2,1)S(1)}, bf16[2,8,128,128]{3,2,1,0:T(8,128)(2,1)S(1)}, u32[]{:S(2)}, u32[]{:S(2)}) collective-permute-start(bf16[2,8,128,128]{3,2,1,0:T(8,128)(2,1)S(1)} %key_pass_sent.1), channel_id=1, source_target_pairs={{0,8},{1,9},{2,10},{3,11},{4,12},{5,13},{6,14},{7,15},{8,0},{9,1},... | collective-permute-start | bytes 1572872 | tf_op jit(solution)/shard_map/ppermute | solution.py:537

commit v5 on v4

--- a/solution.py
+++ b/solution.py
@@ -92,13 +92,15 @@
     rows = lax.broadcasted_iota(jnp.int32, (NBLK, ENTRIES), 0)
     lanes = lax.broadcasted_iota(jnp.int32, (NBLK, ENTRIES), 1)
     spread = jnp.where(lanes % NBLK == rows, 1.0, 0.0).astype(jnp.bfloat16)
+    apart = lax.broadcasted_iota(jnp.int32, (NBLK, NBLK, 2 * GROUP), 2)
     query_rows, key_rows = [], []
     for unit in range(2):
         distance = jnp.abs(order - order_ref[unit * GROUP + member])
         by_query = jnp.zeros((NBLK, ENTRIES), jnp.float32)
         by_key = jnp.zeros((NBLK, ENTRIES), jnp.float32)
         for d in range(1, REACH):
-            blocks = live_ref[d].astype(jnp.float32).astype(jnp.bfloat16)
+            blocks = jnp.sum(jnp.where(apart == d, live_ref[...], 0), axis=2)
+            blocks = blocks.astype(jnp.float32).astype(jnp.bfloat16)
             here = distance == d
             by_query = jnp.where(here, dot(blocks, spread), by_query)
             by_key = jnp.where(here, dot(blocks, spread, TN), by_key)
@@ -109,7 +111,7 @@
 
 
 def gather_kernel(order_src, live_src, out_src, key_src, value_src, query_src, grad_src, key_all, value_all, query_all,
-                  grad_all, delta_all, query_own, grad_own, peak, total, acc, by_query_ref, by_key_ref, delta_src, raw,
+                  grad_all, delta_all, query_own, grad_own, peak, total, acc, by_query_ref, by_key_ref, grad_half, delta_src, raw,
                   grad_raw, out_raw, order_ref, live_ref, send1, recv1, send2, recv2, send3, recv3, load):
     ring = Ring()
     head, half, member = ring.head, ring.half, ring.member
@@ -168,8 +170,9 @@
         own = bufs[a].at[:, member]
         arrived(own, recv1.at[a])
         if a != QUERY:
-            push(a, 0, own, ring.up, 0)
-            push(a, 1, own, ring.down, 1)
+            near = bufs[a].at[0, member] if a == GRAD else own
+            push(a, 0, near, ring.up, 0)
+            push(a, 1, near, ring.down, 1)
         push(a, 2, own, ring.twin, 4)
 
     def pass_raw(number, slot):
@@ -193,9 +196,12 @@
     spread(GRAD)
     fetch_grad = pltpu.make_async_copy(bufs[GRAD].at[:, member], grad_own, load.at[5])
     fetch_grad.start()
+    fetch_half = pltpu.make_async_copy(bufs[GRAD].at[1, member], grad_half, load.at[6])
+    fetch_half.start()
     spread(DELTA)
     fetch_query.wait()
     fetch_grad.wait()
+    fetch_half.wait()
 
     span = WIDE // BLK
     for unit in range(2):
@@ -209,8 +215,8 @@
             top = jnp.max(scores, axis=0, keepdims=True)
             probs = jnp.exp2(scores - top)
             summed = jnp.sum(probs, axis=0, keepdims=True)
-            terms = (probs * (dot(value, grad, NT) - delta)).astype(jnp.bfloat16)
-            partial = dot(key, terms, TN)
+            grads = dot(value, grad, NT) - delta
+            partial = dot(key, (probs * grads).astype(jnp.bfloat16), TN)
             for s in range(span):
                 lanes = slice(s * BLK, (s + 1) * BLK)
                 row = unit * NBLK + i + s
@@ -226,12 +232,12 @@
     arrived(bufs[QUERY].at[:, ring.up], recv1.at[6])
     push(QUERY, 6, bufs[QUERY].at[:, ring.up], ring.twin, 6)
     for a in (KEY, VALUE, GRAD, DELTA):
-        part = bufs[a].at[:, ring.down]
+        part = bufs[a].at[0, ring.down] if a == GRAD else bufs[a].at[:, ring.down]
         arrived(part, recv2.at[a, 0])
         if a != GRAD:
             push(a, 3, bufs[a].at[0, ring.down], ring.up, 2)
         push(a, 4, part, ring.twin, 5)
-        part = bufs[a].at[:, ring.up]
+        part = bufs[a].at[0, ring.up] if a == GRAD else bufs[a].at[:, ring.up]
         arrived(part, recv2.at[a, 1])
         if a != GRAD:
             push(a, 5, bufs[a].at[1, ring.up], ring.down, 3)
@@ -247,8 +253,8 @@
         push(a, 8, part, ring.twin, 8)
     for a in (KEY, VALUE, QUERY, GRAD, DELTA):
         arrived(bufs[a].at[:, ring.twin], recv2.at[a, 4])
-        arrived(bufs[a].at[:, ring.twin_down], recv2.at[a, 5])
-        arrived(bufs[a].at[:, ring.twin_up], recv2.at[a, 6])
+        for number, slot in ((5, ring.twin_down), (6, ring.twin_up)):
+            arrived(bufs[a].at[0, slot] if a == GRAD else bufs[a].at[:, slot], recv2.at[a, number])
         if a == QUERY:
             arrived(bufs[a].at[:, ring.twin_far], recv2.at[a, 7])
         elif a != GRAD:
@@ -265,7 +271,7 @@
 WHOLE = (2, GROUP, NBLK, BLK, HEAD_DIM)
 STATS = (2, GROUP, NBLK, 1, BLK)
 OWN = (2, NBLK, BLK, HEAD_DIM)
-LIMIT = 24 << 20
+LIMIT = 20 << 20
 
 
 def gather_all(order, live, key, value, query, grad, out):
@@ -285,23 +291,24 @@
             jax.ShapeDtypeStruct((ROWS, HEAD_DIM, BLK), full),
             jax.ShapeDtypeStruct((ROWS, ENTRIES), whole),
             jax.ShapeDtypeStruct((ROWS, ENTRIES), whole),
+            jax.ShapeDtypeStruct(OWN[1:], low),
         ),
         in_specs=[HBM] * 7,
-        out_specs=(VMEM, VMEM, VMEM, ANY) + (VMEM,) * 8,
+        out_specs=(VMEM, VMEM, VMEM, ANY) + (VMEM,) * 9,
         scratch_shapes=[
             pltpu.VMEM((HEADS, 1, BLK), full),
             pltpu.VMEM((3, BLK, HEADS * HEAD_DIM), low),
             pltpu.VMEM((BLK, HEADS * HEAD_DIM), low),
             pltpu.VMEM((BLK, HEADS * HEAD_DIM), low),
             pltpu.SMEM((2 * GROUP,), whole),
-            pltpu.VMEM((2 * GROUP, NBLK, NBLK), whole),
+            pltpu.VMEM((NBLK, NBLK, 2 * GROUP), whole),
             pltpu.SemaphoreType.DMA((8,)),
             pltpu.SemaphoreType.DMA((8,)),
             pltpu.SemaphoreType.DMA((5, 9)),
             pltpu.SemaphoreType.DMA((5, 9)),
             pltpu.SemaphoreType.DMA((4,)),
             pltpu.SemaphoreType.DMA((4,)),
-            pltpu.SemaphoreType.DMA((6,)),
+            pltpu.SemaphoreType.DMA((7,)),
         ],
         compiler_params=pltpu.CompilerParams(collective_id=0, has_side_effects=True, vmem_limit_bytes=LIMIT),
         name="gather_all",
@@ -315,7 +322,7 @@
     return (most + CHUNK - 1) // CHUNK
 
 
-def query_kernel(table, query_own, grad_own, delta_all, key_ref, value_ref, peak_in, total_in, acc_in, dq_ref, lse_ref,
+def query_kernel(table, query_own, grad_own, delta_all, key_ref, value_ref, peak_in, total_in, acc_in, kept_ref, sent_ref, lse_ref,
                  peak, total, acc):
     member = place()[2]
     peak[...] = peak_in[...]
@@ -353,10 +360,15 @@
         return carry
 
     lax.fori_loop(0, turns(table, range(ROWS)), step, 0)
-    for row in range(ROWS):
-        unit, i = row // NBLK, row % NBLK
-        lse_ref[unit, i] = peak[row] + jnp.log2(total[row])
-        dq_ref[unit, i] = (acc[row] * (SCALE / total[row])).T.astype(jnp.bfloat16)
+    first = place()[1] == 0
+    for i in range(NBLK):
+        done = []
+        for unit in range(2):
+            row = unit * NBLK + i
+            lse_ref[unit, i] = peak[row] + jnp.log2(total[row])
+            done.append((acc[row] * (SCALE / total[row])).T.astype(jnp.bfloat16))
+        kept_ref[i] = jnp.where(first, done[0], done[1])
+        sent_ref[i] = jnp.where(first, done[1], done[0])
 
 
 def flat(array):
@@ -366,20 +378,44 @@
 def query_pass(table, query_own, grad_own, delta, key, value, peak, total, acc):
     return pl.pallas_call(
         query_kernel,
-        out_shape=(jax.ShapeDtypeStruct(OWN, jnp.bfloat16), jax.ShapeDtypeStruct((2, NBLK, 1, BLK), jnp.float32)),
+        out_shape=(
+            jax.ShapeDtypeStruct(OWN[1:], jnp.bfloat16),
+            jax.ShapeDtypeStruct(OWN[1:], jnp.bfloat16),
+            jax.ShapeDtypeStruct((2, NBLK, 1, BLK), jnp.float32),
+        ),
         in_specs=[SMEM] + [VMEM] * 8,
-        out_specs=(VMEM, VMEM),
+        out_specs=(VMEM,) * 3,
         scratch_shapes=[
             pltpu.VMEM((ROWS, 1, BLK), jnp.float32),
             pltpu.VMEM((ROWS, 1, BLK), jnp.float32),
             pltpu.VMEM((ROWS, HEAD_DIM, BLK), jnp.float32),
         ],
         compiler_params=pltpu.CompilerParams(vmem_limit_bytes=LIMIT),
+        cost_estimate=pl.CostEstimate(flops=4_000_000_000, bytes_accessed=8 << 20, transcendentals=1 << 21),
         name="query_pass",
     )(table, query_own, grad_own, delta, flat(key), flat(value), peak, total, acc)
 
 
-def share_kernel(lse_own, delta_all, query_own, grad_own, key_all, value_all, grad_part, lse_all, grad_all,
+def diagonal(unit, member, query_own, grad_own, key_all, value_all, delta_at, lse_at, key_acc, value_acc):
+    query = query_own[unit].reshape(NBLK * BLK, HEAD_DIM)
+    grad = grad_own[unit].reshape(NBLK * BLK, HEAD_DIM)
+    delta = jnp.concatenate([delta_at(unit, i) for i in range(NBLK)], axis=1)
+    lse = jnp.concatenate([lse_at(unit, i) for i in range(NBLK)], axis=1)
+    span = WIDE // BLK
+    for u in range(0, NBLK, span):
+        key = key_all[unit, member, u : u + span].reshape(WIDE, HEAD_DIM)
+        value = value_all[unit, member, u : u + span].reshape(WIDE, HEAD_DIM)
+        probs = jnp.exp2(dot(key, query, NT) * SCALE2 - lse)
+        terms = (probs * (dot(value, grad, NT) - delta)).astype(jnp.bfloat16)
+        value_part = dot(probs.astype(jnp.bfloat16), grad)
+        key_part = dot(terms, query)
+        for s in range(span):
+            rows = slice(s * BLK, (s + 1) * BLK)
+            value_acc[u + s] = value_part[rows]
+            key_acc[u + s] = key_part[rows]
+
+
+def share_kernel(lse_own, delta_all, query_own, grad_own, key_all, value_all, from_down, from_up, grad_part, lse_all, grad_all,
                  key_acc, value_acc, send, recv, send2, recv2, load):
     ring = Ring()
     member = ring.member
@@ -393,93 +429,85 @@
     for step in range(1, GROUP):
         device = ring.device((member + step) % GROUP)
         pending.append(remote(lse_own, lse_all.at[:, member], send.at[step], recv.at[step], device))
-    mine = pltpu.make_async_copy(lse_own, lse_all.at[:, member], load.at[6])
-    mine.start()
-    pending.append(
-        remote(grad_part.at[0, ring.down], grad_all.at[0, ring.down], send2.at[0], recv2.at[0], ring.device(ring.up))
-    )
-    pending.append(
-        remote(grad_part.at[1, ring.up], grad_all.at[1, ring.up], send2.at[1], recv2.at[1], ring.device(ring.down))
-    )
-    held = (ring.member, ring.up, ring.down, ring.twin, ring.twin_up, ring.twin_down)
-    loads = []
-    for n, slot in enumerate(held):
-        loads.append(pltpu.make_async_copy(grad_part.at[:, slot], grad_all.at[:, slot], load.at[n]))
-        loads[-1].start()
-
-    def relay(n):
-        part = grad_all.at[n, ring.far]
-        arrived(part, recv2.at[n])
-        pending.append(remote(part, part, send2.at[2 + n], recv2.at[2 + n], ring.device(ring.twin)))
-
-    for unit in range(2):
-        query = query_own[unit].reshape(NBLK * BLK, HEAD_DIM)
-        grad = grad_own[unit].reshape(NBLK * BLK, HEAD_DIM)
-        delta = jnp.concatenate([delta_all[unit, member, i] for i in range(NBLK)], axis=1)
-        lse = jnp.concatenate([lse_own[unit, i] for i in range(NBLK)], axis=1)
-        span = WIDE // BLK
-        for u in range(0, NBLK, span):
-            key = key_all[unit, member, u : u + span].reshape(WIDE, HEAD_DIM)
-            value = value_all[unit, member, u : u + span].reshape(WIDE, HEAD_DIM)
-            probs = jnp.exp2(dot(key, query, NT) * SCALE2 - lse)
-            terms = (probs * (dot(value, grad, NT) - delta)).astype(jnp.bfloat16)
-            value_part = dot(probs.astype(jnp.bfloat16), grad)
-            key_part = dot(terms, query)
-            for s in range(span):
-                rows = slice(s * BLK, (s + 1) * BLK)
-                value_acc[unit * NBLK + u + s] = value_part[rows]
-                key_acc[unit * NBLK + u + s] = key_part[rows]
-
-    relay(0)
-    relay(1)
-    mine.wait()
+
+    def push(number, part, target, slot):
+        pending.append(remote(part, target, send2.at[number], recv2.at[number], ring.device(slot)))
+
+    push(0, grad_part.at[0, ring.down], grad_all.at[0, ring.down], ring.up)
+    push(1, from_up, grad_all.at[1, ring.up], ring.down)
+    push(2, from_down, grad_all.at[1, ring.down], ring.twin)
+    push(3, from_up, grad_all.at[1, ring.up], ring.twin)
+    held = [(lse_own, lse_all.at[:, member]), (from_down, grad_all.at[1, ring.down]), (from_up, grad_all.at[1, ring.up])]
+    for slot in (ring.member, ring.twin):
+        held.append((grad_part.at[:, slot], grad_all.at[:, slot]))
+    for slot in (ring.down, ring.up, ring.twin_down, ring.twin_up):
+        held.append((grad_part.at[0, slot], grad_all.at[0, slot]))
+    loads = [pltpu.make_async_copy(part, target, load.at[n]) for n, (part, target) in enumerate(held)]
+    for copy in loads:
+        copy.start()
+
+    diagonal(1 - ring.half, member, query_own, grad_own, key_all, value_all,
+             lambda unit, i: delta_all[unit, member, i], lambda unit, i: lse_own[unit, i], key_acc, value_acc)
+
+    far = (grad_all.at[0, ring.far], grad_all.at[1, ring.far])
+    for n in range(2):
+        arrived(far[n], recv2.at[n])
+        push(4 + n, far[n], far[n], ring.twin)
     for copy in loads:
         copy.wait()
     for step in range(1, GROUP):
         arrived(lse_own, recv.at[step])
-    arrived(grad_all.at[0, ring.twin_far], recv2.at[2])
-    arrived(grad_all.at[1, ring.twin_far], recv2.at[3])
+    arrived(grad_all.at[1, ring.twin_down], recv2.at[2])
+    arrived(grad_all.at[1, ring.twin_up], recv2.at[3])
+    arrived(grad_all.at[0, ring.twin_far], recv2.at[4])
+    arrived(grad_all.at[1, ring.twin_far], recv2.at[5])
     for copy in pending:
         copy.wait_send()
 
 
-def share_totals(lse_own, delta, query_own, grad_own, key, value, grad):
+def share_totals(lse_own, delta, query_own, grad_own, key, value, from_down, from_up, grad):
     return pl.pallas_call(
         share_kernel,
         out_shape=(
             jax.ShapeDtypeStruct(STATS, jnp.float32),
             jax.ShapeDtypeStruct(WHOLE, jnp.bfloat16),
-            jax.ShapeDtypeStruct((ROWS, BLK, HEAD_DIM), jnp.float32),
-            jax.ShapeDtypeStruct((ROWS, BLK, HEAD_DIM), jnp.float32),
+            jax.ShapeDtypeStruct((NBLK, BLK, HEAD_DIM), jnp.float32),
+            jax.ShapeDtypeStruct((NBLK, BLK, HEAD_DIM), jnp.float32),
         ),
-        in_specs=[VMEM] * 6 + [ANY],
+        in_specs=[VMEM] * 8 + [ANY],
         out_specs=(VMEM,) * 4,
         scratch_shapes=[
             pltpu.SemaphoreType.DMA((GROUP,)),
             pltpu.SemaphoreType.DMA((GROUP,)),
-            pltpu.SemaphoreType.DMA((4,)),
-            pltpu.SemaphoreType.DMA((4,)),
-            pltpu.SemaphoreType.DMA((7,)),
+            pltpu.SemaphoreType.DMA((6,)),
+            pltpu.SemaphoreType.DMA((6,)),
+            pltpu.SemaphoreType.DMA((9,)),
         ],
         compiler_params=pltpu.CompilerParams(collective_id=1, has_side_effects=True, vmem_limit_bytes=LIMIT),
         name="share_totals",
-    )(lse_own, delta, query_own, grad_own, key, value, grad)
-
-
-def key_kernel(other, table, key_all, value_all, delta_ref, lse_ref, query_ref, grad_ref, key_in, value_in, out_ref,
+    )(lse_own, delta, query_own, grad_own, key, value, from_down, from_up, grad)
+
+
+def key_kernel(blocks, table, key_all, value_all, delta_ref, lse_ref, query_ref, grad_ref, first_in, second_in, out_ref,
                key_acc, value_acc):
     _, half, member = place()
+    other = len(blocks) < NBLK
     unit = 1 - half if other else half
     base = unit * NBLK
-    for u in range(NBLK):
-        key_acc[u] = key_in[base + u]
-        value_acc[u] = value_in[base + u]
+    if other:
+        for u in blocks:
+            key_acc[u] = first_in[u]
+            value_acc[u] = second_in[u]
+    else:
+        own = (unit * GROUP + member) * NBLK
+        diagonal(unit, member, first_in, second_in, key_all, value_all,
+                 lambda unit, i: delta_ref[own + i], lambda unit, i: lse_ref[own + i], key_acc, value_acc)
 
     def step(turn, carry):
-        for first in range(0, NBLK, PAIR):
-            blocks = range(first, first + PAIR)
+        for first in blocks[::PAIR]:
+            pair = range(first, first + PAIR)
             loads, results = [], []
-            for u in blocks:
+            for u in pair:
                 row = base + u
                 slots = [turn * CHUNK + c for c in range(CHUNK)]
                 entries = [table[row, slot] for slot in slots]
@@ -495,24 +523,24 @@
                 probs = jnp.exp2(scores * SCALE2 - lse)
                 terms = (probs * (grads - delta)).astype(jnp.bfloat16)
                 results.append((dot(probs.astype(jnp.bfloat16), grad), dot(terms, query)))
-            for n, u in enumerate(blocks):
+            for n, u in enumerate(pair):
                 value_acc[u] += results[n][0]
                 key_acc[u] += results[n][1]
         return carry
 
-    lax.fori_loop(0, turns(table, [base + u for u in range(NBLK)]), step, 0)
-    for u in range(NBLK):
-        out_ref[0, u] = (key_acc[u] * SCALE).astype(jnp.bfloat16)
-        out_ref[1, u] = value_acc[u].astype(jnp.bfloat16)
-
-
-def key_pass(other, table, key, value, delta, lse, query, grad, key_acc, value_acc):
+    lax.fori_loop(0, turns(table, [base + u for u in blocks]), step, 0)
+    for n, u in enumerate(blocks):
+        out_ref[0, n] = (key_acc[u] * SCALE).astype(jnp.bfloat16)
+        out_ref[1, n] = value_acc[u].astype(jnp.bfloat16)
+
+
+def key_pass(blocks, table, key, value, delta, lse, query, grad, first, second):
     def kernel(*refs):
-        key_kernel(other, *refs)
+        key_kernel(blocks, *refs)
 
     return pl.pallas_call(
         kernel,
-        out_shape=jax.ShapeDtypeStruct(OWN, jnp.bfloat16),
+        out_shape=jax.ShapeDtypeStruct((2, len(blocks), BLK, HEAD_DIM), jnp.bfloat16),
         in_specs=[SMEM] + [VMEM] * 8,
         out_specs=VMEM,
         scratch_shapes=[
@@ -521,16 +549,20 @@
         ],
         compiler_params=pltpu.CompilerParams(vmem_limit_bytes=LIMIT),
         cost_estimate=pl.CostEstimate(flops=2_000_000_000, bytes_accessed=1 << 20, transcendentals=1 << 20),
-        name="key_pass_sent" if other else "key_pass_kept",
-    )(table, key, value, flat(delta), flat(lse), flat(query), flat(grad), key_acc, value_acc)
+        name="key_pass",
+    )(table, key, value, flat(delta), flat(lse), flat(query), flat(grad), first, second)
 
 
 def local(queries, key_states, value_states, attn_out, grad_out, frame_order, block_live):
-    half = place()[1]
-    (key, value, query, grad, delta, query_own, grad_own, peak, total, acc, by_query, by_key) = gather_all(
-        frame_order, block_live, key_states, value_states, queries, grad_out, attn_out
+    first = lax.axis_index("frame") < GROUP
+    frame_order, first = lax.optimization_barrier((frame_order, first))
+    (key, value, query, grad, delta, query_own, grad_own, peak, total, acc, by_query, by_key, grad_half) = gather_all(
+        frame_order, block_live.transpose(1, 2, 0), key_states, value_states, queries, grad_out, attn_out
     )
-    dq, lse_own = query_pass(by_query, query_own, grad_own, delta, key, value, peak, total, acc)
+    round_up = [(source, source // GROUP * GROUP + (source + 2) % GROUP) for source in range(2 * GROUP)]
+    from_down = lax.ppermute(grad_half, "frame", round_up)
+    from_up = lax.ppermute(grad_half, "frame", [(target, source) for source, target in round_up])
+    dq_kept, dq_sent, lse_own = query_pass(by_query, query_own, grad_own, delta, key, value, peak, total, acc)
     swap = [(source, (source + GROUP) % (2 * GROUP)) for source in range(2 * GROUP)]
 
     def across(sent):
@@ -538,14 +570,20 @@
 
     def join(kept, came):
         kept, came = kept.reshape(NBLK * BLK, HEAD_DIM), came.reshape(NBLK * BLK, HEAD_DIM)
-        return jnp.concatenate([jnp.where(half == 0, kept, came), jnp.where(half == 0, came, kept)], axis=1)
-
-    dq_came = across(jnp.where(half == 0, dq[1], dq[0]))
-    lse, grad, key_acc, value_acc = share_totals(lse_own, delta, query_own, grad_own, key, value, grad)
-    sums = (by_key, key, value, delta, lse, query, grad, key_acc, value_acc)
-    came = across(key_pass(True, *sums))
-    kept = key_pass(False, *sums)
-    return join(jnp.where(half == 0, dq[0], dq[1]), dq_came), join(kept[0], came[0]), join(kept[1], came[1])
+        return jnp.concatenate([jnp.where(first, kept, came), jnp.where(first, came, kept)], axis=1)
+
+    dq_came = across(dq_sent)
+    lse, grad, key_acc, value_acc = share_totals(
+        lse_own, delta, query_own, grad_own, key, value, from_down, from_up, grad
+    )
+    gathered = (by_key, key, value, delta, lse, query, grad)
+    middle = NBLK // 2
+    came = [
+        across(key_pass(blocks, *gathered, key_acc, value_acc)) for blocks in (range(middle), range(middle, NBLK))
+    ]
+    came = jnp.concatenate(came, axis=1)
+    kept = key_pass(range(NBLK), *gathered, query_own, grad_own)
+    return join(dq_kept, dq_came), join(kept[0], came[0]), join(kept[1], came[1])
 
 
 def solution(mesh):

time: 119 us -> 114 us (0.958)
  waiting for transfers between devices: 6.93 us -> 2.94 us
  starting transfers between devices: 1.8 us -> 3.73 us
  local copies, waits for them, and re-layouts: 1.47 us -> 0.05 us
    pallas_call x1, Pallas kernels: 76.2 us -> 70.8 us  [gather_all(): pl.pallas_call(gather_kernel, out_shape=(jax.ShapeDtypeStruct(WHOLE, low)...]
    ppermute x2 -> x3, waiting for transfers between devices: 6.93 us -> 2.94 us  [across(): return lax.ppermute(sent, 'frame', swap)]
    pallas_call x3 -> x4, Pallas kernels: 17.4 us -> 20.7 us  [the longest x3 12.1 us: key_pass(): pl.pallas_call(kernel, out_shape=jax.ShapeDtypeStruct((2, len(blocks), BL...]
    ppermute x0 -> x2, starting transfers between devices: none -> 1.53 us  [the longest x1 1 us: local(): from_down = lax.ppermute(grad_half, 'frame', round_up)]
    unnamed x1, local copies, waits for them, and re-layouts: 1.47 us -> 0.02 us
  transfers between devices with their start and end apart: 2 -> 5, of which waited for: 1 -> 1; matrix products, arithmetic and copies ran while one was open for 1% -> 0% of each run, Pallas kernels for 18% -> 30%
where the time goes in v5:
time: 114 us
  Pallas kernels  105 us (92%)
  starting transfers between devices  3.73 us (3%)
  waiting for transfers between devices  2.94 us (3%)
  other arithmetic  2.04 us (2%)
    pallas_call x1, Pallas kernels, gather_all(): pl.pallas_call(gather_kernel, out_shape=(jax.ShapeDtypeStruct(WHOLE, low)...  70.8 us
    pallas_call x1, Pallas kernels, share_totals(): pl.pallas_call(share_kernel, out_shape=(jax.ShapeDtypeStruct(STATS, jnp.f...  13.2 us
    pallas_call x3, Pallas kernels, key_pass(): pl.pallas_call(kernel, out_shape=jax.ShapeDtypeStruct((2, len(blocks), BL...  12.1 us
    pallas_call x1, Pallas kernels, query_pass(): pl.pallas_call(query_kernel, out_shape=(jax.ShapeDtypeStruct(OWN[1:], jnp...  8.68 us
    ppermute x3, waiting for transfers between devices, across(): return lax.ppermute(sent, 'frame', swap)  2.94 us
  transfers between devices with their start and end apart: 5, of which 1 were waited for; matrix products, arithmetic and copies ran while one was open for 0% of the time, Pallas kernels for 30%

profile of v5, /device:TPU:1, one launch (start us, length us, event | category | flops | bytes accessed | tf_op | source)
XLA Modules:
  0.0 114.2 jit_solution(3431149997171914751)
XLA Ops:
  0.6 70.8 %gather_all.1 = (bf16[2,8,8,128,128]{4,3,2,1,0:T(8,128)(2,1)S(1)}, bf16[2,8,8,128,128]{4,3,2,1,0:T(8,128)(2,1)S(1)}, bf16[2,8,8,128,128]{4,3,2,1,0:T(8,128)(2,1)...) custom-call(s32[16]{0:T(128)} %order_src, ...), custom_call_target="tpu_custom_call" | custom-call | tf_op jit(solution)/shard_map/gather_all/pallas_call | solution.py:279
  71.4 0.5 collective-permute-start.2
  71.9 1.0 collective-permute-start.1
  72.9 8.7 %query_pass.1 = (bf16[8,128,128]{2,1,0:T(8,128)(2,1)S(1)}, bf16[8,128,128]{2,1,0:T(8,128)(2,1)S(1)}, f32[2,8,1,128]{3,2,1,0:T(1,128)S(1)}) custom-call(s32[16,128]{1,0:T(8,128)S(1)} %get-tuple-element.27.table, bf16[2,8,128,128]{3,2,1,0:T(8,128)(2,1)S(1)} %get-tuple-element.28.query_own.refs_7_, ...), custom_call_target="tpu_custom_call" | custom-call | flops 4000000000 | bytes 8388608 | tf_op jit(solution)/shard_map/query_pass/pallas_call | solution.py:379
  81.6 0.6 collective-permute-start
  82.2 0.0 collective-permute-done.2.from_up
  82.2 0.0 collective-permute-done.1.from_down
  82.2 13.2 %share_totals.1 = (f32[2,8,8,1,128]{4,3,2,1,0:T(1,128)S(1)}, bf16[2,8,8,128,128]{4,3,2,1,0:T(8,128)(2,1)S(1)}, f32[8,128,128]{2,1,0:T(8,128)S(1)}, f32[8,128,128]{2,1,0:T(8,128)S(1)}) custom-call(f32[2,8,1,128]{3,2,1,0:T(1,128)S(1)} %get-tuple-element.39.lse_own, f32[2,8,8,1,128]{4,3,2,1,0:T(1,128)S(1)} %get-tuple-element.30.delta_all, ...), custom_call_target="tpu_custom_call" | custom-call | tf_op jit(solution)/shard_map/share_totals/pallas_call | solution.py:469
  95.4 2.7 %key_pass.4 = bf16[2,4,128,128]{3,2,1,0:T(8,128)(2,1)S(1)} custom-call(s32[16,128]{1,0:T(8,128)S(1)} %get-tuple-element.38.refs_0_, bf16[2,8,8,128,128]{4,3,2,1,0:T(8,128)(2,1)S(1)} %get-tuple-element.31.key_all.refs_1_, bf16[2,8,8,128,128]{4,3,2,1,0:T(8,128)(2,1)S(1)} %get-tuple-element.32.value_all.refs_2_, f32[128,1,128]{2,1,0:T(1,128)S(1)} %bitcast.21, ...), custom_call_target="tpu_custom_call" | custom-call | flops 2000000000 | bytes 1048576 | tf_op jit(solution)/shard_map/key_pass/pallas_call | solution.py:541
  98.2 1.3 %collective-permute-start.3 = (bf16[2,4,128,128]{3,2,1,0:T(8,128)(2,1)S(1)}, bf16[2,4,128,128]{3,2,1,0:T(8,128)(2,1)S(1)}, u32[]{:S(2)}, u32[]{:S(2)}) collective-permute-start(bf16[2,4,128,128]{3,2,1,0:T(8,128)(2,1)S(1)} %key_pass.4), channel_id=1, source_target_pairs={{0,8},{1,9},{2,10},{3,11},{4,12},{5,13},{6,14},{7,15},{8,0},{9,1},... | collective-permute-start | bytes 786440 | tf_op jit(solution)/shard_map/ppermute | solution.py:569
  99.4 2.7 %key_pass.5 = bf16[2,4,128,128]{3,2,1,0:T(8,128)(2,1)S(1)} custom-call(s32[16,128]{1,0:T(8,128)S(1)} %get-tuple-element.38.refs_0_, bf16[2,8,8,128,128]{4,3,2,1,0:T(8,128)(2,1)S(1)} %get-tuple-element.31.key_all.refs_1_, bf16[2,8,8,128,128]{4,3,2,1,0:T(8,128)(2,1)S(1)} %get-tuple-element.32.value_all.refs_2_, f32[128,1,128]{2,1,0:T(1,128)S(1)} %bitcast.22, ...), custom_call_target="tpu_custom_call" | custom-call | flops 2000000000 | bytes 1048576 | tf_op jit(solution)/shard_map/key_pass/pallas_call | solution.py:541
  102.1 0.3 collective-permute-start.4
  102.5 0.0 collective-permute-done
  102.5 6.6 %key_pass.3 = bf16[2,8,128,128]{3,2,1,0:T(8,128)(2,1)S(1)} custom-call(s32[16,128]{1,0:T(8,128)S(1)} %get-tuple-element.38.refs_0_, bf16[2,8,8,128,128]{4,3,2,1,0:T(8,128)(2,1)S(1)} %get-tuple-element.31.key_all.refs_1_, bf16[2,8,8,128,128]{4,3,2,1,0:T(8,128)(2,1)S(1)} %get-tuple-element.32.value_all.refs_2_, f32[128,1,128]{2,1,0:T(1,128)S(1)} %bitcast.23, ...), custom_call_target="tpu_custom_call" | custom-call | flops 2000000000 | bytes 1048576 | tf_op jit(solution)/shard_map/key_pass/pallas_call | solution.py:541
  109.2 0.0 collective-permute-done.3
  109.2 2.9 %collective-permute-done.4 = bf16[2,4,128,128]{3,2,1,0:T(8,128)(2,1)S(1)} collective-permute-done((bf16[2,4,128,128]{3,2,1,0:T(8,128)(2,1)S(1)}, bf16[2,4,128,128]{3,2,1,0:T(8,128)(2,1)S(1)}, u32[]{:S(2)}, u32[]{:S(2)}) %collective-permute-start.4) | collective-permute-done | bytes 262176 | tf_op jit(solution)/shard_map/ppermute | solution.py:569
  112.2 0.1 broadcast_select_fusion.1
  112.3 0.9 pad_maximum_fusion.2
  113.1 1.1 pad_maximum_fusion
  (3 shorter events, 0.1 us)
Async XLA Ops:
  71.4 10.8 %collective-permute-start.2 = (bf16[8,128,128]{2,1,0:T(8,128)(2,1)S(1)}, bf16[8,128,128]{2,1,0:T(8,128)(2,1)S(1)}, u32[]{:S(2)}, u32[]{:S(2)}) collective-permute-start(bf16[8,128,128]{2,1,0:T(8,128)(2,1)S(1)} %get-tuple-element.40), channel_id=1, source_target_pairs={{2,0},{3,1},{4,2},{5,3},{6,4},{7,5},{0,6},{1,7},{10,8},{11,9},{12,... | collective-permute-start | bytes 786440 | tf_op jit(solution)/shard_map/ppermute | solution.py:564
  71.9 10.3 %collective-permute-start.1 = (bf16[8,128,128]{2,1,0:T(8,128)(2,1)S(1)}, bf16[8,128,128]{2,1,0:T(8,128)(2,1)S(1)}, u32[]{:S(2)}, u32[]{:S(2)}) collective-permute-start(bf16[8,128,128]{2,1,0:T(8,128)(2,1)S(1)} %get-tuple-element.40), channel_id=1, source_target_pairs={{0,2},{1,3},{2,4},{3,5},{4,6},{5,7},{6,0},{7,1},{8,10},{9,11},{10,... | collective-permute-start | bytes 786440 | tf_op jit(solution)/shard_map/ppermute | solution.py:563
  81.6 20.9 %collective-permute-start = (bf16[8,128,128]{2,1,0:T(8,128)(2,1)S(1)}, bf16[8,128,128]{2,1,0:T(8,128)(2,1)S(1)}, u32[]{:S(2)}, u32[]{:S(2)}) collective-permute-start(bf16[8,128,128]{2,1,0:T(8,128)(2,1)S(1)} %get-tuple-element.37), channel_id=1, source_target_pairs={{0,8},{1,9},{2,10},{3,11},{4,12},{5,13},{6,14},{7,15},{8,0},{9,1},... | collective-permute-start | bytes 786440 | tf_op jit(solution)/shard_map/ppermute | solution.py:569
  98.2 11.0 %collective-permute-start.3 = (bf16[2,4,128,128]{3,2,1,0:T(8,128)(2,1)S(1)}, bf16[2,4,128,128]{3,2,1,0:T(8,128)(2,1)S(1)}, u32[]{:S(2)}, u32[]{:S(2)}) collective-permute-start(bf16[2,4,128,128]{3,2,1,0:T(8,128)(2,1)S(1)} %key_pass.4), channel_id=1, source_target_pairs={{0,8},{1,9},{2,10},{3,11},{4,12},{5,13},{6,14},{7,15},{8,0},{9,1},... | collective-permute-start | bytes 786440 | tf_op jit(solution)/shard_map/ppermute | solution.py:569
  102.1 10.0 %collective-permute-start.4 = (bf16[2,4,128,128]{3,2,1,0:T(8,128)(2,1)S(1)}, bf16[2,4,128,128]{3,2,1,0:T(8,128)(2,1)S(1)}, u32[]{:S(2)}, u32[]{:S(2)}) collective-permute-start(bf16[2,4,128,128]{3,2,1,0:T(8,128)(2,1)S(1)} %key_pass.5), channel_id=1, source_target_pairs={{0,8},{1,9},{2,10},{3,11},{4,12},{5,13},{6,14},{7,15},{8,0},{9,1},... | collective-permute-start | bytes 786440 | tf_op jit(solution)/shard_map/ppermute | solution.py:569

commit v6 on v5

--- a/solution.py
+++ b/solution.py
@@ -21,7 +21,7 @@
 SLOTS = 2 * (REACH - 1) * NBLK
 COUNT_AT = BLK - 1
 CHUNK = 5
-PAIR = 2
+PAIR = 4
 WIDE = 512
 FAR = 1e30
 MESH = pl.DeviceIdType.MESH
@@ -426,9 +426,6 @@
         pl.semaphore_signal(barrier, inc=1, device_id=ring.device(slot), device_id_type=MESH)
     pl.semaphore_wait(barrier, GROUP - 1)
     pending = []
-    for step in range(1, GROUP):
-        device = ring.device((member + step) % GROUP)
-        pending.append(remote(lse_own, lse_all.at[:, member], send.at[step], recv.at[step], device))
 
     def push(number, part, target, slot):
         pending.append(remote(part, target, send2.at[number], recv2.at[number], ring.device(slot)))
@@ -437,6 +434,11 @@
     push(1, from_up, grad_all.at[1, ring.up], ring.down)
     push(2, from_down, grad_all.at[1, ring.down], ring.twin)
     push(3, from_up, grad_all.at[1, ring.up], ring.twin)
+    for step in range(1, GROUP):
+        device = ring.device((member + step) % GROUP)
+        pending.append(remote(lse_own, lse_all.at[:, member], send.at[step], recv.at[step], device))
+
+
     held = [(lse_own, lse_all.at[:, member]), (from_down, grad_all.at[1, ring.down]), (from_up, grad_all.at[1, ring.up])]
     for slot in (ring.member, ring.twin):
         held.append((grad_part.at[:, slot], grad_all.at[:, slot]))

time: 114 us -> 112 us (0.982)
  Pallas kernels: 105 us -> 103 us
  transfers between devices with their start and end apart: 5 -> 5, of which waited for: 1 -> 1; matrix products, arithmetic and copies ran while one was open for 0% -> 0% of each run, Pallas kernels for 30% -> 29%
where the time goes in v6:
time: 112 us
  Pallas kernels  103 us (92%)
  starting transfers between devices  3.75 us (3%)
  waiting for transfers between devices  2.42 us (2%)
  other arithmetic  2.04 us (2%)
    pallas_call x1, Pallas kernels, gather_all(): pl.pallas_call(gather_kernel, out_shape=(jax.ShapeDtypeStruct(WHOLE, low)...  70.8 us
    pallas_call x1, Pallas kernels, share_totals(): pl.pallas_call(share_kernel, out_shape=(jax.ShapeDtypeStruct(STATS, jnp.f...  12.7 us
    pallas_call x3, Pallas kernels, key_pass(): pl.pallas_call(kernel, out_shape=jax.ShapeDtypeStruct((2, len(blocks), BL...  12.1 us
    pallas_call x1, Pallas kernels, query_pass(): pl.pallas_call(query_kernel, out_shape=(jax.ShapeDtypeStruct(OWN[1:], jnp...  7.77 us
    ppermute x3, waiting for transfers between devices, across(): return lax.ppermute(sent, 'frame', swap)  2.42 us
  transfers between devices with their start and end apart: 5, of which 1 were waited for; matrix products, arithmetic and copies ran while one was open for 0% of the time, Pallas kernels for 29%

profile of v6, /device:TPU:1, one launch (start us, length us, event | category | flops | bytes accessed | tf_op | source)
XLA Modules:
  0.0 112.4 jit_solution(15614035732885298938)
XLA Ops:
  0.6 70.8 %gather_all.1 = (bf16[2,8,8,128,128]{4,3,2,1,0:T(8,128)(2,1)S(1)}, bf16[2,8,8,128,128]{4,3,2,1,0:T(8,128)(2,1)S(1)}, bf16[2,8,8,128,128]{4,3,2,1,0:T(8,128)(2,1)...) custom-call(s32[16]{0:T(128)} %order_src, ...), custom_call_target="tpu_custom_call" | custom-call | tf_op jit(solution)/shard_map/gather_all/pallas_call | solution.py:279
  71.4 0.5 collective-permute-start.2
  71.9 1.0 collective-permute-start.1
  72.9 7.8 %query_pass.1 = (bf16[8,128,128]{2,1,0:T(8,128)(2,1)S(1)}, bf16[8,128,128]{2,1,0:T(8,128)(2,1)S(1)}, f32[2,8,1,128]{3,2,1,0:T(1,128)S(1)}) custom-call(s32[16,128]{1,0:T(8,128)S(1)} %get-tuple-element.27.table, bf16[2,8,128,128]{3,2,1,0:T(8,128)(2,1)S(1)} %get-tuple-element.28.query_own.refs_7_, ...), custom_call_target="tpu_custom_call" | custom-call | flops 4000000000 | bytes 8388608 | tf_op jit(solution)/shard_map/query_pass/pallas_call | solution.py:379
  80.7 0.6 collective-permute-start
  81.3 0.0 collective-permute-done.2.from_up
  81.3 0.0 collective-permute-done.1.from_down
  81.3 12.7 %share_totals.1 = (f32[2,8,8,1,128]{4,3,2,1,0:T(1,128)S(1)}, bf16[2,8,8,128,128]{4,3,2,1,0:T(8,128)(2,1)S(1)}, f32[8,128,128]{2,1,0:T(8,128)S(1)}, f32[8,128,128]{2,1,0:T(8,128)S(1)}) custom-call(f32[2,8,1,128]{3,2,1,0:T(1,128)S(1)} %get-tuple-element.39.lse_own, f32[2,8,8,1,128]{4,3,2,1,0:T(1,128)S(1)} %get-tuple-element.30.delta_all, ...), custom_call_target="tpu_custom_call" | custom-call | tf_op jit(solution)/shard_map/share_totals/pallas_call | solution.py:471
  94.0 2.7 %key_pass.4 = bf16[2,4,128,128]{3,2,1,0:T(8,128)(2,1)S(1)} custom-call(s32[16,128]{1,0:T(8,128)S(1)} %get-tuple-element.38.refs_0_, bf16[2,8,8,128,128]{4,3,2,1,0:T(8,128)(2,1)S(1)} %get-tuple-element.31.key_all.refs_1_, bf16[2,8,8,128,128]{4,3,2,1,0:T(8,128)(2,1)S(1)} %get-tuple-element.32.value_all.refs_2_, f32[128,1,128]{2,1,0:T(1,128)S(1)} %bitcast.21, ...), custom_call_target="tpu_custom_call" | custom-call | flops 2000000000 | bytes 1048576 | tf_op jit(solution)/shard_map/key_pass/pallas_call | solution.py:543
  96.8 1.2 %collective-permute-start.3 = (bf16[2,4,128,128]{3,2,1,0:T(8,128)(2,1)S(1)}, bf16[2,4,128,128]{3,2,1,0:T(8,128)(2,1)S(1)}, u32[]{:S(2)}, u32[]{:S(2)}) collective-permute-start(bf16[2,4,128,128]{3,2,1,0:T(8,128)(2,1)S(1)} %key_pass.4), channel_id=1, source_target_pairs={{0,8},{1,9},{2,10},{3,11},{4,12},{5,13},{6,14},{7,15},{8,0},{9,1},... | collective-permute-start | bytes 786440 | tf_op jit(solution)/shard_map/ppermute | solution.py:571
  98.0 2.7 %key_pass.5 = bf16[2,4,128,128]{3,2,1,0:T(8,128)(2,1)S(1)} custom-call(s32[16,128]{1,0:T(8,128)S(1)} %get-tuple-element.38.refs_0_, bf16[2,8,8,128,128]{4,3,2,1,0:T(8,128)(2,1)S(1)} %get-tuple-element.31.key_all.refs_1_, bf16[2,8,8,128,128]{4,3,2,1,0:T(8,128)(2,1)S(1)} %get-tuple-element.32.value_all.refs_2_, f32[128,1,128]{2,1,0:T(1,128)S(1)} %bitcast.22, ...), custom_call_target="tpu_custom_call" | custom-call | flops 2000000000 | bytes 1048576 | tf_op jit(solution)/shard_map/key_pass/pallas_call | solution.py:543
  100.7 0.4 collective-permute-start.4
  101.2 0.0 collective-permute-done
  101.2 6.7 %key_pass.3 = bf16[2,8,128,128]{3,2,1,0:T(8,128)(2,1)S(1)} custom-call(s32[16,128]{1,0:T(8,128)S(1)} %get-tuple-element.38.refs_0_, bf16[2,8,8,128,128]{4,3,2,1,0:T(8,128)(2,1)S(1)} %get-tuple-element.31.key_all.refs_1_, bf16[2,8,8,128,128]{4,3,2,1,0:T(8,128)(2,1)S(1)} %get-tuple-element.32.value_all.refs_2_, f32[128,1,128]{2,1,0:T(1,128)S(1)} %bitcast.23, ...), custom_call_target="tpu_custom_call" | custom-call | flops 2000000000 | bytes 1048576 | tf_op jit(solution)/shard_map/key_pass/pallas_call | solution.py:543
  107.9 0.0 collective-permute-done.3
  107.9 2.4 %collective-permute-done.4 = bf16[2,4,128,128]{3,2,1,0:T(8,128)(2,1)S(1)} collective-permute-done((bf16[2,4,128,128]{3,2,1,0:T(8,128)(2,1)S(1)}, bf16[2,4,128,128]{3,2,1,0:T(8,128)(2,1)S(1)}, u32[]{:S(2)}, u32[]{:S(2)}) %collective-permute-start.4) | collective-permute-done | bytes 262176 | tf_op jit(solution)/shard_map/ppermute | solution.py:571
  110.4 0.1 broadcast_select_fusion.1
  110.5 0.9 pad_maximum_fusion.2
  111.3 1.1 pad_maximum_fusion
  (3 shorter events, 0.1 us)
Async XLA Ops:
  71.4 9.9 %collective-permute-start.2 = (bf16[8,128,128]{2,1,0:T(8,128)(2,1)S(1)}, bf16[8,128,128]{2,1,0:T(8,128)(2,1)S(1)}, u32[]{:S(2)}, u32[]{:S(2)}) collective-permute-start(bf16[8,128,128]{2,1,0:T(8,128)(2,1)S(1)} %get-tuple-element.40), channel_id=1, source_target_pairs={{2,0},{3,1},{4,2},{5,3},{6,4},{7,5},{0,6},{1,7},{10,8},{11,9},{12,... | collective-permute-start | bytes 786440 | tf_op jit(solution)/shard_map/ppermute | solution.py:566
  71.9 9.4 %collective-permute-start.1 = (bf16[8,128,128]{2,1,0:T(8,128)(2,1)S(1)}, bf16[8,128,128]{2,1,0:T(8,128)(2,1)S(1)}, u32[]{:S(2)}, u32[]{:S(2)}) collective-permute-start(bf16[8,128,128]{2,1,0:T(8,128)(2,1)S(1)} %get-tuple-element.40), channel_id=1, source_target_pairs={{0,2},{1,3},{2,4},{3,5},{4,6},{5,7},{6,0},{7,1},{8,10},{9,11},{10,... | collective-permute-start | bytes 786440 | tf_op jit(solution)/shard_map/ppermute | solution.py:565
  80.7 20.4 %collective-permute-start = (bf16[8,128,128]{2,1,0:T(8,128)(2,1)S(1)}, bf16[8,128,128]{2,1,0:T(8,128)(2,1)S(1)}, u32[]{:S(2)}, u32[]{:S(2)}) collective-permute-start(bf16[8,128,128]{2,1,0:T(8,128)(2,1)S(1)} %get-tuple-element.37), channel_id=1, source_target_pairs={{0,8},{1,9},{2,10},{3,11},{4,12},{5,13},{6,14},{7,15},{8,0},{9,1},... | collective-permute-start | bytes 786440 | tf_op jit(solution)/shard_map/ppermute | solution.py:571
  96.8 11.1 %collective-permute-start.3 = (bf16[2,4,128,128]{3,2,1,0:T(8,128)(2,1)S(1)}, bf16[2,4,128,128]{3,2,1,0:T(8,128)(2,1)S(1)}, u32[]{:S(2)}, u32[]{:S(2)}) collective-permute-start(bf16[2,4,128,128]{3,2,1,0:T(8,128)(2,1)S(1)} %key_pass.4), channel_id=1, source_target_pairs={{0,8},{1,9},{2,10},{3,11},{4,12},{5,13},{6,14},{7,15},{8,0},{9,1},... | collective-permute-start | bytes 786440 | tf_op jit(solution)/shard_map/ppermute | solution.py:571
  100.7 9.6 %collective-permute-start.4 = (bf16[2,4,128,128]{3,2,1,0:T(8,128)(2,1)S(1)}, bf16[2,4,128,128]{3,2,1,0:T(8,128)(2,1)S(1)}, u32[]{:S(2)}, u32[]{:S(2)}) collective-permute-start(bf16[2,4,128,128]{3,2,1,0:T(8,128)(2,1)S(1)} %key_pass.5), channel_id=1, source_target_pairs={{0,8},{1,9},{2,10},{3,11},{4,12},{5,13},{6,14},{7,15},{8,0},{9,1},... | collective-permute-start | bytes 786440 | tf_op jit(solution)/shard_map/ppermute | solution.py:571
